TPU v7x, 256 devices: a whole 4x4x8 slice. The times are simulated.
256 devices in a mesh: shot: 16 (over y_lo, z), space: 16 (over y_hi, x, core).
Axes of the slice: x: 4, y: 4 (y_hi: 2, y_lo: 2; y = y_hi * 2 + y_lo), z: 8, core: 2. Of those that a mesh axis runs over, the one named last changes fastest.
Arguments:
- velocity: float32 [256, 128, 128], P('space'), may hold values from 2 to 6
- layer_widths: int32 [6], replicated, may hold values from 2 to 6
- forward_prev: float32 [16, 256, 128, 128], P('shot', 'space'), may hold values from -6 to 6
- forward_now: float32 [16, 256, 128, 128], P('shot', 'space'), may hold values from -6 to 6
- adjoint_now: float32 [16, 256, 128, 128], P('shot', 'space'), may hold values from -6 to 6
- adjoint_later: float32 [16, 256, 128, 128], P('shot', 'space'), may hold values from -6 to 6
- source_cell: int32 [16, 3], P('shot'), may hold values from 0 to 255, as said below
- wavelet: float32 [16, 6], P('shot'), may hold values from -40 to 40
- receiver_cells: int32 [16, 3, 2048], P('shot'), may hold values from 0 to 255, as said below
- residuals: float32 [16, 6, 2048], P('shot'), may hold values from -40 to 40
Outputs:
- forward_last: float32 [16, 256, 128, 128], P('shot', 'space')
- adjoint_first: float32 [16, 256, 128, 128], P('shot', 'space')
- gradient: float32 [256, 128, 128], P('space', 'shot')
Inputs may be any that keep to these rules, and one draw needn't show every extreme that they name: `source_cell`: each shot's source is a cell of the grid, given as x, y, z indices below 256, 128, 128. `receiver_cells`: each receiver is a cell of the grid, given as x, y, z indices below 256, 128, 128; several receivers may share a cell.
All inputs are finite; a program needn't handle non-finite values.
Results may differ from a plain program's by a relative error of at most 0.0003.
Values sent between devices are 32-bit elements; how exact they have to be, the bound alone decides.
No kernel may reach another device: no remote copies, remote signals or barrier semaphores. Data moves between devices by JAX's collectives and lax.ppermute only.
A program may use at most 128 MiB of HBM per device.

v0:
```python
import functools

import jax
import jax.numpy as jnp
import numpy as np
from jax import lax
from jax.experimental import pallas as pl
from jax.experimental.pallas import tpu as pltpu
from jax.sharding import PartitionSpec as P

SCALE = 5040.0
CENTRE = -43050.0
SIDE = (8064.0, -1008.0, 128.0, -9.0)
DT_OVER_H = 0.07
DAMPING_RATE = 0.15
LOAD = 256
F32, BF16 = jnp.float32, jnp.bfloat16
VMEM = pltpu.VMEM
SMEM_SPEC = pl.BlockSpec(memory_space=pltpu.SMEM)
VMEM_SPEC = pl.BlockSpec(memory_space=pltpu.VMEM)


def banded(n):
    offset = np.abs(np.arange(n)[:, None] - np.arange(n)[None, :])
    band = np.zeros((n, n), np.float32)
    for distance, coeff in enumerate(SIDE, start=1):
        band[offset == distance] = coeff
    return band


def halves(value):
    high = value.astype(BF16)
    return high, (value - high.astype(F32)).astype(BF16)


def fill_planes(scal, planes, cells_y, cells_z):
    rows = lax.broadcasted_iota(jnp.int32, (cells_y, cells_z), 0)
    lanes = lax.broadcasted_iota(jnp.int32, (cells_y, cells_z), 1)
    absorb = (rows < scal[2]) | (rows >= cells_y - scal[3]) | (lanes < scal[4]) | (lanes >= cells_z - scal[5])
    damping = jnp.where(absorb, DAMPING_RATE, 0.0).astype(F32)
    full = jnp.full((cells_y, cells_z), DAMPING_RATE, F32)
    for kind, damp in enumerate((damping, full)):
        inverse = 1.0 / (1.0 + damp)
        planes[kind, 0] = inverse
        planes[kind, 1] = 2.0 * inverse
        planes[kind, 2] = (1.0 - damp) * inverse
    planes[2] = jnp.zeros((3, cells_y, cells_z), F32)


def kind_of(scal, x, total_x):
    at = scal[6] + x
    outside = (at < 0) | (at >= total_x)
    absorbing = (at < scal[0]) | (at >= total_x - scal[1])
    return jnp.where(outside, 2, jnp.where(absorbing, 1, 0))


def substep(scal, src, prev, prev_off, weight, weight_off, planes, tz, ty, inject, store, low_x, layers, total_x, unroll):
    cells_y = src.shape[1]
    rows = 16

    def body(group, carry):
        base = group * unroll
        partial = []
        for u in range(unroll):
            high, low = halves(src[base + u + 4])
            along_z = jnp.dot(jnp.concatenate([high, low], axis=1), tz, preferred_element_type=F32)
            along_y = jnp.dot(ty, jnp.concatenate([high, low], axis=0), preferred_element_type=F32)
            partial.append(along_z + along_y)
        kinds = [kind_of(scal, low_x + base + u, total_x) for u in range(unroll)]
        for chunk in range(cells_y // rows):
            at = slice(chunk * rows, (chunk + 1) * rows)
            column = [src[base + i, at, :] for i in range(unroll + 8)]
            for u in range(unroll):
                centre = column[u + 4]
                total = partial[u][at, :] + CENTRE * centre
                for distance, coeff in enumerate(SIDE, start=1):
                    total = total + coeff * (column[u + 4 - distance] + column[u + 4 + distance])
                if inject is not None:
                    total = total + inject[base + u, at, :]
                kind = kinds[u]
                new = (
                    planes[kind, 0, at, :] * (weight[base + u + weight_off, at, :] * total)
                    + planes[kind, 1, at, :] * centre
                    - planes[kind, 2, at, :] * prev[base + u + prev_off, at, :]
                )
                store(base + u, at, new)
        return carry

    lax.fori_loop(0, layers // unroll, body, 0)


def add_source(scal, amplitude, weight, weight_off, planes, dest, dest_off, low_x, layers, total_x):
    x = scal[7] - scal[6] - low_x

    @pl.when((x >= 0) & (x < layers))
    def _():
        kind = kind_of(scal, low_x + x, total_x)
        row = pl.ds(scal[8], 1)
        lane = lax.broadcasted_iota(jnp.int32, (1, dest.shape[2]), 1)
        gain = planes[kind, 0, row, :] * weight[x + weight_off, row, :] * (SCALE * amplitude)
        dest[x + dest_off, row, :] = dest[x + dest_off, row, :] + jnp.where(lane == scal[9], gain, 0.0)


def block_kernel(first, last, forward, level, total_x, names, *refs):
    r = dict(zip(names, refs))
    scal, planes, ext = r["scal"], r["planes"], r["ext"]
    cells_y, cells_z = ext.shape[1:]
    width = ext.shape[0] - 16
    half = width // 2
    fill_planes(scal, planes, cells_y, cells_z)
    if first:
        ext[:8] = r["from_low"][:8]
        ext[8 : 8 + width] = r["own"][...]
        ext[8 + width :] = r["from_high"][:8]
        prev = r["prev"]
        prev[:4] = r["from_low"][8:12]
        prev[4 : 4 + width] = r["own_prev"][...]
        prev[4 + width :] = r["from_high"][8:12]
        if forward:
            weight = r["weight_out"]
            gain = DT_OVER_H * DT_OVER_H / SCALE
            weight[:4] = gain * r["from_low"][12:] * r["from_low"][12:]
            weight[4 : 4 + width] = gain * r["speeds"][...] * r["speeds"][...]
            weight[4 + width :] = gain * r["from_high"][12:] * r["from_high"][12:]
        else:
            weight = r["weight"]
    else:
        ext[:8] = r["from_low"][...]
        ext[8 : 8 + half] = r["own_low"][...]
        ext[8 + half : 8 + width] = r["own_high"][...]
        ext[8 + width :] = r["from_high"][...]
        prev, weight = r["prev"], r["weight"]
    tz, ty = r["tz"][...], r["ty"][...]
    middle = r["middle"]

    def store_middle(x, at, new):
        middle[x, at, :] = new

    substep(scal, ext, prev, 0, weight, 0, planes, tz, ty, None if forward else r["inject_a"], store_middle, -4, width + 8, total_x, 4)
    if forward:
        add_source(scal, r["wave"][0, level], weight, 0, planes, middle, 0, -4, width + 8, total_x)

    final = r["final"]

    def store_final(x, at, new):
        final[x, at, :] = new

    inject = None if forward else r["inject_b"].at[pl.ds(4, width)]
    substep(scal, middle, ext, 8, weight, 4, planes, tz, ty, inject, store_final, 0, width, total_x, 4)
    if forward:
        add_source(scal, r["wave"][0, level + 1], weight, 4, planes, final, 0, 0, width, total_x)
    if not last:
        r["out_low"][...] = final[:half]
        r["out_high"][...] = final[half:]


def place_kernel(low_off, scal, cells, values, *refs):
    outs, (counts, table) = refs[:-2], refs[-2:]
    layers, cells_y, cells_z = outs[0].shape
    steps, receivers = values.shape
    groups = receivers // 128
    x = cells[0:1, :] - scal[6] + low_off
    inside = (x >= 0) & (x < layers)
    key = jnp.where(inside, x * cells_y + cells[1:2, :], -1)
    flag = jnp.where(inside, 1.0, 0.0).astype(F32)
    flag_rows = jnp.concatenate([flag[:, g * 128 : (g + 1) * 128] for g in range(groups)], axis=0)
    r0 = lax.broadcasted_iota(jnp.int32, (128, 128), 0)
    r1 = lax.broadcasted_iota(jnp.int32, (128, 128), 1)
    upper = jnp.where(r0 <= r1, 1.0, 0.0).astype(BF16)
    within = jnp.dot(flag_rows.astype(BF16), upper, preferred_element_type=F32)
    g0 = lax.broadcasted_iota(jnp.int32, (groups, groups), 0)
    g1 = lax.broadcasted_iota(jnp.int32, (groups, groups), 1)
    before = jnp.where(g1 < g0, 1.0, 0.0).astype(BF16)
    totals = jnp.broadcast_to(within[:, 127:128], (groups, 128)).astype(BF16)
    rank = within - flag_rows + jnp.dot(before, totals, preferred_element_type=F32)
    rank = jnp.where(flag_rows > 0.0, rank, -1.0)
    for g in range(groups):
        counts[0:1, g * 128 : (g + 1) * 128] = rank[g : g + 1, :]
    number = jnp.sum(flag).astype(jnp.int32)
    table[...] = jnp.zeros(table.shape, BF16)
    high_key = key // 128
    parts = [high_key.astype(F32), (key - high_key * 128).astype(F32), cells[2:3, :].astype(F32)]
    table[0:16] = jnp.concatenate(parts + [jnp.zeros((13, receivers), F32)], axis=0).astype(BF16)
    scaled = values[...] * SCALE
    high = scaled.astype(BF16)
    rest = scaled - high.astype(F32)
    mid = rest.astype(BF16)
    pad = jnp.zeros((16 - steps, receivers), F32)
    table[16:32] = jnp.concatenate([high.astype(F32), pad], axis=0).astype(BF16)
    table[32:48] = jnp.concatenate([mid.astype(F32), pad], axis=0).astype(BF16)

    def one_load(load, carry):
        slot = lax.broadcasted_iota(jnp.int32, (LOAD, receivers), 0) + load * LOAD
        pick = jnp.where(slot == counts[0:1, :].astype(jnp.int32), 1.0, 0.0).astype(BF16)
        nt = (((1,), (1,)), ((), ()))
        picked = lax.dot_general(table[...], pick, nt, preferred_element_type=F32)
        column = lax.dot_general(pick, table[...], nt, preferred_element_type=F32)
        filled = (lax.broadcasted_iota(jnp.int32, (1, LOAD), 1) + load * LOAD) < number
        spot = (picked[0:1] * 128.0 + picked[1:2]).astype(jnp.int32)
        spot = jnp.where(filled, spot, -1)
        lane = lax.broadcasted_iota(jnp.int32, (LOAD, cells_z), 1)
        at_z = lane == column[:, 2:3].astype(jnp.int32)
        right_high = jnp.concatenate([jnp.where(at_z, column[:, 16 + s : 17 + s], 0.0) for s in range(steps)], axis=1).astype(BF16)
        right_mid = jnp.concatenate([jnp.where(at_z, column[:, 32 + s : 33 + s], 0.0) for s in range(steps)], axis=1).astype(BF16)

        def one_layer(layer, c):
            row = lax.broadcasted_iota(jnp.int32, (cells_y, LOAD), 0) + layer * cells_y
            left = jnp.where(row == spot, 1.0, 0.0).astype(BF16)
            placed = jnp.dot(left, right_high, preferred_element_type=F32)
            placed = placed + jnp.dot(left, right_mid, preferred_element_type=F32)

            @pl.when(load == 0)
            def _():
                for s in range(steps):
                    outs[s][layer] = placed[:, s * cells_z : (s + 1) * cells_z]

            @pl.when(load > 0)
            def _():
                for s in range(steps):
                    outs[s][layer] = outs[s][layer] + placed[:, s * cells_z : (s + 1) * cells_z]

            return c

        lax.fori_loop(0, layers, one_layer, 0)
        return carry

    lax.fori_loop(0, jnp.maximum((number + LOAD - 1) // LOAD, 1), one_load, 0)


def image_kernel(me_ref, count, *refs):
    fields, outs = refs[:14], refs[14:]
    f, a = fields[:8], fields[8:]
    me = me_ref[0]
    low_bit, top_bit = me & 1, me >> 3
    half = outs[0].shape[1]

    def piece(x0, chunk):
        rows = pl.ds(pl.multiple_of(chunk * 8, 8), 8)

        def read(ref):
            off = (ref.shape[0] - 2 * half) // 2
            return ref[off + x0 : off + x0 + half, rows, :]

        f_values = [read(ref) for ref in f]
        slopes = [f_values[i + 1] - f_values[i] for i in range(7)]
        total = read(a[0]) * (slopes[1] - slopes[0])
        for n in range(1, 6):
            total = total + read(a[n]) * (slopes[n + 1] - slopes[n])
        return total * (1.0 / count)

    def body(j, carry):
        for which in range(2):
            outs[which][j] = piece(0, (top_bit ^ which) * 8 + j)
            outs[2 + which][j] = piece(half, j * 2 + (low_bit ^ which))
        return carry

    lax.fori_loop(0, 8, body, 0)


def call(kernel, out_shapes, inputs, scratch=(), smem=1, cost=(0, 0), name=None):
    vmem_inputs = [x for x in inputs[smem:]]
    return pl.pallas_call(
        kernel,
        out_shape=out_shapes,
        in_specs=[SMEM_SPEC] * smem + [VMEM_SPEC] * len(vmem_inputs),
        out_specs=[VMEM_SPEC] * len(out_shapes),
        scratch_shapes=list(scratch),
        compiler_params=pltpu.CompilerParams(vmem_limit_bytes=VLIM),
        cost_estimate=pl.CostEstimate(flops=cost[0], bytes_accessed=cost[1], transcendentals=0),
        name=name,
    )(*inputs[:smem], *vmem_inputs)


VLIM = 48 * 1024 * 1024


def per_device(velocity, layer_widths, forward_prev, forward_now, adjoint_now, adjoint_later, source_cell, wavelet, receiver_cells, residuals):
    width, cells_y, cells_z = velocity.shape
    total_x = width * lax.axis_size("space")
    start_x = lax.axis_index("space") * width
    shots = lax.axis_size("shot")
    steps = wavelet.shape[1]
    half = width // 2
    me = lax.axis_index("shot").astype(jnp.int32)
    scal = jnp.concatenate([layer_widths, start_x.astype(jnp.int32)[None], source_cell[0]])
    band = banded(cells_z)
    tz = jnp.asarray(np.concatenate([band, band], axis=0), BF16)
    ty = jnp.asarray(np.concatenate([banded(cells_y)] * 2, axis=1), BF16)
    sds = lambda n: jax.ShapeDtypeStruct((n, cells_y, cells_z), F32)
    count = lax.axis_size("space")
    up = [(i, i + 1) for i in range(count - 1)]
    down = [(b, a) for a, b in up]

    def exchange(to_low, to_high):
        return lax.ppermute(to_high, "space", up), lax.ppermute(to_low, "space", down)

    fp, fn, an, al = forward_prev[0], forward_now[0], adjoint_now[0], adjoint_later[0]
    f_in = exchange(
        jnp.concatenate([fn[:half], fp[:4], velocity[:4]]),
        jnp.concatenate([fn[half:], fp[width - 4 :], velocity[width - 4 :]]),
    )
    a_in = exchange(
        jnp.concatenate([an[:half], al[:4]]),
        jnp.concatenate([an[half:], al[width - 4 :]]),
    )
    sources = call(
        functools.partial(place_kernel, 4),
        [sds(width + 8)] * steps,
        [scal, receiver_cells[0], residuals[0]],
        [pltpu.VMEM((1, residuals.shape[2]), F32), pltpu.VMEM((48, residuals.shape[2]), BF16)],
        name="place_receivers",
    )
    planes = pltpu.VMEM((3, 3, cells_y, cells_z), F32)
    ext = pltpu.VMEM((width + 16, cells_y, cells_z), F32)
    prev_scratch = pltpu.VMEM((width + 8, cells_y, cells_z), F32)
    final_scratch = pltpu.VMEM((width, cells_y, cells_z), F32)

    def block(first, last, forward, level, inputs):
        names = [n for n, _ in inputs]
        outs, out_names = [sds(width + 8)], ["middle"]
        if first and forward:
            outs.append(sds(width + 8))
            out_names.append("weight_out")
        scratch, scratch_names = [planes, ext], ["planes", "ext"]
        if first:
            scratch.append(prev_scratch)
            scratch_names.append("prev")
        if last:
            outs.append(sds(width))
            out_names.append("final")
        else:
            outs += [sds(half)] * 2
            out_names += ["out_low", "out_high"]
        outs_names_scratch = list(scratch_names)
        if not last:
            scratch.append(final_scratch)
            outs_names_scratch.append("final")
        smem = 2 if forward else 1
        got = call(
            functools.partial(block_kernel, first, last, forward, level, total_x, names + out_names + outs_names_scratch),
            outs,
            [v for _, v in inputs],
            scratch,
            smem,
            name=("forward" if forward else "adjoint") + "_block",
        )
        return dict(zip(out_names, got))

    tables = [("tz", tz), ("ty", ty)]
    f0 = block(True, False, True, 0, [("scal", scal), ("wave", wavelet), ("from_low", f_in[0]), ("own", fn), ("from_high", f_in[1]), ("own_prev", fp), ("speeds", velocity)] + tables)
    weight = f0["weight_out"]
    f_in = exchange(f0["out_low"], f0["out_high"])
    a0 = block(True, False, False, 0, [("scal", scal), ("from_low", a_in[0]), ("own", an), ("from_high", a_in[1]), ("own_prev", al), ("weight", weight), ("inject_a", sources[5]), ("inject_b", sources[4])] + tables)
    a_in = exchange(a0["out_low"], a0["out_high"])

    def later(last, forward, level, before, arrived, extra):
        head = [("scal", scal)] + ([("wave", wavelet)] if forward else [])
        return block(False, last, forward, level, head + [("from_low", arrived[0]), ("own_low", before["out_low"]), ("own_high", before["out_high"]), ("from_high", arrived[1]), ("prev", before["middle"]), ("weight", weight)] + extra + tables)

    f1 = later(False, True, 2, f0, f_in, [])
    f_in = exchange(f1["out_low"], f1["out_high"])
    a1 = later(False, False, 0, a0, a_in, [("inject_a", sources[3]), ("inject_b", sources[2])])
    a_in = exchange(a1["out_low"], a1["out_high"])
    f2 = later(True, True, 4, f1, f_in, [])
    a2 = later(True, False, 0, a1, a_in, [("inject_a", sources[1]), ("inject_b", sources[0])])

    whole = lambda d: jnp.concatenate([d["out_low"], d["out_high"]])
    f_all = [fp, fn, f0["middle"], whole(f0), f1["middle"], whole(f1), f2["middle"], f2["final"]]
    a_all = [a2["final"], a2["middle"], whole(a1), a1["middle"], whole(a0), a0["middle"]]
    part = jax.ShapeDtypeStruct((8, half, 8, cells_z), F32)
    keep_a, send_a, keep_b, send_b = call(
        functools.partial(lambda c, m, *refs: image_kernel(m, c, *refs), shots),
        [part] * 4,
        [me[None]] + f_all + a_all,
        name="image",
    )
    gradient = reduce_shots(me, keep_a, send_a, keep_b, send_b)
    return f2["final"][None], a2["final"][None], gradient


def flip(value, bit):
    return lax.ppermute(value, "shot", [(i, i ^ bit) for i in range(lax.axis_size("shot"))])


def reduce_shots(me, keep_a, send_a, keep_b, send_b):
    got_a, got_b = flip(send_a, 8), flip(send_b, 1)
    low_bit, top_bit = me & 1, me >> 3
    mid = (me >> 1) & 3
    half = keep_a.shape[1:]
    pick = lambda v, axis, i: lax.dynamic_index_in_dim(v, i, axis, keepdims=False)
    ka, ga = (v.reshape((4, 2) + half) for v in (keep_a, got_a))
    kb, gb = (v.reshape((2, 4) + half) for v in (keep_b, got_b))
    sa = pick(ka, 1, 1 - low_bit) + pick(ga, 1, 1 - low_bit)
    sb = pick(kb, 0, 1 - top_bit) + pick(gb, 0, 1 - top_bit)
    ra, rb = flip(sa, 1), flip(sb, 8)
    wa = pick(ka, 1, low_bit) + pick(ga, 1, low_bit) + ra
    wb = pick(kb, 0, top_bit) + pick(gb, 0, top_bit) + rb
    both = jnp.concatenate([wa, wb], axis=1)
    total = pick(both, 0, mid)
    for d in (1, 2, 3):
        total = total + flip(pick(both, 0, mid ^ d), 2 * d)
    return total


def solution(mesh):
    placed = (
        P("space", None, None),
        P(),
        P("shot", "space", None, None),
        P("shot", "space", None, None),
        P("shot", "space", None, None),
        P("shot", "space", None, None),
        P("shot", None),
        P("shot", None),
        P("shot", None, None),
        P("shot", None, None),
    )
    return jax.shard_map(
        per_device,
        mesh=mesh,
        in_specs=placed,
        out_specs=(P("shot", "space", None, None), P("shot", "space", None, None), P("space", "shot", None)),
        check_vma=False,
    )
```

profile of v0, /device:TPU:16, one launch (start us, length us, event | category | flops | bytes accessed | tf_op | source)
XLA Modules:
  0.0 173.0 jit_solution(4471061876269590350)
XLA Ops:
  0.7 1.4 slice_bitcast_fusion.2
  3.6 2.0 %collective-permute-start = (f32[16,128,128]{2,1,0:T(8,128)}, f32[16,128,128]{2,1,0:T(8,128)}, u32[]{:S(2)}, u32[]{:S(2)}) collective-permute-start(f32[16,128,128]{2,1,0:T(8,128)} %pad_maximum_fusion), channel_id=1, source_target_pairs={{0,1},{1,2},{2,3},{3,4},{4,5},{5,6},{6,7},{7,8},{8,9},{9,10},{10,1... | collective-permute-start | bytes 3145736 | tf_op jit(solution)/shard_map/ppermute | solution.py:295
  6.7 7.2 %collective-permute-start.1 = (f32[16,128,128]{2,1,0:T(8,128)}, f32[16,128,128]{2,1,0:T(8,128)}, u32[]{:S(2)}, u32[]{:S(2)}) collective-permute-start(f32[16,128,128]{2,1,0:T(8,128)} %pad_maximum_fusion.1), channel_id=1, source_target_pairs={{1,0},{2,1},{3,2},{4,3},{5,4},{6,5},{7,6},{8,7},{9,8},{10,9},{11,1... | collective-permute-start | bytes 3145736 | tf_op jit(solution)/shard_map/ppermute | solution.py:295
  15.2 1.9 %collective-permute-start.6 = (f32[12,128,128]{2,1,0:T(8,128)}, f32[12,128,128]{2,1,0:T(8,128)}, u32[]{:S(2)}, u32[]{:S(2)}) collective-permute-start(f32[12,128,128]{2,1,0:T(8,128)} %pad_maximum_fusion.6), channel_id=1, source_target_pairs={{0,1},{1,2},{2,3},{3,4},{4,5},{5,6},{6,7},{7,8},{8,9},{9,10},{10,1... | collective-permute-start | bytes 2359304 | tf_op jit(solution)/shard_map/ppermute | solution.py:295
  18.0 7.2 %collective-permute-start.7 = (f32[12,128,128]{2,1,0:T(8,128)}, f32[12,128,128]{2,1,0:T(8,128)}, u32[]{:S(2)}, u32[]{:S(2)}) collective-permute-start(f32[12,128,128]{2,1,0:T(8,128)} %pad_maximum_fusion.7), channel_id=1, source_target_pairs={{1,0},{2,1},{3,2},{4,3},{5,4},{6,5},{7,6},{8,7},{9,8},{10,9},{11,1... | collective-permute-start | bytes 2359304 | tf_op jit(solution)/shard_map/ppermute | solution.py:295
  25.4 11.5 %place_receivers.1 = (f32[24,128,128]{2,1,0:T(8,128)S(1)}, f32[24,128,128]{2,1,0:T(8,128)S(1)}, f32[24,128,128]{2,1,0:T(8,128)S(1)}, f32[24,128,128]{2,1,0:T(8,1...) custom-call(s32[10]{0:T(128)S(1)} %pad_add_fusion.refs_0_.scal, s32[3,2048]{1,0:T(4,128)S(1)} %bitcast.84, ...), custom_call_target="tpu_custom_call" | custom-call | tf_op jit(solution)/shard_map/place_receivers/pallas_call | solution.py:262
  40.4 8.3 %forward_block.3 = (f32[24,128,128]{2,1,0:T(8,128)}, f32[24,128,128]{2,1,0:T(8,128)}, f32[8,128,128]{2,1,0:T(8,128)}, f32[8,128,128]{2,1,0:T(8,128)}) custom-call(s32[10]{0:T(128)S(1)} %pad_add_fusion.refs_0_.scal, f32[1,6]{1,0:T(1,128)S(1)} %copy-done.18, f32[16,128,128]{2,1,0:T(8,128)} %collective-permute-done.refs_2_, f32[16,128,128]{2,1,0:T(8,128)S(1)} %bitcast.73, ...), custom_call_target="tpu_custom_call" | custom-call | tf_op jit(solution)/shard_map/forward_block/pallas_call | solution.py:262
  48.7 8.7 %adjoint_block.3 = (f32[24,128,128]{2,1,0:T(8,128)}, f32[8,128,128]{2,1,0:T(8,128)}, f32[8,128,128]{2,1,0:T(8,128)}) custom-call(s32[10]{0:T(128)S(1)} %pad_add_fusion.refs_0_.scal, f32[12,128,128]{2,1,0:T(8,128)} %collective-permute-done.6.refs_1_, f32[16,128,128]{2,1,0:T(8,128)S(1)} %bitcast.77, f32[12,128,128]{2,1,0:T(8,128)} %collective-permute-done.7.refs_3_, ...), custom_call_target="tpu_custom_call" | custom-call | tf_op jit(solution)/shard_map/adjoint_block/pallas_call | solution.py:262
  57.4 1.9 %collective-permute-start.8 = (f32[8,128,128]{2,1,0:T(8,128)}, f32[8,128,128]{2,1,0:T(8,128)S(1)}, u32[]{:S(2)}, u32[]{:S(2)}) collective-permute-start(f32[8,128,128]{2,1,0:T(8,128)} %get-tuple-element.40.refs_3_), channel_id=1, source_target_pairs={{0,1},{1,2},{2,3},{3,4},{4,5},{5,6},{6,7},{7,8},{8,9},{9,10},{10,1... | collective-permute-start | bytes 1572872 | tf_op jit(solution)/shard_map/ppermute | solution.py:295
  59.4 7.3 %collective-permute-start.9 = (f32[8,128,128]{2,1,0:T(8,128)}, f32[8,128,128]{2,1,0:T(8,128)S(1)}, u32[]{:S(2)}, u32[]{:S(2)}) collective-permute-start(f32[8,128,128]{2,1,0:T(8,128)} %get-tuple-element.41.refs_2_), channel_id=1, source_target_pairs={{1,0},{2,1},{3,2},{4,3},{5,4},{6,5},{7,6},{8,7},{9,8},{10,9},{11,1... | collective-permute-start | bytes 1572872 | tf_op jit(solution)/shard_map/ppermute | solution.py:295
  66.6 1.9 %collective-permute-start.2 = (f32[8,128,128]{2,1,0:T(8,128)}, f32[8,128,128]{2,1,0:T(8,128)}, u32[]{:S(2)}, u32[]{:S(2)}) collective-permute-start(f32[8,128,128]{2,1,0:T(8,128)} %get-tuple-element.30.refs_4_), channel_id=1, source_target_pairs={{0,1},{1,2},{2,3},{3,4},{4,5},{5,6},{6,7},{7,8},{8,9},{9,10},{10,1... | collective-permute-start | bytes 1572872 | tf_op jit(solution)/shard_map/ppermute | solution.py:295
  68.6 7.3 %collective-permute-start.3 = (f32[8,128,128]{2,1,0:T(8,128)}, f32[8,128,128]{2,1,0:T(8,128)}, u32[]{:S(2)}, u32[]{:S(2)}) collective-permute-start(f32[8,128,128]{2,1,0:T(8,128)} %get-tuple-element.31.refs_3_), channel_id=1, source_target_pairs={{1,0},{2,1},{3,2},{4,3},{5,4},{6,5},{7,6},{8,7},{9,8},{10,9},{11,1... | collective-permute-start | bytes 1572872 | tf_op jit(solution)/shard_map/ppermute | solution.py:295
  79.5 7.7 %adjoint_block.4 = (f32[24,128,128]{2,1,0:T(8,128)S(1)}, f32[8,128,128]{2,1,0:T(8,128)S(1)}, f32[8,128,128]{2,1,0:T(8,128)S(1)}) custom-call(s32[10]{0:T(128)S(1)} %pad_add_fusion.refs_0_.scal, f32[8,128,128]{2,1,0:T(8,128)S(1)} %copy-done.15, f32[8,128,128]{2,1,0:T(8,128)} %get-tuple-element.41.refs_2_, f32[8,128,128]{2,1,0:T(8,128)} %get-tuple-element.40.refs_3_, ...), custom_call_target="tpu_custom_call" | custom-call | tf_op jit(solution)/shard_map/adjoint_block/pallas_call | solution.py:262
  87.3 1.9 %collective-permute-start.10 = (f32[8,128,128]{2,1,0:T(8,128)S(1)}, f32[8,128,128]{2,1,0:T(8,128)S(1)}, u32[]{:S(2)}, u32[]{:S(2)}) collective-permute-start(f32[8,128,128]{2,1,0:T(8,128)S(1)} %get-tuple-element.45.refs_3_), channel_id=1, source_target_pairs={{0,1},{1,2},{2,3},{3,4},{4,5},{5,6},{6,7},{7,8},{8,9},{9,10},{10,1... | collective-permute-start | bytes 1572872 | tf_op jit(solution)/shard_map/ppermute | solution.py:295
  89.2 7.3 %collective-permute-start.11 = (f32[8,128,128]{2,1,0:T(8,128)S(1)}, f32[8,128,128]{2,1,0:T(8,128)S(1)}, u32[]{:S(2)}, u32[]{:S(2)}) collective-permute-start(f32[8,128,128]{2,1,0:T(8,128)S(1)} %get-tuple-element.46.refs_2_), channel_id=1, source_target_pairs={{1,0},{2,1},{3,2},{4,3},{5,4},{6,5},{7,6},{8,7},{9,8},{10,9},{11,1... | collective-permute-start | bytes 1572872 | tf_op jit(solution)/shard_map/ppermute | solution.py:295
  96.5 7.0 %forward_block.4 = (f32[24,128,128]{2,1,0:T(8,128)S(1)}, f32[8,128,128]{2,1,0:T(8,128)S(1)}, f32[8,128,128]{2,1,0:T(8,128)S(1)}) custom-call(s32[10]{0:T(128)S(1)} %pad_add_fusion.refs_0_.scal, f32[1,6]{1,0:T(1,128)S(1)} %copy-done.18, f32[8,128,128]{2,1,0:T(8,128)} %collective-permute-done.2.refs_2_, f32[8,128,128]{2,1,0:T(8,128)} %get-tuple-element.31.refs_3_, ...), custom_call_target="tpu_custom_call" | custom-call | tf_op jit(solution)/shard_map/forward_block/pallas_call | solution.py:262
  103.5 1.9 %collective-permute-start.4 = (f32[8,128,128]{2,1,0:T(8,128)S(1)}, f32[8,128,128]{2,1,0:T(8,128)S(1)}, u32[]{:S(2)}, u32[]{:S(2)}) collective-permute-start(f32[8,128,128]{2,1,0:T(8,128)S(1)} %get-tuple-element.34.refs_4_), channel_id=1, source_target_pairs={{0,1},{1,2},{2,3},{3,4},{4,5},{5,6},{6,7},{7,8},{8,9},{9,10},{10,1... | collective-permute-start | bytes 1572872 | tf_op jit(solution)/shard_map/ppermute | solution.py:295
  105.4 7.3 %collective-permute-start.5 = (f32[8,128,128]{2,1,0:T(8,128)S(1)}, f32[8,128,128]{2,1,0:T(8,128)S(1)}, u32[]{:S(2)}, u32[]{:S(2)}) collective-permute-start(f32[8,128,128]{2,1,0:T(8,128)S(1)} %get-tuple-element.35.refs_3_), channel_id=1, source_target_pairs={{1,0},{2,1},{3,2},{4,3},{5,4},{6,5},{7,6},{8,7},{9,8},{10,9},{11,1... | collective-permute-start | bytes 1572872 | tf_op jit(solution)/shard_map/ppermute | solution.py:295
  112.7 2.3 %pad_maximum_fusion.5.refs_12_ = f32[16,128,128]{2,1,0:T(8,128)} fusion(f32[8,128,128]{2,1,0:T(8,128)} %get-tuple-element.40.refs_3_, f32[8,128,128]{2,1,0:T(8,128)} %get-tuple-element.41.refs_2_), kind=kLoop, calls=%fused_computation.5 | loop fusion | flops 262144 | bytes 2097152 | tf_op jit(solution)/shard_map/concatenate | solution.py:367
  117.6 1.8 %collective-permute-done.5.refs_5_ = f32[8,128,128]{2,1,0:T(8,128)S(1)} collective-permute-done((f32[8,128,128]{2,1,0:T(8,128)S(1)}, f32[8,128,128]{2,1,0:T(8,128)S(1)}, u32[]{:S(2)}, u32[]{:S(2)}) %collective-permute-start.5) | collective-permute-done | bytes 524320 | tf_op jit(solution)/shard_map/ppermute | solution.py:295
  119.4 6.9 %forward_block.5 = (f32[24,128,128]{2,1,0:T(8,128)S(1)}, f32[16,128,128]{2,1,0:T(8,128)}) custom-call(s32[10]{0:T(128)S(1)} %pad_add_fusion.refs_0_.scal, f32[1,6]{1,0:T(1,128)S(1)} %copy-done.18, f32[8,128,128]{2,1,0:T(8,128)S(1)} %collective-permute-done.4.refs_2_, f32[8,128,128]{2,1,0:T(8,128)S(1)} %get-tuple-element.35.refs_3_, ...), custom_call_target="tpu_custom_call" | custom-call | tf_op jit(solution)/shard_map/forward_block/pallas_call | solution.py:262
  127.5 7.9 %adjoint_block.5 = (f32[24,128,128]{2,1,0:T(8,128)S(1)}, f32[16,128,128]{2,1,0:T(8,128)}) custom-call(s32[10]{0:T(128)S(1)} %pad_add_fusion.refs_0_.scal, f32[8,128,128]{2,1,0:T(8,128)S(1)} %collective-permute-done.10.refs_1_, f32[8,128,128]{2,1,0:T(8,128)S(1)} %get-tuple-element.46.refs_2_, f32[8,128,128]{2,1,0:T(8,128)S(1)} %get-tuple-element.45.refs_3_, ...), custom_call_target="tpu_custom_call" | custom-call | tf_op jit(solution)/shard_map/adjoint_block/pallas_call | solution.py:262
  136.6 6.9 %image.1 = (f32[8,8,8,128]{3,2,1,0:T(8,128)S(1)}, f32[8,8,8,128]{3,2,1,0:T(8,128)S(1)}, f32[8,8,8,128]{3,2,1,0:T(8,128)S(1)}, f32[8,8,8,128]{3,2,1,0:T(8,128)S(1)}) custom-call(s32[1]{0:T(128)} %bitcast.16.m, f32[16,128,128]{2,1,0:T(8,128)S(1)} %bitcast.76, f32[16,128,128]{2,1,0:T(8,128)S(1)} %bitcast.74, f32[24,128,128]{2,1,0:T(8,128)} %get-tuple-element.32.refs_6_.refs_2_, ...), custom_call_target="tpu_custom_call" | custom-call | tf_op jit(solution)/shard_map/image/pallas_call | solution.py:262
  143.5 2.0 %collective-permute-start.14 = (f32[8,8,8,128]{3,2,1,0:T(8,128)S(1)}, f32[8,8,8,128]{3,2,1,0:T(8,128)S(1)}, u32[]{:S(2)}, u32[]{:S(2)}) collective-permute-start(f32[8,8,8,128]{3,2,1,0:T(8,128)S(1)} %get-tuple-element.56), channel_id=1, source_target_pairs={{0,16},{16,0},{32,48},{48,32},{64,80},{80,64},{96,112},{112,96},{1... | collective-permute-start | bytes 786440 | tf_op jit(solution)/shard_map/ppermute | solution.py:382
  146.8 3.8 %collective-permute-done.14 = f32[8,8,8,128]{3,2,1,0:T(8,128)S(1)} collective-permute-done((f32[8,8,8,128]{3,2,1,0:T(8,128)S(1)}, f32[8,8,8,128]{3,2,1,0:T(8,128)S(1)}, u32[]{:S(2)}, u32[]{:S(2)}) %collective-permute-start.14) | collective-permute-done | bytes 262176 | tf_op jit(solution)/shard_map/ppermute | solution.py:382
  150.6 1.4 collective-permute-start.15
  152.0 1.4 collective-permute-start.13
  153.4 2.3 %collective-permute-done.15 = f32[4,8,8,128]{3,2,1,0:T(8,128)S(1)} collective-permute-done((f32[4,8,8,128]{3,2,1,0:T(8,128)S(1)}, f32[4,8,8,128]{3,2,1,0:T(8,128)S(1)}, u32[]{:S(2)}, u32[]{:S(2)}) %collective-permute-start.15) | collective-permute-done | bytes 131104 | tf_op jit(solution)/shard_map/ppermute | solution.py:382
  157.1 4.8 %collective-permute-start.16 = (f32[16,8,128]{2,1,0:T(8,128)S(1)}, f32[16,8,128]{2,1,0:T(8,128)S(1)}, u32[]{:S(2)}, u32[]{:S(2)}) collective-permute-start(f32[16,8,128]{2,1,0:T(8,128)S(1)} %get-tuple-element.67), channel_id=1, source_target_pairs={{0,32},{16,48},{32,0},{48,16},{64,96},{80,112},{96,64},{112,80},{1... | collective-permute-start | bytes 196616 | tf_op jit(solution)/shard_map/ppermute | solution.py:382
  161.9 4.1 %collective-permute-start.17 = (f32[16,8,128]{2,1,0:T(8,128)S(1)}, f32[16,8,128]{2,1,0:T(8,128)S(1)}, u32[]{:S(2)}, u32[]{:S(2)}) collective-permute-start(f32[16,8,128]{2,1,0:T(8,128)S(1)} %get-tuple-element.68), channel_id=1, source_target_pairs={{0,64},{16,80},{32,96},{48,112},{64,0},{80,16},{96,32},{112,48},{1... | collective-permute-start | bytes 196616 | tf_op jit(solution)/shard_map/ppermute | solution.py:382
  165.9 4.1 %collective-permute-done.17 = f32[16,8,128]{2,1,0:T(8,128)S(1)} collective-permute-done((f32[16,8,128]{2,1,0:T(8,128)S(1)}, f32[16,8,128]{2,1,0:T(8,128)S(1)}, u32[]{:S(2)}, u32[]{:S(2)}) %collective-permute-start.17) | collective-permute-done | bytes 65568 | tf_op jit(solution)/shard_map/ppermute | solution.py:382
  170.0 2.4 %collective-permute-done.18 = f32[16,8,128]{2,1,0:T(8,128)S(1)} collective-permute-done((f32[16,8,128]{2,1,0:T(8,128)S(1)}, f32[16,8,128]{2,1,0:T(8,128)S(1)}, u32[]{:S(2)}, u32[]{:S(2)}) %collective-permute-start.18) | collective-permute-done | bytes 65568 | tf_op jit(solution)/shard_map/ppermute | solution.py:382
  (84 shorter events, 20.4 us)
Async XLA Ops:
  3.6 10.4 %copy-start.4 = (f32[1,16,128,128]{3,2,1,0:T(8,128)S(1)}, f32[1,16,128,128]{3,2,1,0:T(8,128)}, u32[]{:S(2)}) copy-start(f32[1,16,128,128]{3,2,1,0:T(8,128)} %param.16) | copy-start | bytes 3145732
  3.6 36.8 %collective-permute-start = (f32[16,128,128]{2,1,0:T(8,128)}, f32[16,128,128]{2,1,0:T(8,128)}, u32[]{:S(2)}, u32[]{:S(2)}) collective-permute-start(f32[16,128,128]{2,1,0:T(8,128)} %pad_maximum_fusion), channel_id=1, source_target_pairs={{0,1},{1,2},{2,3},{3,4},{4,5},{5,6},{6,7},{7,8},{8,9},{9,10},{10,1... | collective-permute-start | bytes 3145736 | tf_op jit(solution)/shard_map/ppermute | solution.py:295
  5.6 8.4 %copy-start.7 = (f32[1,16,128,128]{3,2,1,0:T(8,128)S(1)}, f32[1,16,128,128]{3,2,1,0:T(8,128)}, u32[]{:S(2)}) copy-start(f32[1,16,128,128]{3,2,1,0:T(8,128)} %param.17) | copy-start | bytes 3145732
  6.7 33.7 %collective-permute-start.1 = (f32[16,128,128]{2,1,0:T(8,128)}, f32[16,128,128]{2,1,0:T(8,128)}, u32[]{:S(2)}, u32[]{:S(2)}) collective-permute-start(f32[16,128,128]{2,1,0:T(8,128)} %pad_maximum_fusion.1), channel_id=1, source_target_pairs={{1,0},{2,1},{3,2},{4,3},{5,4},{6,5},{7,6},{8,7},{9,8},{10,9},{11,1... | collective-permute-start | bytes 3145736 | tf_op jit(solution)/shard_map/ppermute | solution.py:295
  14.1 11.2 %copy-start.20 = (f32[1,6,2048]{2,0,1:T(1,128)S(1)}, f32[1,6,2048]{2,0,1:T(1,128)}, u32[]{:S(2)}) copy-start(f32[1,6,2048]{2,0,1:T(1,128)} %param.21) | copy-start | bytes 147460
  14.1 11.2 %copy-start.21 = (s32[1,3,2048]{2,0,1:T(1,128)S(1)}, s32[1,3,2048]{2,0,1:T(1,128)}, u32[]{:S(2)}) copy-start(s32[1,3,2048]{2,0,1:T(1,128)} %param.20) | copy-start | bytes 73732
  14.1 11.2 %copy-start.22 = (s32[1,3]{1,0:T(1,128)S(1)}, s32[1,3]{1,0:T(1,128)}, u32[]{:S(2)}) copy-start(s32[1,3]{1,0:T(1,128)} %param.18) | copy-start | bytes 40
  14.2 11.2 %copy-start.23 = (s32[6]{0:T(128)S(1)}, s32[6]{0:T(128)}, u32[]{:S(2)}) copy-start(s32[6]{0:T(128)} %param.13) | copy-start | bytes 76
  14.2 26.2 %copy-start = (f32[1,16,128,128]{3,2,1,0:T(8,128)S(1)}, f32[1,16,128,128]{3,2,1,0:T(8,128)}, u32[]{:S(2)}) copy-start(f32[1,16,128,128]{3,2,1,0:T(8,128)} %param.15) | copy-start | bytes 3145732
  14.2 26.2 %copy-start.5 = (bf16[256,128]{1,0:T(8,128)(2,1)S(1)}, bf16[256,128]{1,0:T(8,128)(2,1)}, u32[]{:S(2)}) copy-start(bf16[256,128]{1,0:T(8,128)(2,1)} %constant.53.clone.refs_7_.refs_8_.refs_9_) | copy-start | bytes 196612
  14.2 26.2 %copy-start.6 = (bf16[128,256]{1,0:T(8,128)(2,1)S(1)}, bf16[128,256]{1,0:T(8,128)(2,1)}, u32[]{:S(2)}) copy-start(bf16[128,256]{1,0:T(8,128)(2,1)} %constant.54.clone.refs_8_.refs_9_.refs_10_) | copy-start | bytes 196612
  14.2 26.2 %copy-start.18 = (f32[1,6]{1,0:T(1,128)S(1)}, f32[1,6]{1,0:T(1,128)}, u32[]{:S(2)}) copy-start(f32[1,6]{1,0:T(1,128)} %refs_1_.5) | copy-start | bytes 76
  15.2 33.6 %collective-permute-start.6 = (f32[12,128,128]{2,1,0:T(8,128)}, f32[12,128,128]{2,1,0:T(8,128)}, u32[]{:S(2)}, u32[]{:S(2)}) collective-permute-start(f32[12,128,128]{2,1,0:T(8,128)} %pad_maximum_fusion.6), channel_id=1, source_target_pairs={{0,1},{1,2},{2,3},{3,4},{4,5},{5,6},{6,7},{7,8},{8,9},{9,10},{10,1... | collective-permute-start | bytes 2359304 | tf_op jit(solution)/shard_map/ppermute | solution.py:295
  18.0 30.7 %collective-permute-start.7 = (f32[12,128,128]{2,1,0:T(8,128)}, f32[12,128,128]{2,1,0:T(8,128)}, u32[]{:S(2)}, u32[]{:S(2)}) collective-permute-start(f32[12,128,128]{2,1,0:T(8,128)} %pad_maximum_fusion.7), channel_id=1, source_target_pairs={{1,0},{2,1},{3,2},{4,3},{5,4},{6,5},{7,6},{8,7},{9,8},{10,9},{11,1... | collective-permute-start | bytes 2359304 | tf_op jit(solution)/shard_map/ppermute | solution.py:295
  40.4 8.3 %copy-start.8 = (f32[1,16,128,128]{3,2,1,0:T(8,128)S(1)}, f32[1,16,128,128]{3,2,1,0:T(8,128)}, u32[]{:S(2)}) copy-start(f32[1,16,128,128]{3,2,1,0:T(8,128)} %param.17) | copy-start | bytes 3145732
  57.4 18.4 %collective-permute-start.8 = (f32[8,128,128]{2,1,0:T(8,128)}, f32[8,128,128]{2,1,0:T(8,128)S(1)}, u32[]{:S(2)}, u32[]{:S(2)}) collective-permute-start(f32[8,128,128]{2,1,0:T(8,128)} %get-tuple-element.40.refs_3_), channel_id=1, source_target_pairs={{0,1},{1,2},{2,3},{3,4},{4,5},{5,6},{6,7},{7,8},{8,9},{9,10},{10,1... | collective-permute-start | bytes 1572872 | tf_op jit(solution)/shard_map/ppermute | solution.py:295
  59.4 17.3 %collective-permute-start.9 = (f32[8,128,128]{2,1,0:T(8,128)}, f32[8,128,128]{2,1,0:T(8,128)S(1)}, u32[]{:S(2)}, u32[]{:S(2)}) collective-permute-start(f32[8,128,128]{2,1,0:T(8,128)} %get-tuple-element.41.refs_2_), channel_id=1, source_target_pairs={{1,0},{2,1},{3,2},{4,3},{5,4},{6,5},{7,6},{8,7},{9,8},{10,9},{11,1... | collective-permute-start | bytes 1572872 | tf_op jit(solution)/shard_map/ppermute | solution.py:295
  66.6 29.8 %collective-permute-start.2 = (f32[8,128,128]{2,1,0:T(8,128)}, f32[8,128,128]{2,1,0:T(8,128)}, u32[]{:S(2)}, u32[]{:S(2)}) collective-permute-start(f32[8,128,128]{2,1,0:T(8,128)} %get-tuple-element.30.refs_4_), channel_id=1, source_target_pairs={{0,1},{1,2},{2,3},{3,4},{4,5},{5,6},{6,7},{7,8},{8,9},{9,10},{10,1... | collective-permute-start | bytes 1572872 | tf_op jit(solution)/shard_map/ppermute | solution.py:295
  68.6 27.9 %collective-permute-start.3 = (f32[8,128,128]{2,1,0:T(8,128)}, f32[8,128,128]{2,1,0:T(8,128)}, u32[]{:S(2)}, u32[]{:S(2)}) collective-permute-start(f32[8,128,128]{2,1,0:T(8,128)} %get-tuple-element.31.refs_3_), channel_id=1, source_target_pairs={{1,0},{2,1},{3,2},{4,3},{5,4},{6,5},{7,6},{8,7},{9,8},{10,9},{11,1... | collective-permute-start | bytes 1572872 | tf_op jit(solution)/shard_map/ppermute | solution.py:295
  87.3 40.2 %copy-start.2 = (f32[24,128,128]{2,1,0:T(8,128)}, f32[24,128,128]{2,1,0:T(8,128)S(1)}, u32[]{:S(2)}) copy-start(f32[24,128,128]{2,1,0:T(8,128)S(1)} %get-tuple-element.47.refs_5_.refs_11_) | copy-start | bytes 4718596
  87.3 40.2 %collective-permute-start.10 = (f32[8,128,128]{2,1,0:T(8,128)S(1)}, f32[8,128,128]{2,1,0:T(8,128)S(1)}, u32[]{:S(2)}, u32[]{:S(2)}) collective-permute-start(f32[8,128,128]{2,1,0:T(8,128)S(1)} %get-tuple-element.45.refs_3_), channel_id=1, source_target_pairs={{0,1},{1,2},{2,3},{3,4},{4,5},{5,6},{6,7},{7,8},{8,9},{9,10},{10,1... | collective-permute-start | bytes 1572872 | tf_op jit(solution)/shard_map/ppermute | solution.py:295
  89.2 38.3 %collective-permute-start.11 = (f32[8,128,128]{2,1,0:T(8,128)S(1)}, f32[8,128,128]{2,1,0:T(8,128)S(1)}, u32[]{:S(2)}, u32[]{:S(2)}) collective-permute-start(f32[8,128,128]{2,1,0:T(8,128)S(1)} %get-tuple-element.46.refs_2_), channel_id=1, source_target_pairs={{1,0},{2,1},{3,2},{4,3},{5,4},{6,5},{7,6},{8,7},{9,8},{10,9},{11,1... | collective-permute-start | bytes 1572872 | tf_op jit(solution)/shard_map/ppermute | solution.py:295
  103.5 15.9 %copy-start.3 = (f32[24,128,128]{2,1,0:T(8,128)}, f32[24,128,128]{2,1,0:T(8,128)S(1)}, u32[]{:S(2)}) copy-start(f32[24,128,128]{2,1,0:T(8,128)S(1)} %get-tuple-element.36.refs_6_.refs_4_) | copy-start | bytes 4718596
  103.5 14.1 %collective-permute-start.4 = (f32[8,128,128]{2,1,0:T(8,128)S(1)}, f32[8,128,128]{2,1,0:T(8,128)S(1)}, u32[]{:S(2)}, u32[]{:S(2)}) collective-permute-start(f32[8,128,128]{2,1,0:T(8,128)S(1)} %get-tuple-element.34.refs_4_), channel_id=1, source_target_pairs={{0,1},{1,2},{2,3},{3,4},{4,5},{5,6},{6,7},{7,8},{8,9},{9,10},{10,1... | collective-permute-start | bytes 1572872 | tf_op jit(solution)/shard_map/ppermute | solution.py:295
  105.4 13.9 %collective-permute-start.5 = (f32[8,128,128]{2,1,0:T(8,128)S(1)}, f32[8,128,128]{2,1,0:T(8,128)S(1)}, u32[]{:S(2)}, u32[]{:S(2)}) collective-permute-start(f32[8,128,128]{2,1,0:T(8,128)S(1)} %get-tuple-element.35.refs_3_), channel_id=1, source_target_pairs={{1,0},{2,1},{3,2},{4,3},{5,4},{6,5},{7,6},{8,7},{9,8},{10,9},{11,1... | collective-permute-start | bytes 1572872 | tf_op jit(solution)/shard_map/ppermute | solution.py:295
  143.5 7.1 %collective-permute-start.14 = (f32[8,8,8,128]{3,2,1,0:T(8,128)S(1)}, f32[8,8,8,128]{3,2,1,0:T(8,128)S(1)}, u32[]{:S(2)}, u32[]{:S(2)}) collective-permute-start(f32[8,8,8,128]{3,2,1,0:T(8,128)S(1)} %get-tuple-element.56), channel_id=1, source_target_pairs={{0,16},{16,0},{32,48},{48,32},{64,80},{80,64},{96,112},{112,96},{1... | collective-permute-start | bytes 786440 | tf_op jit(solution)/shard_map/ppermute | solution.py:382
  145.5 6.5 %collective-permute-start.12 = (f32[8,8,8,128]{3,2,1,0:T(8,128)S(1)}, f32[8,8,8,128]{3,2,1,0:T(8,128)S(1)}, u32[]{:S(2)}, u32[]{:S(2)}) collective-permute-start(f32[8,8,8,128]{3,2,1,0:T(8,128)S(1)} %get-tuple-element.54), channel_id=1, source_target_pairs={{0,128},{16,144},{32,160},{48,176},{64,192},{80,208},{96,224},{112... | collective-permute-start | bytes 786440 | tf_op jit(solution)/shard_map/ppermute | solution.py:382
  150.6 5.1 %collective-permute-start.15 = (f32[4,8,8,128]{3,2,1,0:T(8,128)S(1)}, f32[4,8,8,128]{3,2,1,0:T(8,128)S(1)}, u32[]{:S(2)}, u32[]{:S(2)}) collective-permute-start(f32[4,8,8,128]{3,2,1,0:T(8,128)S(1)} %add_bitcast_fusion), channel_id=1, source_target_pairs={{0,128},{16,144},{32,160},{48,176},{64,192},{80,208},{96,224},{112... | collective-permute-start | bytes 393224 | tf_op jit(solution)/shard_map/ppermute | solution.py:382
  152.0 5.1 %collective-permute-start.13 = (f32[4,8,8,128]{3,2,1,0:T(8,128)S(1)}, f32[4,8,8,128]{3,2,1,0:T(8,128)S(1)}, u32[]{:S(2)}, u32[]{:S(2)}) collective-permute-start(f32[4,8,8,128]{3,2,1,0:T(8,128)S(1)} %fusion), channel_id=1, source_target_pairs={{0,16},{16,0},{32,48},{48,32},{64,80},{80,64},{96,112},{112,96},{1... | collective-permute-start | bytes 393224 | tf_op jit(solution)/shard_map/ppermute | solution.py:382
  157.1 8.8 %collective-permute-start.16 = (f32[16,8,128]{2,1,0:T(8,128)S(1)}, f32[16,8,128]{2,1,0:T(8,128)S(1)}, u32[]{:S(2)}, u32[]{:S(2)}) collective-permute-start(f32[16,8,128]{2,1,0:T(8,128)S(1)} %get-tuple-element.67), channel_id=1, source_target_pairs={{0,32},{16,48},{32,0},{48,16},{64,96},{80,112},{96,64},{112,80},{1... | collective-permute-start | bytes 196616 | tf_op jit(solution)/shard_map/ppermute | solution.py:382
  161.9 8.2 %collective-permute-start.17 = (f32[16,8,128]{2,1,0:T(8,128)S(1)}, f32[16,8,128]{2,1,0:T(8,128)S(1)}, u32[]{:S(2)}, u32[]{:S(2)}) collective-permute-start(f32[16,8,128]{2,1,0:T(8,128)S(1)} %get-tuple-element.68), channel_id=1, source_target_pairs={{0,64},{16,80},{32,96},{48,112},{64,0},{80,16},{96,32},{112,48},{1... | collective-permute-start | bytes 196616 | tf_op jit(solution)/shard_map/ppermute | solution.py:382
  165.9 6.5 %collective-permute-start.18 = (f32[16,8,128]{2,1,0:T(8,128)S(1)}, f32[16,8,128]{2,1,0:T(8,128)S(1)}, u32[]{:S(2)}, u32[]{:S(2)}) collective-permute-start(f32[16,8,128]{2,1,0:T(8,128)S(1)} %get-tuple-element.69), channel_id=1, source_target_pairs={{0,96},{16,112},{32,64},{48,80},{64,32},{80,48},{96,0},{112,16},{1... | collective-permute-start | bytes 196616 | tf_op jit(solution)/shard_map/ppermute | solution.py:382
  (11 other events, 13.0 us)
where the time goes:
time: 174 us; the launch traced here: 173 us
  starting transfers between devices  70 us (40%)
  Pallas kernels  64.8 us (37%)
  waiting for transfers between devices  15.9 us (9%)
  local copies, waits for them, and re-layouts  11.6 us (7%)
  other arithmetic  9.5 us (5%)
    pallas_call x8, Pallas kernels, call(): pl.pallas_call(kernel, out_shape=out_shapes, in_specs=[SMEM_SPEC] * smem...  64.8 us
    ppermute x6, starting transfers between devices, exchange(): lax.ppermute(to_low, 'space', down)  43.5 us
    ppermute x7, starting transfers between devices, flip(): lax.ppermute(value, 'shot', [(i, i ^ bit) for i in range(lax.axis_size('s...  14.9 us
    ppermute x7, waiting for transfers between devices, flip(): lax.ppermute(value, 'shot', [(i, i ^ bit) for i in range(lax.axis_size('s...  13.9 us
    ppermute x6, starting transfers between devices, exchange(): lax.ppermute(to_high, 'space', up)  11.6 us
    unnamed x50, local copies, waits for them, and re-layouts  10 us
    concatenate x4, other arithmetic, per_device(): whole = lambda d: jnp.concatenate([d['out_low'], d['out_high']])  4.67 us
  transfers between devices with their start and end apart: 19, of which 7 were waited for; matrix products, arithmetic and copies ran while one was open for 5% of the time, Pallas kernels for 24%

commit v1 on v0

v1 whole, which is shorter than its diff:
```python
import functools

import jax
import jax.numpy as jnp
import numpy as np
from jax import lax
from jax.experimental import pallas as pl
from jax.experimental.pallas import tpu as pltpu
from jax.sharding import PartitionSpec as P

SCALE = 5040.0
CENTRE = -43050.0
SIDE = (8064.0, -1008.0, 128.0, -9.0)
DT_OVER_H = 0.07
DAMPING_RATE = 0.15
BATCH = 8
LOAD = 256
F32, BF16 = jnp.float32, jnp.bfloat16
VMEM = pltpu.VMEM
SMEM_SPEC = pl.BlockSpec(memory_space=pltpu.SMEM)
VMEM_SPEC = pl.BlockSpec(memory_space=pltpu.VMEM)


def banded(n):
    offset = np.abs(np.arange(n)[:, None] - np.arange(n)[None, :])
    band = np.zeros((n, n), np.float32)
    for distance, coeff in enumerate(SIDE, start=1):
        band[offset == distance] = coeff
    return band


def halves(value):
    high = value.astype(BF16)
    return high, (value - high.astype(F32)).astype(BF16)


def fill_planes(scal, planes, cells_y, cells_z):
    rows = lax.broadcasted_iota(jnp.int32, (cells_y, cells_z), 0)
    lanes = lax.broadcasted_iota(jnp.int32, (cells_y, cells_z), 1)
    absorb = (rows < scal[2]) | (rows >= cells_y - scal[3]) | (lanes < scal[4]) | (lanes >= cells_z - scal[5])
    damping = jnp.where(absorb, DAMPING_RATE, 0.0).astype(F32)
    full = jnp.full((cells_y, cells_z), DAMPING_RATE, F32)
    for kind, damp in enumerate((damping, full)):
        inverse = 1.0 / (1.0 + damp)
        planes[kind, 0] = inverse
        planes[kind, 1] = 2.0 * inverse
        planes[kind, 2] = (1.0 - damp) * inverse
    planes[2] = jnp.zeros((3, cells_y, cells_z), F32)


def kind_of(scal, x, total_x):
    at = scal[6] + x
    outside = (at < 0) | (at >= total_x)
    absorbing = (at < scal[0]) | (at >= total_x - scal[1])
    return jnp.where(outside, 2, jnp.where(absorbing, 1, 0))


def right_of(table, load, level, cells_z):
    rows = pl.ds(pl.multiple_of(load * LOAD, LOAD), LOAD)
    lane = lax.broadcasted_iota(jnp.int32, (LOAD, cells_z), 1)
    at_z = lane == table[rows, 0:1].astype(jnp.int32)
    parts = [jnp.where(at_z, table[rows, 16 * p + level : 16 * p + level + 1], 0.0) for p in (1, 2)]
    return jnp.concatenate(parts, axis=1).astype(BF16)


def placed_layers(spots, load, right, first_layer, cells_y, cells_z):
    row = lax.broadcasted_iota(jnp.int32, (BATCH * cells_y, LOAD), 0) + first_layer * cells_y
    left = jnp.where(row == spots[pl.ds(load, 1), :], 1.0, 0.0).astype(BF16)
    both = jnp.dot(left, right, preferred_element_type=F32)
    return both[:, :cells_z] + both[:, cells_z:]


def substep(scal, src, prev, prev_off, weight, weight_off, planes, tz, ty, inject, dest, low_x, layers, total_x):
    cells_y, cells_z = src.shape[1:]
    rows = 16
    if inject is not None:
        spots, table, loads, level, inject_off = inject
        right = right_of(table, 0, level, cells_z)

    def body(group, carry):
        base = group * BATCH
        high, low = halves(src[pl.ds(base + 4, BATCH)])
        side_by_side = jnp.concatenate([high, low], axis=2).reshape(BATCH * cells_y, 2 * cells_z)
        along_z = jnp.dot(side_by_side, tz, preferred_element_type=F32)
        stacked = jnp.concatenate(
            [jnp.concatenate([part[u] for u in range(BATCH)], axis=1) for part in (high, low)], axis=0
        )
        along_y = jnp.dot(ty, stacked, preferred_element_type=F32)
        if inject is not None:
            along_z = along_z + placed_layers(spots, 0, right, base + inject_off, cells_y, cells_z)
        partial = [
            along_z[u * cells_y : (u + 1) * cells_y] + along_y[:, u * cells_z : (u + 1) * cells_z]
            for u in range(BATCH)
        ]
        kinds = [kind_of(scal, low_x + base + u, total_x) for u in range(BATCH)]
        for chunk in range(cells_y // rows):
            at = slice(chunk * rows, (chunk + 1) * rows)
            column = [src[base + i, at, :] for i in range(BATCH + 8)]
            for u in range(BATCH):
                centre = column[u + 4]
                total = partial[u][at, :] + CENTRE * centre
                for distance, coeff in enumerate(SIDE, start=1):
                    total = total + coeff * (column[u + 4 - distance] + column[u + 4 + distance])
                kind = kinds[u]
                dest[base + u, at, :] = (
                    planes[kind, 0, at, :] * (weight[base + u + weight_off, at, :] * total)
                    + planes[kind, 1, at, :] * centre
                    - planes[kind, 2, at, :] * prev[base + u + prev_off, at, :]
                )
        return carry

    lax.fori_loop(0, layers // BATCH, body, 0)
    if inject is not None:

        def another_load(load, carry):
            more = right_of(table, load, level, cells_z)

            def some_layers(group, c):
                base = group * BATCH
                placed = placed_layers(spots, load, more, base + inject_off, cells_y, cells_z)
                for u in range(BATCH):
                    kind = kind_of(scal, low_x + base + u, total_x)
                    term = planes[kind, 0] * (weight[base + u + weight_off] * placed[u * cells_y : (u + 1) * cells_y])
                    dest[base + u] = dest[base + u] + term
                return c

            return lax.fori_loop(0, layers // BATCH, some_layers, carry)

        lax.fori_loop(1, loads[0], another_load, 0)


def add_source(scal, amplitude, weight, weight_off, planes, dest, dest_off, low_x, layers, total_x):
    x = scal[7] - scal[6] - low_x

    @pl.when((x >= 0) & (x < layers))
    def _():
        kind = kind_of(scal, low_x + x, total_x)
        row = pl.ds(scal[8], 1)
        lane = lax.broadcasted_iota(jnp.int32, (1, dest.shape[2]), 1)
        gain = planes[kind, 0, row, :] * weight[x + weight_off, row, :] * (SCALE * amplitude)
        dest[x + dest_off, row, :] = dest[x + dest_off, row, :] + jnp.where(lane == scal[9], gain, 0.0)


def block_kernel(first, last, forward, level, total_x, names, *refs):
    r = dict(zip(names, refs))
    scal, planes, ext, weight = r["scal"], r["planes"], r["ext"], r["weight"]
    width = r["own"].shape[0]
    half = width // 2
    odd = scal[10]
    low_edge, high_edge = scal[6] == 0, scal[6] + width == total_x
    at_edge = low_edge | high_edge
    halo_a, halo_b = pl.ds((1 - odd) * (8 + width), 8), pl.ds(odd * (8 + width), 8)
    ext[halo_a] = r["from_a"][:8]
    ext[halo_b] = jnp.where(at_edge, 0.0, r["from_b"][:8])
    ext[8 : 8 + width] = r["own"][...]
    if first:
        prev = r["prev"]
        thin_a, thin_b = pl.ds((1 - odd) * (4 + width), 4), pl.ds(odd * (4 + width), 4)
        prev[thin_a] = r["from_a"][8:12]
        prev[thin_b] = r["from_b"][8:12]
        prev[4 : 4 + width] = r["own_prev"][...]
        if forward:
            gain = DT_OVER_H * DT_OVER_H / SCALE
            weight[thin_a] = gain * r["from_a"][12:] * r["from_a"][12:]
            weight[thin_b] = gain * r["from_b"][12:] * r["from_b"][12:]
            weight[4 : 4 + width] = gain * r["speeds"][...] * r["speeds"][...]
    else:
        prev = r["prev"]
    tz, ty = r["tz"][...], r["ty"][...]
    middle, final = r["middle"], r["final"]
    inject = (lambda n, off: None) if forward else (lambda n, off: (r["spots"], r["table"], r["loads"], n, off))
    substep(scal, ext, prev, 0, weight, 0, planes, tz, ty, inject(level, 0), middle, -4, width + 8, total_x)
    if forward:
        add_source(scal, r["wave"][0, level], weight, 0, planes, middle, 0, -4, width + 8, total_x)
    substep(scal, middle, ext, 8, weight, 4, planes, tz, ty, inject(level - 1, 4), final, 0, width, total_x)
    if forward:
        add_source(scal, r["wave"][0, level + 1], weight, 4, planes, final, 0, 0, width, total_x)
    if not last:
        r["to_a"][...] = final[pl.ds((1 - odd) * half, half)]
        r["to_b"][...] = final[pl.ds(odd * half, half)]


def receivers_kernel(low_off, layers, cells_y, cells_z, scal, cells, values, loads, spots, table, planes, counts, entries):
    fill_planes(scal, planes, cells_y, cells_z)
    steps, receivers = values.shape
    groups = receivers // 128
    x = cells[0:1, :] - scal[6] + low_off
    inside = (x >= 0) & (x < layers)
    key = jnp.where(inside, x * cells_y + cells[1:2, :], -1)
    flag = jnp.where(inside, 1.0, 0.0).astype(F32)
    flag_rows = jnp.concatenate([flag[:, g * 128 : (g + 1) * 128] for g in range(groups)], axis=0)
    r0 = lax.broadcasted_iota(jnp.int32, (128, 128), 0)
    r1 = lax.broadcasted_iota(jnp.int32, (128, 128), 1)
    upper = jnp.where(r0 <= r1, 1.0, 0.0).astype(BF16)
    within = jnp.dot(flag_rows.astype(BF16), upper, preferred_element_type=F32)
    g0 = lax.broadcasted_iota(jnp.int32, (groups, groups), 0)
    g1 = lax.broadcasted_iota(jnp.int32, (groups, groups), 1)
    before = jnp.where(g1 < g0, 1.0, 0.0).astype(BF16)
    totals = jnp.broadcast_to(within[:, 127:128], (groups, 128)).astype(BF16)
    rank = within - flag_rows + jnp.dot(before, totals, preferred_element_type=F32)
    rank = jnp.where(flag_rows > 0.0, rank, -1.0)
    for g in range(groups):
        counts[0:1, g * 128 : (g + 1) * 128] = rank[g : g + 1, :]
    number = jnp.sum(flag).astype(jnp.int32)
    filled_loads = jnp.maximum((number + LOAD - 1) // LOAD, 1)
    loads[0] = filled_loads
    high_key = key // 128
    parts = [cells[2:3, :].astype(F32), high_key.astype(F32), (key - high_key * 128).astype(F32)]
    entries[0:16] = jnp.concatenate(parts + [jnp.zeros((13, receivers), F32)], axis=0).astype(BF16)
    scaled = values[...] * SCALE
    high = scaled.astype(BF16)
    rest = (scaled - high.astype(F32)).astype(BF16)
    pad = jnp.zeros((16 - steps, receivers), BF16)
    entries[16:32] = jnp.concatenate([high, pad], axis=0)
    entries[32:48] = jnp.concatenate([rest, pad], axis=0)
    entries[48:] = jnp.zeros((entries.shape[0] - 48, receivers), BF16)

    def one_load(load, carry):
        slot = lax.broadcasted_iota(jnp.int32, (LOAD, receivers), 0) + load * LOAD
        pick = jnp.where(slot == counts[0:1, :].astype(jnp.int32), 1.0, 0.0).astype(BF16)
        nt = (((1,), (1,)), ((), ()))
        picked = lax.dot_general(entries[0:16], pick, nt, preferred_element_type=F32)
        column = lax.dot_general(pick, entries[...], nt, preferred_element_type=F32)
        filled = (lax.broadcasted_iota(jnp.int32, (1, LOAD), 1) + load * LOAD) < number
        spot = (picked[1:2] * 128.0 + picked[2:3]).astype(jnp.int32)
        spots[pl.ds(load, 1), :] = jnp.where(filled, spot, -1)
        table[pl.ds(pl.multiple_of(load * LOAD, LOAD), LOAD), :] = column
        return carry

    lax.fori_loop(0, filled_loads, one_load, 0)


def image_kernel(me_ref, count, *refs):
    fields, outs = refs[:14], refs[14:]
    f, a = fields[:8], fields[8:]
    me = me_ref[0]
    low_bit, top_bit = me & 1, me >> 3
    half = outs[0].shape[1]

    def piece(x0, chunk):
        rows = pl.ds(pl.multiple_of(chunk * 8, 8), 8)

        def read(ref):
            off = (ref.shape[0] - 2 * half) // 2
            return ref[off + x0 : off + x0 + half, rows, :]

        f_values = [read(ref) for ref in f]
        slopes = [f_values[i + 1] - f_values[i] for i in range(7)]
        total = read(a[0]) * (slopes[1] - slopes[0])
        for n in range(1, 6):
            total = total + read(a[n]) * (slopes[n + 1] - slopes[n])
        return total * (1.0 / count)

    def body(j, carry):
        for which in range(2):
            outs[which][j] = piece(0, (top_bit ^ which) * 8 + j)
            outs[2 + which][j] = piece(half, j * 2 + (low_bit ^ which))
        return carry

    lax.fori_loop(0, 8, body, 0)


def pack_kernel(plan, width, count, scal, *refs):
    inputs, outs, sems = refs[:count], refs[count:-1], refs[-1]
    copies = []
    for out, at_high in zip(outs, (1 - scal[10], scal[10])):
        at = 0
        for array, layers in zip(inputs, plan):
            source = array.at[pl.ds(at_high * (width - layers), layers)]
            copies.append(pltpu.make_async_copy(source, out.at[pl.ds(at, layers)], sems.at[len(copies)]))
            at += layers
    for copy in copies:
        copy.start()
    for copy in copies:
        copy.wait()


def pack(scal, arrays, plan):
    out = jax.ShapeDtypeStruct((sum(plan),) + arrays[0].shape[1:], F32)
    return pl.pallas_call(
        functools.partial(pack_kernel, plan, arrays[0].shape[0], len(arrays)),
        out_shape=[out] * 2,
        in_specs=[SMEM_SPEC] + [pl.BlockSpec(memory_space=pltpu.HBM)] * len(arrays),
        out_specs=[VMEM_SPEC] * 2,
        scratch_shapes=[pltpu.SemaphoreType.DMA((2 * len(plan),))],
        compiler_params=pltpu.CompilerParams(vmem_limit_bytes=VLIM),
        cost_estimate=pl.CostEstimate(flops=0, bytes_accessed=4 << 20, transcendentals=0),
        name="pack",
    )(scal, *arrays)


def call(kernel, out_shapes, inputs, scratch=(), smem=1, cost=(0, 14 << 20), name=None, out_specs=None):
    vmem_inputs = [x for x in inputs[smem:]]
    return pl.pallas_call(
        kernel,
        out_shape=out_shapes,
        in_specs=[SMEM_SPEC] * smem + [VMEM_SPEC] * len(vmem_inputs),
        out_specs=out_specs or [VMEM_SPEC] * len(out_shapes),
        scratch_shapes=list(scratch),
        compiler_params=pltpu.CompilerParams(vmem_limit_bytes=VLIM),
        cost_estimate=pl.CostEstimate(flops=cost[0], bytes_accessed=cost[1], transcendentals=0),
        name=name,
    )(*inputs[:smem], *vmem_inputs)


VLIM = 14 * 1024 * 1024


def per_device(velocity, layer_widths, forward_prev, forward_now, adjoint_now, adjoint_later, source_cell, wavelet, receiver_cells, residuals):
    width, cells_y, cells_z = velocity.shape
    total_x = width * lax.axis_size("space")
    shots = lax.axis_size("shot")
    half = width // 2
    me = lax.axis_index("shot").astype(jnp.int32)
    place = lax.axis_index("space").astype(jnp.int32)
    scal = jnp.concatenate([layer_widths, (place * width)[None], source_cell[0], (place % 2)[None]])
    band = banded(cells_z)
    tz = jnp.asarray(np.concatenate([band, band], axis=0), BF16)
    ty = jnp.asarray(np.concatenate([banded(cells_y)] * 2, axis=1), BF16)
    sds = lambda n: jax.ShapeDtypeStruct((n, cells_y, cells_z), F32)
    count = lax.axis_size("space")
    swap_a = [(i, i ^ 1) for i in range(count)]
    swap_b = [(i, (i + (1 if i % 2 else -1)) % count) for i in range(count)]

    def exchange(to_a, to_b):
        from_b = lax.ppermute(to_b, "space", swap_b)
        return lax.ppermute(to_a, "space", swap_a), from_b

    fp, fn, an, al = forward_prev[0], forward_now[0], adjoint_now[0], adjoint_later[0]
    f_in = exchange(*pack(scal, [fn, fp, velocity], (half, 4, 4)))
    a_in = exchange(*pack(scal, [an, al], (half, 4)))
    receivers = residuals.shape[2]
    slots = receivers // LOAD
    loads, spots, table, planes = call(
        functools.partial(receivers_kernel, 4, width + 8, cells_y, cells_z),
        [
            jax.ShapeDtypeStruct((1,), jnp.int32),
            jax.ShapeDtypeStruct((slots, LOAD), jnp.int32),
            jax.ShapeDtypeStruct((receivers, 128), F32),
            jax.ShapeDtypeStruct((3, 3, cells_y, cells_z), F32),
        ],
        [scal, receiver_cells[0], residuals[0]],
        [pltpu.VMEM((1, receivers), F32), pltpu.VMEM((128, receivers), BF16)],
        name="list_receivers",
        out_specs=[SMEM_SPEC] + [VMEM_SPEC] * 3,
    )
    tables = [("planes", planes), ("tz", tz), ("ty", ty)]

    def block(first, last, forward, level, arrived, own, extra):
        inputs = [("scal", scal), ("wave", wavelet) if forward else ("loads", loads)]
        inputs += [("from_a", arrived[0]), ("from_b", arrived[1]), ("own", own)] + extra + tables
        if not forward:
            inputs += [("spots", spots), ("table", table)]
        outs, out_names = [sds(width + 8), sds(width)], ["middle", "final"]
        if first and forward:
            outs.append(sds(width + 8))
            out_names.append("weight")
        if not last:
            outs += [sds(half)] * 2
            out_names += ["to_a", "to_b"]
        scratch, scratch_names = [pltpu.VMEM((width + 16, cells_y, cells_z), F32)], ["ext"]
        if first:
            scratch.append(pltpu.VMEM((width + 8, cells_y, cells_z), F32))
            scratch_names.append("prev")
        names = [n for n, _ in inputs] + out_names + scratch_names
        got = call(
            functools.partial(block_kernel, first, last, forward, level, total_x, names),
            outs,
            [v for _, v in inputs],
            scratch,
            2,
            name=("forward" if forward else "adjoint") + "_block",
        )
        return dict(zip(out_names, got))

    def begin(forward, level, arrived, own, own_prev, extra):
        return block(True, False, forward, level, arrived, own, [("own_prev", own_prev)] + extra)

    def go_on(last, forward, level, arrived, before):
        return block(False, last, forward, level, arrived, before["final"], [("prev", before["middle"]), ("weight", weight)])

    f0 = begin(True, 0, f_in, fn, fp, [("speeds", velocity)])
    weight = f0["weight"]
    f_in = exchange(f0["to_a"], f0["to_b"])
    a0 = begin(False, 5, a_in, an, al, [("weight", weight)])
    a_in = exchange(a0["to_a"], a0["to_b"])
    f1 = go_on(False, True, 2, f_in, f0)
    f_in = exchange(f1["to_a"], f1["to_b"])
    a1 = go_on(False, False, 3, a_in, a0)
    a_in = exchange(a1["to_a"], a1["to_b"])
    f2 = go_on(True, True, 4, f_in, f1)
    a2 = go_on(True, False, 1, a_in, a1)

    f_all = [fp, fn, f0["middle"], f0["final"], f1["middle"], f1["final"], f2["middle"], f2["final"]]
    a_all = [a2["final"], a2["middle"], a1["final"], a1["middle"], a0["final"], a0["middle"]]
    part = jax.ShapeDtypeStruct((8, half, 8, cells_z), F32)
    keep_a, send_a, keep_b, send_b = call(
        functools.partial(lambda c, m, *refs: image_kernel(m, c, *refs), shots),
        [part] * 4,
        [me[None]] + f_all + a_all,
        name="image",
    )
    gradient = reduce_shots(me, keep_a, send_a, keep_b, send_b)
    return f2["final"][None], a2["final"][None], gradient


def flip(value, bit):
    return lax.ppermute(value, "shot", [(i, i ^ bit) for i in range(lax.axis_size("shot"))])


def reduce_shots(me, keep_a, send_a, keep_b, send_b):
    got_a, got_b = flip(send_a, 8), flip(send_b, 1)
    low_bit, top_bit = me & 1, me >> 3
    mid = (me >> 1) & 3
    half = keep_a.shape[1:]
    pick = lambda v, axis, i: lax.dynamic_index_in_dim(v, i, axis, keepdims=False)
    ka, ga = (v.reshape((4, 2) + half) for v in (keep_a, got_a))
    kb, gb = (v.reshape((2, 4) + half) for v in (keep_b, got_b))
    sa = pick(ka, 1, 1 - low_bit) + pick(ga, 1, 1 - low_bit)
    sb = pick(kb, 0, 1 - top_bit) + pick(gb, 0, 1 - top_bit)
    ra, rb = flip(sa, 1), flip(sb, 8)
    wa = pick(ka, 1, low_bit) + pick(ga, 1, low_bit) + ra
    wb = pick(kb, 0, top_bit) + pick(gb, 0, top_bit) + rb
    both = jnp.concatenate([wa, wb], axis=1)
    total = pick(both, 0, mid)
    for d in (1, 2, 3):
        total = total + flip(pick(both, 0, mid ^ d), 2 * d)
    return total


def solution(mesh):
    placed = (
        P("space", None, None),
        P(),
        P("shot", "space", None, None),
        P("shot", "space", None, None),
        P("shot", "space", None, None),
        P("shot", "space", None, None),
        P("shot", None),
        P("shot", None),
        P("shot", None, None),
        P("shot", None, None),
    )
    return jax.shard_map(
        per_device,
        mesh=mesh,
        in_specs=placed,
        out_specs=(P("shot", "space", None, None), P("shot", "space", None, None), P("space", "shot", None)),
        check_vma=False,
    )
```

time: 174 us -> 125 us (0.72)
  the two profiles are of different devices: /device:TPU:16 before, /device:TPU:32 now
where the time goes in v1:
time: 125 us; the launch traced here: 124 us
  Pallas kernels  40.1 us (32%)
  waiting for transfers between devices  37.4 us (30%)
  starting transfers between devices  29.6 us (24%)
  local copies, waits for them, and re-layouts  14.4 us (12%)
  other arithmetic  1.5 us (1%)
    pallas_call x8, Pallas kernels, call(): pl.pallas_call(kernel, out_shape=out_shapes, in_specs=[SMEM_SPEC] * smem...  38.6 us
    ppermute x6, waiting for transfers between devices, exchange(): from_b = lax.ppermute(to_b, 'space', swap_b)  20.1 us
    ppermute x6, starting transfers between devices, exchange(): from_b = lax.ppermute(to_b, 'space', swap_b)  18.1 us
    ppermute x7, waiting for transfers between devices, flip(): lax.ppermute(value, 'shot', [(i, i ^ bit) for i in range(lax.axis_size('s...  17.3 us
    unnamed x74, local copies, waits for them, and re-layouts  14.4 us
    ppermute x7, starting transfers between devices, flip(): lax.ppermute(value, 'shot', [(i, i ^ bit) for i in range(lax.axis_size('s...  11.2 us
  transfers between devices with their start and end apart: 19, of which 9 were waited for; matrix products, arithmetic and copies ran while one was open for 0% of the time, Pallas kernels for 21%

profile of v1, /device:TPU:32, one launch (start us, length us, event | category | flops | bytes accessed | tf_op | source)
XLA Modules:
  0.0 124.0 jit_solution(2577524894120756506)
XLA Ops:
  1.4 1.2 copy-done
  2.6 1.2 copy-done.2
  3.8 1.2 copy-done.20
  6.0 5.5 %collective-permute-start.1 = (f32[16,128,128]{2,1,0:T(8,128)S(1)}, f32[16,128,128]{2,1,0:T(8,128)S(1)}, u32[]{:S(2)}, u32[]{:S(2)}) collective-permute-start(f32[16,128,128]{2,1,0:T(8,128)S(1)} %get-tuple-element.37), channel_id=1, source_target_pairs={{0,15},{1,2},{2,1},{3,4},{4,3},{5,6},{6,5},{7,8},{8,7},{9,10},{10,... | collective-permute-start | bytes 3145736 | tf_op jit(solution)/shard_map/ppermute | solution.py:326
  13.3 1.6 %list_receivers.1 = (s32[1]{0:T(128)}, s32[8,256]{1,0:T(8,128)S(1)}, f32[2048,128]{1,0:T(8,128)S(1)}, f32[3,3,128,128]{3,2,1,0:T(8,128)S(1)}) custom-call(s32[11]{0:T(128)S(1)} %pad_add_fusion.scal.refs_0_, s32[3,2048]{1,0:T(4,128)S(1)} %bitcast.75, f32[6,2048]{1,0:T(8,128)S(1)} %bitcast.74), custom_call_target="tpu_custom_call" | custom-call | bytes 14680064 | tf_op jit(solution)/shard_map/list_receivers/pallas_call | solution.py:294
  15.0 9.0 %collective-permute-done.1.refs_3_ = f32[16,128,128]{2,1,0:T(8,128)S(1)} collective-permute-done((f32[16,128,128]{2,1,0:T(8,128)S(1)}, f32[16,128,128]{2,1,0:T(8,128)S(1)}, u32[]{:S(2)}, u32[]{:S(2)}) %collective-permute-start.1) | collective-permute-done | bytes 1048608 | tf_op jit(solution)/shard_map/ppermute | solution.py:326
  24.0 4.3 %forward_block.3 = (f32[24,128,128]{2,1,0:T(8,128)S(1)}, f32[16,128,128]{2,1,0:T(8,128)S(1)}, f32[24,128,128]{2,1,0:T(8,128)S(1)}, f32[8,128,128]{2,1,0:T(8,128)S(1)}, f32[8,128,128]{2,1,0:T(8,128)S(1)}) custom-call(s32[11]{0:T(128)S(1)} %pad_add_fusion.scal.refs_0_, f32[1,6]{1,0:T(1,128)S(1)} %copy-done.33, ...), custom_call_target="tpu_custom_call" | custom-call | bytes 14680064 | tf_op jit(solution)/shard_map/forward_block/pallas_call | solution.py:294
  28.4 4.0 %collective-permute-done.7.refs_3_ = f32[12,128,128]{2,1,0:T(8,128)S(1)} collective-permute-done((f32[12,128,128]{2,1,0:T(8,128)S(1)}, f32[12,128,128]{2,1,0:T(8,128)S(1)}, u32[]{:S(2)}, u32[]{:S(2)}) %collective-permute-start.7) | collective-permute-done | bytes 786464 | tf_op jit(solution)/shard_map/ppermute | solution.py:326
  32.4 5.5 %adjoint_block.3 = (f32[24,128,128]{2,1,0:T(8,128)S(1)}, f32[16,128,128]{2,1,0:T(8,128)S(1)}, f32[8,128,128]{2,1,0:T(8,128)S(1)}, f32[8,128,128]{2,1,0:T(8,128)S(1)}) custom-call(s32[11]{0:T(128)S(1)} %pad_add_fusion.scal.refs_0_, s32[1]{0:T(128)} %get-tuple-element.49.refs_1_, f32[12,128,128]{2,1,0:T(8,128)S(1)} %collective-permute-done.6.refs_2_, ...), custom_call_target="tpu_custom_call" | custom-call | bytes 14680064 | tf_op jit(solution)/shard_map/adjoint_block/pallas_call | solution.py:294
  38.1 5.4 %collective-permute-start.9 = (f32[8,128,128]{2,1,0:T(8,128)S(1)}, f32[8,128,128]{2,1,0:T(8,128)S(1)}, u32[]{:S(2)}, u32[]{:S(2)}) collective-permute-start(f32[8,128,128]{2,1,0:T(8,128)S(1)} %get-tuple-element.55), channel_id=1, source_target_pairs={{0,15},{1,2},{2,1},{3,4},{4,3},{5,6},{6,5},{7,8},{8,7},{9,10},{10,... | collective-permute-start | bytes 1572872 | tf_op jit(solution)/shard_map/ppermute | solution.py:326
  43.9 6.4 %collective-permute-done.9.refs_3_ = f32[8,128,128]{2,1,0:T(8,128)S(1)} collective-permute-done((f32[8,128,128]{2,1,0:T(8,128)S(1)}, f32[8,128,128]{2,1,0:T(8,128)S(1)}, u32[]{:S(2)}, u32[]{:S(2)}) %collective-permute-start.9) | collective-permute-done | bytes 524320 | tf_op jit(solution)/shard_map/ppermute | solution.py:326
  50.4 6.6 %adjoint_block.4 = (f32[24,128,128]{2,1,0:T(8,128)S(1)}, f32[16,128,128]{2,1,0:T(8,128)S(1)}, f32[8,128,128]{2,1,0:T(8,128)}, f32[8,128,128]{2,1,0:T(8,128)}) custom-call(s32[11]{0:T(128)S(1)} %pad_add_fusion.scal.refs_0_, s32[1]{0:T(128)} %get-tuple-element.49.refs_1_, f32[8,128,128]{2,1,0:T(8,128)S(1)} %collective-permute-done.8.refs_2_, ...), custom_call_target="tpu_custom_call" | custom-call | bytes 14680064 | tf_op jit(solution)/shard_map/adjoint_block/pallas_call | solution.py:294
  57.0 1.2 copy-done.11
  59.1 5.3 %collective-permute-start.11 = (f32[8,128,128]{2,1,0:T(8,128)}, f32[8,128,128]{2,1,0:T(8,128)}, u32[]{:S(2)}, u32[]{:S(2)}) collective-permute-start(f32[8,128,128]{2,1,0:T(8,128)} %get-tuple-element.59), channel_id=1, source_target_pairs={{0,15},{1,2},{2,1},{3,4},{4,3},{5,6},{6,5},{7,8},{8,7},{9,10},{10,... | collective-permute-start | bytes 1572872 | tf_op jit(solution)/shard_map/ppermute | solution.py:326
  64.5 5.1 %forward_block.4 = (f32[24,128,128]{2,1,0:T(8,128)S(1)}, f32[16,128,128]{2,1,0:T(8,128)S(1)}, f32[8,128,128]{2,1,0:T(8,128)}, f32[8,128,128]{2,1,0:T(8,128)}) custom-call(s32[11]{0:T(128)S(1)} %pad_add_fusion.scal.refs_0_, f32[1,6]{1,0:T(1,128)S(1)} %copy-done.33, f32[8,128,128]{2,1,0:T(8,128)S(1)} %collective-permute-done.2.refs_2_, ...), custom_call_target="tpu_custom_call" | custom-call | bytes 14680064 | tf_op jit(solution)/shard_map/forward_block/pallas_call | solution.py:294
  69.6 1.2 copy-done.14
  70.8 1.0 copy-done.18
  72.3 1.2 copy-done.6
  73.5 1.4 %copy-done.12 = f32[24,128,128]{2,1,0:T(8,128)S(1)} copy-done((f32[24,128,128]{2,1,0:T(8,128)S(1)}, f32[24,128,128]{2,1,0:T(8,128)}, u32[]{:S(2)}) %copy-start.12) | copy-done | bytes 1572888
  75.0 1.2 copy-done.25
  76.2 7.6 %adjoint_block.5 = (f32[24,128,128]{2,1,0:T(8,128)S(1)}, f32[16,128,128]{2,1,0:T(8,128)}) custom-call(s32[11]{0:T(128)S(1)} %pad_add_fusion.scal.refs_0_, s32[1]{0:T(128)} %get-tuple-element.49.refs_1_, f32[8,128,128]{2,1,0:T(8,128)} %collective-permute-done.10.refs_2_, f32[8,128,128]{2,1,0:T(8,128)} %collective-permute-done.11.refs_3_, ...), custom_call_target="tpu_custom_call" | custom-call | bytes 14680064 | tf_op jit(solution)/shard_map/adjoint_block/pallas_call | solution.py:294
  84.4 5.9 %forward_block.5 = (f32[24,128,128]{2,1,0:T(8,128)S(1)}, f32[16,128,128]{2,1,0:T(8,128)}) custom-call(s32[11]{0:T(128)S(1)} %pad_add_fusion.scal.refs_0_, f32[1,6]{1,0:T(1,128)S(1)} %copy-done.33, f32[8,128,128]{2,1,0:T(8,128)} %collective-permute-done.4.refs_2_, f32[8,128,128]{2,1,0:T(8,128)} %collective-permute-done.5.refs_3_, ...), custom_call_target="tpu_custom_call" | custom-call | bytes 14680064 | tf_op jit(solution)/shard_map/forward_block/pallas_call | solution.py:294
  90.4 1.2 copy-done.31
  91.6 1.2 copy-done.32
  92.8 2.0 %image.1 = (f32[8,8,8,128]{3,2,1,0:T(8,128)S(1)}, f32[8,8,8,128]{3,2,1,0:T(8,128)S(1)}, f32[8,8,8,128]{3,2,1,0:T(8,128)S(1)}, f32[8,8,8,128]{3,2,1,0:T(8,128)S(1)}) custom-call(s32[1]{0:T(128)} %bitcast.9.m, f32[16,128,128]{2,1,0:T(8,128)S(1)} %bitcast.63, f32[16,128,128]{2,1,0:T(8,128)S(1)} %bitcast.60, f32[24,128,128]{2,1,0:T(8,128)S(1)} %copy-done.8, ...), custom_call_target="tpu_custom_call" | custom-call | bytes 14680064 | tf_op jit(solution)/shard_map/image/pallas_call | solution.py:294
  95.7 6.9 %collective-permute-done.14 = f32[8,8,8,128]{3,2,1,0:T(8,128)S(1)} collective-permute-done((f32[8,8,8,128]{3,2,1,0:T(8,128)S(1)}, f32[8,8,8,128]{3,2,1,0:T(8,128)S(1)}, u32[]{:S(2)}, u32[]{:S(2)}) %collective-permute-start.14) | collective-permute-done | bytes 262176 | tf_op jit(solution)/shard_map/ppermute | solution.py:408
  103.4 1.7 %collective-permute-start.13 = (f32[4,8,8,128]{3,2,1,0:T(8,128)S(1)}, f32[4,8,8,128]{3,2,1,0:T(8,128)S(1)}, u32[]{:S(2)}, u32[]{:S(2)}) collective-permute-start(f32[4,8,8,128]{3,2,1,0:T(8,128)S(1)} %fusion), channel_id=1, source_target_pairs={{0,16},{16,0},{32,48},{48,32},{64,80},{80,64},{96,112},{112,96},{1... | collective-permute-start | bytes 393224 | tf_op jit(solution)/shard_map/ppermute | solution.py:408
  105.0 2.6 %collective-permute-done.15 = f32[4,8,8,128]{3,2,1,0:T(8,128)S(1)} collective-permute-done((f32[4,8,8,128]{3,2,1,0:T(8,128)S(1)}, f32[4,8,8,128]{3,2,1,0:T(8,128)S(1)}, u32[]{:S(2)}, u32[]{:S(2)}) %collective-permute-start.15) | collective-permute-done | bytes 131104 | tf_op jit(solution)/shard_map/ppermute | solution.py:408
  108.5 3.4 %collective-permute-start.16 = (f32[16,8,128]{2,1,0:T(8,128)S(1)}, f32[16,8,128]{2,1,0:T(8,128)S(1)}, u32[]{:S(2)}, u32[]{:S(2)}) collective-permute-start(f32[16,8,128]{2,1,0:T(8,128)S(1)} %get-tuple-element.69), channel_id=1, source_target_pairs={{0,32},{16,48},{32,0},{48,16},{64,96},{80,112},{96,64},{112,80},{1... | collective-permute-start | bytes 196616 | tf_op jit(solution)/shard_map/ppermute | solution.py:408
  111.8 4.5 %collective-permute-start.17 = (f32[16,8,128]{2,1,0:T(8,128)S(1)}, f32[16,8,128]{2,1,0:T(8,128)S(1)}, u32[]{:S(2)}, u32[]{:S(2)}) collective-permute-start(f32[16,8,128]{2,1,0:T(8,128)S(1)} %get-tuple-element.70), channel_id=1, source_target_pairs={{0,64},{16,80},{32,96},{48,112},{64,0},{80,16},{96,32},{112,48},{1... | collective-permute-start | bytes 196616 | tf_op jit(solution)/shard_map/ppermute | solution.py:408
  116.3 4.2 %collective-permute-done.17 = f32[16,8,128]{2,1,0:T(8,128)S(1)} collective-permute-done((f32[16,8,128]{2,1,0:T(8,128)S(1)}, f32[16,8,128]{2,1,0:T(8,128)S(1)}, u32[]{:S(2)}, u32[]{:S(2)}) %collective-permute-start.17) | collective-permute-done | bytes 65568 | tf_op jit(solution)/shard_map/ppermute | solution.py:408
  120.5 2.9 %collective-permute-done.18 = f32[16,8,128]{2,1,0:T(8,128)S(1)} collective-permute-done((f32[16,8,128]{2,1,0:T(8,128)S(1)}, f32[16,8,128]{2,1,0:T(8,128)S(1)}, u32[]{:S(2)}, u32[]{:S(2)}) %collective-permute-start.18) | collective-permute-done | bytes 65568 | tf_op jit(solution)/shard_map/ppermute | solution.py:408
  (97 shorter events, 9.2 us)
Async XLA Ops:
  5.1 18.9 %copy-start.21 = (f32[16,128,128]{2,1,0:T(8,128)S(1)}, f32[16,128,128]{2,1,0:T(8,128)}, u32[]{:S(2)}) copy-start(f32[16,128,128]{2,1,0:T(8,128)} %refs_6_.1) | copy-start | bytes 3145732
  5.9 18.1 %copy-start.1 = (f32[1,16,128,128]{3,2,1,0:T(8,128)S(1)}, f32[1,16,128,128]{3,2,1,0:T(8,128)}, u32[]{:S(2)}) copy-start(f32[1,16,128,128]{3,2,1,0:T(8,128)} %param.15) | copy-start | bytes 3145732
  5.9 18.1 %copy-start.3 = (f32[1,16,128,128]{3,2,1,0:T(8,128)S(1)}, f32[1,16,128,128]{3,2,1,0:T(8,128)}, u32[]{:S(2)}) copy-start(f32[1,16,128,128]{3,2,1,0:T(8,128)} %param.14) | copy-start | bytes 3145732
  5.9 18.1 %copy-start.29 = (bf16[256,128]{1,0:T(8,128)(2,1)S(1)}, bf16[256,128]{1,0:T(8,128)(2,1)}, u32[]{:S(2)}) copy-start(bf16[256,128]{1,0:T(8,128)(2,1)} %constant.62.clone.refs_8_) | copy-start | bytes 196612
  5.9 18.1 %copy-start.30 = (bf16[128,256]{1,0:T(8,128)(2,1)S(1)}, bf16[128,256]{1,0:T(8,128)(2,1)}, u32[]{:S(2)}) copy-start(bf16[128,256]{1,0:T(8,128)(2,1)} %constant.63.clone.refs_9_) | copy-start | bytes 196612
  5.9 18.1 %copy-start.33 = (f32[1,6]{1,0:T(1,128)S(1)}, f32[1,6]{1,0:T(1,128)}, u32[]{:S(2)}) copy-start(f32[1,6]{1,0:T(1,128)} %refs_1_.5) | copy-start | bytes 76
  5.9 9.0 %collective-permute-start = (f32[16,128,128]{2,1,0:T(8,128)S(1)}, f32[16,128,128]{2,1,0:T(8,128)S(1)}, u32[]{:S(2)}, u32[]{:S(2)}) collective-permute-start(f32[16,128,128]{2,1,0:T(8,128)S(1)} %get-tuple-element.36), channel_id=1, source_target_pairs={{0,1},{1,0},{2,3},{3,2},{4,5},{5,4},{6,7},{7,6},{8,9},{9,8},{10,11... | collective-permute-start | bytes 3145736 | tf_op jit(solution)/shard_map/ppermute | solution.py:327
  6.0 18.0 %collective-permute-start.1 = (f32[16,128,128]{2,1,0:T(8,128)S(1)}, f32[16,128,128]{2,1,0:T(8,128)S(1)}, u32[]{:S(2)}, u32[]{:S(2)}) collective-permute-start(f32[16,128,128]{2,1,0:T(8,128)S(1)} %get-tuple-element.37), channel_id=1, source_target_pairs={{0,15},{1,2},{2,1},{3,4},{4,3},{5,6},{6,5},{7,8},{8,7},{9,10},{10,... | collective-permute-start | bytes 3145736 | tf_op jit(solution)/shard_map/ppermute | solution.py:326
  12.2 16.1 %collective-permute-start.6 = (f32[12,128,128]{2,1,0:T(8,128)S(1)}, f32[12,128,128]{2,1,0:T(8,128)S(1)}, u32[]{:S(2)}, u32[]{:S(2)}) collective-permute-start(f32[12,128,128]{2,1,0:T(8,128)S(1)} %get-tuple-element.50), channel_id=1, source_target_pairs={{0,1},{1,0},{2,3},{3,2},{4,5},{5,4},{6,7},{7,6},{8,9},{9,8},{10,11... | collective-permute-start | bytes 2359304 | tf_op jit(solution)/shard_map/ppermute | solution.py:327
  12.3 20.1 %collective-permute-start.7 = (f32[12,128,128]{2,1,0:T(8,128)S(1)}, f32[12,128,128]{2,1,0:T(8,128)S(1)}, u32[]{:S(2)}, u32[]{:S(2)}) collective-permute-start(f32[12,128,128]{2,1,0:T(8,128)S(1)} %get-tuple-element.51), channel_id=1, source_target_pairs={{0,15},{1,2},{2,1},{3,4},{4,3},{5,6},{6,5},{7,8},{8,7},{9,10},{10,... | collective-permute-start | bytes 2359304 | tf_op jit(solution)/shard_map/ppermute | solution.py:326
  15.0 35.4 %copy-start.5 = (f32[2048,128]{1,0:T(8,128)}, f32[2048,128]{1,0:T(8,128)S(1)}, u32[]{:S(2)}) copy-start(f32[2048,128]{1,0:T(8,128)S(1)} %get-tuple-element.53.refs_11_) | copy-start | bytes 3145732
  28.3 36.2 %copy-start.7 = (f32[24,128,128]{2,1,0:T(8,128)}, f32[24,128,128]{2,1,0:T(8,128)S(1)}, u32[]{:S(2)}) copy-start(f32[24,128,128]{2,1,0:T(8,128)S(1)} %get-tuple-element.42.refs_5_.refs_2_) | copy-start | bytes 4718596
  28.4 36.2 %copy-start.16 = (f32[16,128,128]{2,1,0:T(8,128)}, f32[16,128,128]{2,1,0:T(8,128)S(1)}, u32[]{:S(2)}) copy-start(f32[16,128,128]{2,1,0:T(8,128)S(1)} %get-tuple-element.41.refs_4_.refs_3_) | copy-start | bytes 3145732
  38.0 19.0 %copy-start.9 = (f32[24,128,128]{2,1,0:T(8,128)}, f32[24,128,128]{2,1,0:T(8,128)S(1)}, u32[]{:S(2)}) copy-start(f32[24,128,128]{2,1,0:T(8,128)S(1)} %get-tuple-element.57.refs_5_.refs_13_) | copy-start | bytes 4718596
  38.0 19.0 %copy-start.22 = (f32[16,128,128]{2,1,0:T(8,128)}, f32[16,128,128]{2,1,0:T(8,128)S(1)}, u32[]{:S(2)}) copy-start(f32[16,128,128]{2,1,0:T(8,128)S(1)} %get-tuple-element.56.refs_4_.refs_12_) | copy-start | bytes 3145732
  38.0 6.0 %collective-permute-start.8 = (f32[8,128,128]{2,1,0:T(8,128)S(1)}, f32[8,128,128]{2,1,0:T(8,128)S(1)}, u32[]{:S(2)}, u32[]{:S(2)}) collective-permute-start(f32[8,128,128]{2,1,0:T(8,128)S(1)} %get-tuple-element.54), channel_id=1, source_target_pairs={{0,1},{1,0},{2,3},{3,2},{4,5},{5,4},{6,7},{7,6},{8,9},{9,8},{10,11... | collective-permute-start | bytes 1572872 | tf_op jit(solution)/shard_map/ppermute | solution.py:327
  38.1 12.3 %collective-permute-start.9 = (f32[8,128,128]{2,1,0:T(8,128)S(1)}, f32[8,128,128]{2,1,0:T(8,128)S(1)}, u32[]{:S(2)}, u32[]{:S(2)}) collective-permute-start(f32[8,128,128]{2,1,0:T(8,128)S(1)} %get-tuple-element.55), channel_id=1, source_target_pairs={{0,15},{1,2},{2,1},{3,4},{4,3},{5,6},{6,5},{7,8},{8,7},{9,10},{10,... | collective-permute-start | bytes 1572872 | tf_op jit(solution)/shard_map/ppermute | solution.py:326
  43.5 21.0 %collective-permute-start.2 = (f32[8,128,128]{2,1,0:T(8,128)S(1)}, f32[8,128,128]{2,1,0:T(8,128)S(1)}, u32[]{:S(2)}, u32[]{:S(2)}) collective-permute-start(f32[8,128,128]{2,1,0:T(8,128)S(1)} %get-tuple-element.39), channel_id=1, source_target_pairs={{0,1},{1,0},{2,3},{3,2},{4,5},{5,4},{6,7},{7,6},{8,9},{9,8},{10,11... | collective-permute-start | bytes 1572872 | tf_op jit(solution)/shard_map/ppermute | solution.py:327
  43.5 21.0 %collective-permute-start.3 = (f32[8,128,128]{2,1,0:T(8,128)S(1)}, f32[8,128,128]{2,1,0:T(8,128)S(1)}, u32[]{:S(2)}, u32[]{:S(2)}) collective-permute-start(f32[8,128,128]{2,1,0:T(8,128)S(1)} %get-tuple-element.40), channel_id=1, source_target_pairs={{0,15},{1,2},{2,1},{3,4},{4,3},{5,6},{6,5},{7,8},{8,7},{9,10},{10,... | collective-permute-start | bytes 1572872 | tf_op jit(solution)/shard_map/ppermute | solution.py:326
  59.1 13.2 %collective-permute-start.10 = (f32[8,128,128]{2,1,0:T(8,128)}, f32[8,128,128]{2,1,0:T(8,128)}, u32[]{:S(2)}, u32[]{:S(2)}) collective-permute-start(f32[8,128,128]{2,1,0:T(8,128)} %get-tuple-element.58), channel_id=1, source_target_pairs={{0,1},{1,0},{2,3},{3,2},{4,5},{5,4},{6,7},{7,6},{8,9},{9,8},{10,11... | collective-permute-start | bytes 1572872 | tf_op jit(solution)/shard_map/ppermute | solution.py:327
  59.1 13.2 %collective-permute-start.11 = (f32[8,128,128]{2,1,0:T(8,128)}, f32[8,128,128]{2,1,0:T(8,128)}, u32[]{:S(2)}, u32[]{:S(2)}) collective-permute-start(f32[8,128,128]{2,1,0:T(8,128)} %get-tuple-element.59), channel_id=1, source_target_pairs={{0,15},{1,2},{2,1},{3,4},{4,3},{5,6},{6,5},{7,8},{8,7},{9,10},{10,... | collective-permute-start | bytes 1572872 | tf_op jit(solution)/shard_map/ppermute | solution.py:326
  71.8 12.0 %collective-permute-start.4 = (f32[8,128,128]{2,1,0:T(8,128)}, f32[8,128,128]{2,1,0:T(8,128)}, u32[]{:S(2)}, u32[]{:S(2)}) collective-permute-start(f32[8,128,128]{2,1,0:T(8,128)} %get-tuple-element.44), channel_id=1, source_target_pairs={{0,1},{1,0},{2,3},{3,2},{4,5},{5,4},{6,7},{7,6},{8,9},{9,8},{10,11... | collective-permute-start | bytes 1572872 | tf_op jit(solution)/shard_map/ppermute | solution.py:327
  71.8 12.5 %collective-permute-start.5 = (f32[8,128,128]{2,1,0:T(8,128)}, f32[8,128,128]{2,1,0:T(8,128)}, u32[]{:S(2)}, u32[]{:S(2)}) collective-permute-start(f32[8,128,128]{2,1,0:T(8,128)} %get-tuple-element.45), channel_id=1, source_target_pairs={{0,15},{1,2},{2,1},{3,4},{4,3},{5,6},{6,5},{7,8},{8,7},{9,10},{10,... | collective-permute-start | bytes 1572872 | tf_op jit(solution)/shard_map/ppermute | solution.py:326
  76.2 14.1 %copy-start.17 = (f32[16,128,128]{2,1,0:T(8,128)S(1)}, f32[16,128,128]{2,1,0:T(8,128)}, u32[]{:S(2)}) copy-start(f32[16,128,128]{2,1,0:T(8,128)} %copy-done.16) | copy-start | bytes 3145732
  76.2 14.1 %copy-start.23 = (f32[16,128,128]{2,1,0:T(8,128)S(1)}, f32[16,128,128]{2,1,0:T(8,128)}, u32[]{:S(2)}) copy-start(f32[16,128,128]{2,1,0:T(8,128)} %copy-done.22) | copy-start | bytes 3145732
  94.8 7.8 %collective-permute-start.14 = (f32[8,8,8,128]{3,2,1,0:T(8,128)S(1)}, f32[8,8,8,128]{3,2,1,0:T(8,128)S(1)}, u32[]{:S(2)}, u32[]{:S(2)}) collective-permute-start(f32[8,8,8,128]{3,2,1,0:T(8,128)S(1)} %get-tuple-element.68), channel_id=1, source_target_pairs={{0,16},{16,0},{32,48},{48,32},{64,80},{80,64},{96,112},{112,96},{1... | collective-permute-start | bytes 786440 | tf_op jit(solution)/shard_map/ppermute | solution.py:408
  95.6 7.7 %collective-permute-start.12 = (f32[8,8,8,128]{3,2,1,0:T(8,128)S(1)}, f32[8,8,8,128]{3,2,1,0:T(8,128)S(1)}, u32[]{:S(2)}, u32[]{:S(2)}) collective-permute-start(f32[8,8,8,128]{3,2,1,0:T(8,128)S(1)} %get-tuple-element.66), channel_id=1, source_target_pairs={{0,128},{16,144},{32,160},{48,176},{64,192},{80,208},{96,224},{112... | collective-permute-start | bytes 786440 | tf_op jit(solution)/shard_map/ppermute | solution.py:408
  102.6 5.1 %collective-permute-start.15 = (f32[4,8,8,128]{3,2,1,0:T(8,128)S(1)}, f32[4,8,8,128]{3,2,1,0:T(8,128)S(1)}, u32[]{:S(2)}, u32[]{:S(2)}) collective-permute-start(f32[4,8,8,128]{3,2,1,0:T(8,128)S(1)} %add_bitcast_fusion), channel_id=1, source_target_pairs={{0,128},{16,144},{32,160},{48,176},{64,192},{80,208},{96,224},{112... | collective-permute-start | bytes 393224 | tf_op jit(solution)/shard_map/ppermute | solution.py:408
  103.4 5.1 %collective-permute-start.13 = (f32[4,8,8,128]{3,2,1,0:T(8,128)S(1)}, f32[4,8,8,128]{3,2,1,0:T(8,128)S(1)}, u32[]{:S(2)}, u32[]{:S(2)}) collective-permute-start(f32[4,8,8,128]{3,2,1,0:T(8,128)S(1)} %fusion), channel_id=1, source_target_pairs={{0,16},{16,0},{32,48},{48,32},{64,80},{80,64},{96,112},{112,96},{1... | collective-permute-start | bytes 393224 | tf_op jit(solution)/shard_map/ppermute | solution.py:408
  108.5 7.9 %collective-permute-start.16 = (f32[16,8,128]{2,1,0:T(8,128)S(1)}, f32[16,8,128]{2,1,0:T(8,128)S(1)}, u32[]{:S(2)}, u32[]{:S(2)}) collective-permute-start(f32[16,8,128]{2,1,0:T(8,128)S(1)} %get-tuple-element.69), channel_id=1, source_target_pairs={{0,32},{16,48},{32,0},{48,16},{64,96},{80,112},{96,64},{112,80},{1... | collective-permute-start | bytes 196616 | tf_op jit(solution)/shard_map/ppermute | solution.py:408
  111.8 8.7 %collective-permute-start.17 = (f32[16,8,128]{2,1,0:T(8,128)S(1)}, f32[16,8,128]{2,1,0:T(8,128)S(1)}, u32[]{:S(2)}, u32[]{:S(2)}) collective-permute-start(f32[16,8,128]{2,1,0:T(8,128)S(1)} %get-tuple-element.70), channel_id=1, source_target_pairs={{0,64},{16,80},{32,96},{48,112},{64,0},{80,16},{96,32},{112,48},{1... | collective-permute-start | bytes 196616 | tf_op jit(solution)/shard_map/ppermute | solution.py:408
  116.3 7.1 %collective-permute-start.18 = (f32[16,8,128]{2,1,0:T(8,128)S(1)}, f32[16,8,128]{2,1,0:T(8,128)S(1)}, u32[]{:S(2)}, u32[]{:S(2)}) collective-permute-start(f32[16,8,128]{2,1,0:T(8,128)S(1)} %get-tuple-element.71), channel_id=1, source_target_pairs={{0,96},{16,112},{32,64},{48,80},{64,32},{80,48},{96,0},{112,16},{1... | collective-permute-start | bytes 196616 | tf_op jit(solution)/shard_map/ppermute | solution.py:408
  (23 other events, 97.9 us)

commit v2 on v1

--- a/solution.py
+++ b/solution.py
@@ -13,6 +13,7 @@
 SIDE = (8064.0, -1008.0, 128.0, -9.0)
 DT_OVER_H = 0.07
 DAMPING_RATE = 0.15
+SHOTS = 16
 BATCH = 8
 LOAD = 256
 F32, BF16 = jnp.float32, jnp.bfloat16
@@ -63,19 +64,21 @@
     return jnp.concatenate(parts, axis=1).astype(BF16)
 
 
-def placed_layers(spots, load, right, first_layer, cells_y, cells_z):
-    row = lax.broadcasted_iota(jnp.int32, (BATCH * cells_y, LOAD), 0) + first_layer * cells_y
-    left = jnp.where(row == spots[pl.ds(load, 1), :], 1.0, 0.0).astype(BF16)
+def one_hot_rows(spots, load, first_layer, layers, cells_y):
+    row = lax.broadcasted_iota(jnp.int32, (layers * cells_y, LOAD), 0) + first_layer * cells_y
+    return jnp.where(row == spots[pl.ds(load, 1), :], 1.0, 0.0).astype(BF16)
+
+
+def placed(left, right, cells_z):
     both = jnp.dot(left, right, preferred_element_type=F32)
     return both[:, :cells_z] + both[:, cells_z:]
 
 
-def substep(scal, src, prev, prev_off, weight, weight_off, planes, tz, ty, inject, dest, low_x, layers, total_x):
+def substep(scal, src, prev, prev_off, weight, weight_off, planes, tz, ty, inject, dest, low_x, layers, total_x, each=None, late=None):
     cells_y, cells_z = src.shape[1:]
     rows = 16
     if inject is not None:
-        spots, table, loads, level, inject_off = inject
-        right = right_of(table, 0, level, cells_z)
+        r, level, inject_off = inject
 
     def body(group, carry):
         base = group * BATCH
@@ -87,7 +90,8 @@
         )
         along_y = jnp.dot(ty, stacked, preferred_element_type=F32)
         if inject is not None:
-            along_z = along_z + placed_layers(spots, 0, right, base + inject_off, cells_y, cells_z)
+            first_row = pl.multiple_of((base + inject_off) * cells_y, cells_y)
+            along_z = along_z + placed(r["left"][pl.ds(first_row, BATCH * cells_y), :], r["rights"][level], cells_z)
         partial = [
             along_z[u * cells_y : (u + 1) * cells_y] + along_y[:, u * cells_z : (u + 1) * cells_z]
             for u in range(BATCH)
@@ -102,34 +106,38 @@
                 for distance, coeff in enumerate(SIDE, start=1):
                     total = total + coeff * (column[u + 4 - distance] + column[u + 4 + distance])
                 kind = kinds[u]
-                dest[base + u, at, :] = (
+                before = prev[base + u + prev_off, at, :]
+                new = (
                     planes[kind, 0, at, :] * (weight[base + u + weight_off, at, :] * total)
                     + planes[kind, 1, at, :] * centre
-                    - planes[kind, 2, at, :] * prev[base + u + prev_off, at, :]
+                    - planes[kind, 2, at, :] * before
                 )
+                dest[base + u, at, :] = new
+                if each is not None:
+                    each(base + u, at, new, centre, before)
         return carry
 
     lax.fori_loop(0, layers // BATCH, body, 0)
     if inject is not None:
 
         def another_load(load, carry):
-            more = right_of(table, load, level, cells_z)
-
-            def some_layers(group, c):
-                base = group * BATCH
-                placed = placed_layers(spots, load, more, base + inject_off, cells_y, cells_z)
-                for u in range(BATCH):
-                    kind = kind_of(scal, low_x + base + u, total_x)
-                    term = planes[kind, 0] * (weight[base + u + weight_off] * placed[u * cells_y : (u + 1) * cells_y])
-                    dest[base + u] = dest[base + u] + term
+            more = right_of(r["table"], load, level, cells_z)
+
+            def one_layer(x, c):
+                left = one_hot_rows(r["spots"], load, x + inject_off, 1, cells_y)
+                kind = kind_of(scal, low_x + x, total_x)
+                term = planes[kind, 0] * (weight[x + weight_off] * placed(left, more, cells_z))
+                dest[x] = dest[x] + term
+                if late is not None:
+                    late(x, slice(None), term)
                 return c
 
-            return lax.fori_loop(0, layers // BATCH, some_layers, carry)
-
-        lax.fori_loop(1, loads[0], another_load, 0)
-
-
-def add_source(scal, amplitude, weight, weight_off, planes, dest, dest_off, low_x, layers, total_x):
+            return lax.fori_loop(0, layers, one_layer, carry)
+
+        lax.fori_loop(1, r["loads"][0], another_load, 0)
+
+
+def add_source(scal, amplitude, weight, weight_off, planes, dest, low_x, layers, total_x, late=None):
     x = scal[7] - scal[6] - low_x
 
     @pl.when((x >= 0) & (x < layers))
@@ -138,7 +146,10 @@
         row = pl.ds(scal[8], 1)
         lane = lax.broadcasted_iota(jnp.int32, (1, dest.shape[2]), 1)
         gain = planes[kind, 0, row, :] * weight[x + weight_off, row, :] * (SCALE * amplitude)
-        dest[x + dest_off, row, :] = dest[x + dest_off, row, :] + jnp.where(lane == scal[9], gain, 0.0)
+        term = jnp.where(lane == scal[9], gain, 0.0)
+        dest[x, row, :] = dest[x, row, :] + term
+        if late is not None:
+            late(x, row, term)
 
 
 def block_kernel(first, last, forward, level, total_x, names, *refs):
@@ -147,6 +158,7 @@
     width = r["own"].shape[0]
     half = width // 2
     odd = scal[10]
+    r["turn"][0] = r["after"][0]
     low_edge, high_edge = scal[6] == 0, scal[6] + width == total_x
     at_edge = low_edge | high_edge
     halo_a, halo_b = pl.ds((1 - odd) * (8 + width), 8), pl.ds(odd * (8 + width), 8)
@@ -168,19 +180,67 @@
         prev = r["prev"]
     tz, ty = r["tz"][...], r["ty"][...]
     middle, final = r["middle"], r["final"]
-    inject = (lambda n, off: None) if forward else (lambda n, off: (r["spots"], r["table"], r["loads"], n, off))
+    inject = (lambda n, off: None) if forward else (lambda n, off: (r, n, off))
     substep(scal, ext, prev, 0, weight, 0, planes, tz, ty, inject(level, 0), middle, -4, width + 8, total_x)
     if forward:
-        add_source(scal, r["wave"][0, level], weight, 0, planes, middle, 0, -4, width + 8, total_x)
-    substep(scal, middle, ext, 8, weight, 4, planes, tz, ty, inject(level - 1, 4), final, 0, width, total_x)
+        add_source(scal, r["wave"][0, level], weight, 0, planes, middle, -4, width + 8, total_x)
+
+    each = late = None
+    image = r.get("image")
     if forward:
-        add_source(scal, r["wave"][0, level + 1], weight, 4, planes, final, 0, 0, width, total_x)
+
+        def curvatures(x, at, new, centre, before):
+            return centre - 2.0 * before + prev[x + 4, at, :], new - 2.0 * centre + before
+
+        if last:
+
+            def each(x, at, *states):
+                early, recent = curvatures(x, at, *states)
+                terms = r["adjoint_early"][x, at, :] * early + r["adjoint_recent"][x + 4, at, :] * recent
+                image[x, at, :] = r["image_in"][x, at, :] + terms
+
+            def late(x, at, term):
+                image[x, at, :] = image[x, at, :] + r["adjoint_recent"][x + 4, at, :] * term
+
+        else:
+
+            def each(x, at, *states):
+                r["curve_early"][x, at, :], r["curve_recent"][x, at, :] = curvatures(x, at, *states)
+
+            def late(x, at, term):
+                r["curve_recent"][x, at, :] = r["curve_recent"][x, at, :] + term
+
+    elif not first:
+
+        def each(x, at, new, centre, before):
+            terms = centre * r["curve_recent"][x, at, :] + new * r["curve_early"][x, at, :]
+            image[x, at, :] = r["image_in"][x, at, :] + terms if last else terms
+
+        def late(x, at, term):
+            image[x, at, :] = image[x, at, :] + term * r["curve_early"][x, at, :]
+
+    substep(scal, middle, ext, 8, weight, 4, planes, tz, ty, inject(level - 1, 4), final, 0, width, total_x, each, late)
+    if forward:
+        add_source(scal, r["wave"][0, level + 1], weight, 4, planes, final, 0, width, total_x, late)
     if not last:
         r["to_a"][...] = final[pl.ds((1 - odd) * half, half)]
         r["to_b"][...] = final[pl.ds(odd * half, half)]
-
-
-def receivers_kernel(low_off, layers, cells_y, cells_z, scal, cells, values, loads, spots, table, planes, counts, entries):
+    elif not forward:
+        low_bit, top_bit = scal[11] & 1, scal[11] >> 3
+        shares = [[r["keep_low"], r["send_low"]], [r["keep_high"], r["send_high"]]]
+        share = 1.0 / SHOTS
+
+        def one_chunk(j, carry):
+            for which in range(2):
+                for upper, chunk in enumerate(((top_bit ^ which) * 8 + j, j * 2 + (low_bit ^ which))):
+                    at = pl.ds(pl.multiple_of(chunk * 8, 8), 8)
+                    shares[upper][which][j] = share * image[upper * half : (upper + 1) * half, at, :]
+            return carry
+
+        lax.fori_loop(0, 8, one_chunk, 0)
+
+
+def receivers_kernel(low_off, layers, cells_y, cells_z, scal, cells, values, loads, spots, table, left, rights, planes, counts, entries):
     fill_planes(scal, planes, cells_y, cells_z)
     steps, receivers = values.shape
     groups = receivers // 128
@@ -228,36 +288,11 @@
         return carry
 
     lax.fori_loop(0, filled_loads, one_load, 0)
-
-
-def image_kernel(me_ref, count, *refs):
-    fields, outs = refs[:14], refs[14:]
-    f, a = fields[:8], fields[8:]
-    me = me_ref[0]
-    low_bit, top_bit = me & 1, me >> 3
-    half = outs[0].shape[1]
-
-    def piece(x0, chunk):
-        rows = pl.ds(pl.multiple_of(chunk * 8, 8), 8)
-
-        def read(ref):
-            off = (ref.shape[0] - 2 * half) // 2
-            return ref[off + x0 : off + x0 + half, rows, :]
-
-        f_values = [read(ref) for ref in f]
-        slopes = [f_values[i + 1] - f_values[i] for i in range(7)]
-        total = read(a[0]) * (slopes[1] - slopes[0])
-        for n in range(1, 6):
-            total = total + read(a[n]) * (slopes[n + 1] - slopes[n])
-        return total * (1.0 / count)
-
-    def body(j, carry):
-        for which in range(2):
-            outs[which][j] = piece(0, (top_bit ^ which) * 8 + j)
-            outs[2 + which][j] = piece(half, j * 2 + (low_bit ^ which))
-        return carry
-
-    lax.fori_loop(0, 8, body, 0)
+    for group in range(layers // BATCH):
+        at = slice(group * BATCH * cells_y, (group + 1) * BATCH * cells_y)
+        left[at, :] = one_hot_rows(spots, 0, group * BATCH, BATCH, cells_y)
+    for step in range(steps):
+        rights[step] = right_of(table, 0, step, cells_z)
 
 
 def pack_kernel(plan, width, count, scal, *refs):
@@ -286,7 +321,7 @@
         compiler_params=pltpu.CompilerParams(vmem_limit_bytes=VLIM),
         cost_estimate=pl.CostEstimate(flops=0, bytes_accessed=4 << 20, transcendentals=0),
         name="pack",
-    )(scal, *arrays)
+    )(scal, *[pltpu.with_memory_space_constraint(x, pltpu.HBM) for x in arrays])
 
 
 def call(kernel, out_shapes, inputs, scratch=(), smem=1, cost=(0, 14 << 20), name=None, out_specs=None):
@@ -303,17 +338,16 @@
     )(*inputs[:smem], *vmem_inputs)
 
 
-VLIM = 14 * 1024 * 1024
+VLIM = 10 * 1024 * 1024
 
 
 def per_device(velocity, layer_widths, forward_prev, forward_now, adjoint_now, adjoint_later, source_cell, wavelet, receiver_cells, residuals):
     width, cells_y, cells_z = velocity.shape
     total_x = width * lax.axis_size("space")
-    shots = lax.axis_size("shot")
     half = width // 2
     me = lax.axis_index("shot").astype(jnp.int32)
     place = lax.axis_index("space").astype(jnp.int32)
-    scal = jnp.concatenate([layer_widths, (place * width)[None], source_cell[0], (place % 2)[None]])
+    scal = jnp.concatenate([layer_widths, (place * width)[None], source_cell[0], (place % 2)[None], me[None]])
     band = banded(cells_z)
     tz = jnp.asarray(np.concatenate([band, band], axis=0), BF16)
     ty = jnp.asarray(np.concatenate([banded(cells_y)] * 2, axis=1), BF16)
@@ -331,26 +365,28 @@
     a_in = exchange(*pack(scal, [an, al], (half, 4)))
     receivers = residuals.shape[2]
     slots = receivers // LOAD
-    loads, spots, table, planes = call(
+    loads, spots, table, left, rights, planes = call(
         functools.partial(receivers_kernel, 4, width + 8, cells_y, cells_z),
         [
             jax.ShapeDtypeStruct((1,), jnp.int32),
             jax.ShapeDtypeStruct((slots, LOAD), jnp.int32),
             jax.ShapeDtypeStruct((receivers, 128), F32),
+            jax.ShapeDtypeStruct(((width + 8) * cells_y, LOAD), BF16),
+            jax.ShapeDtypeStruct((residuals.shape[1], LOAD, 2 * cells_z), BF16),
             jax.ShapeDtypeStruct((3, 3, cells_y, cells_z), F32),
         ],
         [scal, receiver_cells[0], residuals[0]],
         [pltpu.VMEM((1, receivers), F32), pltpu.VMEM((128, receivers), BF16)],
         name="list_receivers",
-        out_specs=[SMEM_SPEC] + [VMEM_SPEC] * 3,
+        out_specs=[SMEM_SPEC] + [VMEM_SPEC] * 5,
     )
     tables = [("planes", planes), ("tz", tz), ("ty", ty)]
 
-    def block(first, last, forward, level, arrived, own, extra):
-        inputs = [("scal", scal), ("wave", wavelet) if forward else ("loads", loads)]
+    def block(first, last, forward, level, arrived, own, extra, after):
+        inputs = [("scal", scal), ("wave", wavelet) if forward else ("loads", loads), ("after", after)]
         inputs += [("from_a", arrived[0]), ("from_b", arrived[1]), ("own", own)] + extra + tables
         if not forward:
-            inputs += [("spots", spots), ("table", table)]
+            inputs += [("spots", spots), ("table", table), ("left", left), ("rights", rights)]
         outs, out_names = [sds(width + 8), sds(width)], ["middle", "final"]
         if first and forward:
             outs.append(sds(width + 8))
@@ -358,49 +394,67 @@
         if not last:
             outs += [sds(half)] * 2
             out_names += ["to_a", "to_b"]
+            if forward:
+                outs += [sds(width)] * 2
+                out_names += ["curve_early", "curve_recent"]
+            elif not first:
+                outs.append(sds(width))
+                out_names.append("image")
+        elif forward:
+            outs.append(sds(width))
+            out_names.append("image")
+        else:
+            outs += [jax.ShapeDtypeStruct((8, half, 8, cells_z), F32)] * 4
+            out_names += ["keep_low", "send_low", "keep_high", "send_high"]
         scratch, scratch_names = [pltpu.VMEM((width + 16, cells_y, cells_z), F32)], ["ext"]
         if first:
             scratch.append(pltpu.VMEM((width + 8, cells_y, cells_z), F32))
             scratch_names.append("prev")
+        if last:
+            outs.pop(0)
+            out_names.pop(0)
+            scratch.append(pltpu.VMEM((width + 8, cells_y, cells_z), F32))
+            scratch_names.append("middle")
+        if last and not forward:
+            scratch.append(pltpu.VMEM((width, cells_y, cells_z), F32))
+            scratch_names.append("image")
+        out_specs = [VMEM_SPEC] * len(outs)
+        outs.append(jax.ShapeDtypeStruct((1,), jnp.int32))
+        out_names.append("turn")
+        out_specs.append(SMEM_SPEC)
         names = [n for n, _ in inputs] + out_names + scratch_names
         got = call(
             functools.partial(block_kernel, first, last, forward, level, total_x, names),
             outs,
             [v for _, v in inputs],
             scratch,
-            2,
+            3,
             name=("forward" if forward else "adjoint") + "_block",
+            out_specs=out_specs,
         )
         return dict(zip(out_names, got))
 
-    def begin(forward, level, arrived, own, own_prev, extra):
-        return block(True, False, forward, level, arrived, own, [("own_prev", own_prev)] + extra)
-
-    def go_on(last, forward, level, arrived, before):
-        return block(False, last, forward, level, arrived, before["final"], [("prev", before["middle"]), ("weight", weight)])
-
-    f0 = begin(True, 0, f_in, fn, fp, [("speeds", velocity)])
+    def begin(forward, level, arrived, own, own_prev, extra, after):
+        return block(True, False, forward, level, arrived, own, [("own_prev", own_prev)] + extra, after)
+
+    def go_on(last, forward, level, arrived, before, after, more=()):
+        extra = [("prev", before["middle"]), ("weight", weight)] + list(more)
+        return block(False, last, forward, level, arrived, before["final"], extra, after)
+
+    f0 = begin(True, 0, f_in, fn, fp, [("speeds", velocity)], loads)
     weight = f0["weight"]
     f_in = exchange(f0["to_a"], f0["to_b"])
-    a0 = begin(False, 5, a_in, an, al, [("weight", weight)])
+    a0 = begin(False, 5, a_in, an, al, [("weight", weight)], f0["turn"])
     a_in = exchange(a0["to_a"], a0["to_b"])
-    f1 = go_on(False, True, 2, f_in, f0)
+    f1 = go_on(False, True, 2, f_in, f0, a0["turn"])
     f_in = exchange(f1["to_a"], f1["to_b"])
-    a1 = go_on(False, False, 3, a_in, a0)
+    curves = lambda block: [(n, block[n]) for n in ("curve_early", "curve_recent")]
+    a1 = go_on(False, False, 3, a_in, a0, f1["turn"], curves(f1))
     a_in = exchange(a1["to_a"], a1["to_b"])
-    f2 = go_on(True, True, 4, f_in, f1)
-    a2 = go_on(True, False, 1, a_in, a1)
-
-    f_all = [fp, fn, f0["middle"], f0["final"], f1["middle"], f1["final"], f2["middle"], f2["final"]]
-    a_all = [a2["final"], a2["middle"], a1["final"], a1["middle"], a0["final"], a0["middle"]]
-    part = jax.ShapeDtypeStruct((8, half, 8, cells_z), F32)
-    keep_a, send_a, keep_b, send_b = call(
-        functools.partial(lambda c, m, *refs: image_kernel(m, c, *refs), shots),
-        [part] * 4,
-        [me[None]] + f_all + a_all,
-        name="image",
-    )
-    gradient = reduce_shots(me, keep_a, send_a, keep_b, send_b)
+    fields = [("adjoint_early", a0["final"]), ("adjoint_recent", a0["middle"]), ("image_in", a1["image"])]
+    f2 = go_on(True, True, 4, f_in, f1, a1["turn"], fields)
+    a2 = go_on(True, False, 1, a_in, a1, f2["turn"], curves(f0) + [("image_in", f2["image"])])
+    gradient = reduce_shots(me, a2["keep_low"], a2["send_low"], a2["keep_high"], a2["send_high"])
     return f2["final"][None], a2["final"][None], gradient
 
 

time: 125 us -> 111 us (0.89)
  local copies, waits for them, and re-layouts: 14.4 us -> 0.84 us
  waiting for transfers between devices: 37.4 us -> 29 us
  Pallas kernels: 40.1 us -> 47.5 us
  starting transfers between devices: 29.6 us -> 32.3 us
    unnamed x74 -> x22, local copies, waits for them, and re-layouts: 14.4 us -> 0.09 us
    ppermute x6, waiting for transfers between devices: 20.1 us -> 11.5 us  [exchange(): from_b = lax.ppermute(to_b, 'space', swap_b)]
    pallas_call x8 -> x7, Pallas kernels: 38.6 us -> 43.4 us  [call(): pl.pallas_call(kernel, out_shape=out_shapes, in_specs=[SMEM_SPEC] * smem...]
    pallas_call x2, Pallas kernels: 1.46 us -> 4.02 us  [pack(): pl.pallas_call(functools.partial(pack_kernel, plan, arrays[0].shape[0], l...]
    ppermute x6, starting transfers between devices: 18.1 us -> 19.6 us  [exchange(): from_b = lax.ppermute(to_b, 'space', swap_b)]
  transfers between devices with their start and end apart: 19 -> 19, of which waited for: 9 -> 9; matrix products, arithmetic and copies ran while one was open for 0% -> 0% of each run, Pallas kernels for 21% -> 33%
where the time goes in v2:
time: 111 us
  Pallas kernels  47.5 us (43%)
  starting transfers between devices  32.3 us (29%)
  waiting for transfers between devices  29 us (26%)
    pallas_call x7, Pallas kernels, call(): pl.pallas_call(kernel, out_shape=out_shapes, in_specs=[SMEM_SPEC] * smem...  43.4 us
    ppermute x6, starting transfers between devices, exchange(): from_b = lax.ppermute(to_b, 'space', swap_b)  19.6 us
    ppermute x7, waiting for transfers between devices, flip(): lax.ppermute(value, 'shot', [(i, i ^ bit) for i in range(lax.axis_size('s...  17.5 us
    ppermute x7, starting transfers between devices, flip(): lax.ppermute(value, 'shot', [(i, i ^ bit) for i in range(lax.axis_size('s...  11.9 us
    ppermute x6, waiting for transfers between devices, exchange(): from_b = lax.ppermute(to_b, 'space', swap_b)  11.5 us
    pallas_call x2, Pallas kernels, pack(): pl.pallas_call(functools.partial(pack_kernel, plan, arrays[0].shape[0], l...  4.02 us
  transfers between devices with their start and end apart: 19, of which 9 were waited for; matrix products, arithmetic and copies ran while one was open for 0% of the time, Pallas kernels for 33%

profile of v2, /device:TPU:32, one launch (start us, length us, event | category | flops | bytes accessed | tf_op | source)
XLA Modules:
  0.0 111.3 jit_solution(6069157858142502609)
XLA Ops:
  0.6 0.8 concatenate.6.scal.refs_0_
  1.4 2.1 %pack.2 = (f32[16,128,128]{2,1,0:T(8,128)S(1)}, f32[16,128,128]{2,1,0:T(8,128)S(1)}) custom-call(s32[12]{0:T(128)S(1)} %concatenate.6.scal.refs_0_, f32[16,128,128]{2,1,0:T(8,128)} %bitcast.62, f32[16,128,128]{2,1,0:T(8,128)} %bitcast.64, f32[16,128,128]{2,1,0:T(8,128)} %refs_7_.1), custom_call_target="tpu_custom_call" | custom-call | bytes 4194304 | tf_op jit(solution)/shard_map/pack/pallas_call | solution.py:315
  3.7 5.5 %collective-permute-start.1 = (f32[16,128,128]{2,1,0:T(8,128)S(1)}, f32[16,128,128]{2,1,0:T(8,128)S(1)}, u32[]{:S(2)}, u32[]{:S(2)}) collective-permute-start(f32[16,128,128]{2,1,0:T(8,128)S(1)} %get-tuple-element.49), channel_id=1, source_target_pairs={{0,15},{1,2},{2,1},{3,4},{4,3},{5,6},{6,5},{7,8},{8,7},{9,10},{10,... | collective-permute-start | bytes 3145736 | tf_op jit(solution)/shard_map/ppermute | solution.py:360
  9.2 1.9 %pack.3 = (f32[12,128,128]{2,1,0:T(8,128)S(1)}, f32[12,128,128]{2,1,0:T(8,128)S(1)}) custom-call(s32[12]{0:T(128)S(1)} %concatenate.6.scal.refs_0_, f32[16,128,128]{2,1,0:T(8,128)} %bitcast.58, f32[16,128,128]{2,1,0:T(8,128)} %bitcast.60), custom_call_target="tpu_custom_call" | custom-call | bytes 4194304 | tf_op jit(solution)/shard_map/pack/pallas_call | solution.py:315
  11.2 0.9 collective-permute-start.3
  12.2 2.6 %list_receivers.1 = (s32[1]{0:T(128)}, s32[8,256]{1,0:T(8,128)S(1)}, f32[2048,128]{1,0:T(8,128)S(1)}, bf16[3072,256]{1,0:T(8,128)(2,1)S(1)}, bf16[6,256,256]{2,1...) custom-call(s32[12]{0:T(128)S(1)} %concatenate.6.scal.refs_0_, s32[3,2048]{1,0:T(4,128)S(1)} %bitcast.71, f32[6,2048]{1,0:T(8,128)S(1)} %bitcast.70), custom_call_target="tpu_custom_call" | custom-call | bytes 14680064 | tf_op jit(solution)/shard_map/list_receivers/pallas_call | solution.py:329
  14.8 6.8 %collective-permute-done.1.refs_4_ = f32[16,128,128]{2,1,0:T(8,128)S(1)} collective-permute-done((f32[16,128,128]{2,1,0:T(8,128)S(1)}, f32[16,128,128]{2,1,0:T(8,128)S(1)}, u32[]{:S(2)}, u32[]{:S(2)}) %collective-permute-start.1) | collective-permute-done | bytes 1048608 | tf_op jit(solution)/shard_map/ppermute | solution.py:360
  21.7 6.0 %forward_block.3 = (f32[24,128,128]{2,1,0:T(8,128)S(1)}, f32[16,128,128]{2,1,0:T(8,128)S(1)}, f32[24,128,128]{2,1,0:T(8,128)S(1)}, f32[8,128,128]{2,1,0:T(8,128)...) custom-call(s32[12]{0:T(128)S(1)} %concatenate.6.scal.refs_0_, ...), custom_call_target="tpu_custom_call" | custom-call | bytes 14680064 | tf_op jit(solution)/shard_map/forward_block/pallas_call | solution.py:329
  27.8 5.4 %collective-permute-start.5 = (f32[8,128,128]{2,1,0:T(8,128)S(1)}, f32[8,128,128]{2,1,0:T(8,128)S(1)}, u32[]{:S(2)}, u32[]{:S(2)}) collective-permute-start(f32[8,128,128]{2,1,0:T(8,128)S(1)} %get-tuple-element.61), channel_id=1, source_target_pairs={{0,15},{1,2},{2,1},{3,4},{4,3},{5,6},{6,5},{7,8},{8,7},{9,10},{10,... | collective-permute-start | bytes 1572872 | tf_op jit(solution)/shard_map/ppermute | solution.py:360
  33.3 7.2 %adjoint_block.3 = (f32[24,128,128]{2,1,0:T(8,128)S(1)}, f32[16,128,128]{2,1,0:T(8,128)S(1)}, f32[8,128,128]{2,1,0:T(8,128)S(1)}, f32[8,128,128]{2,1,0:T(8,128)S(1)}, s32[1]{0:T(128)}) custom-call(s32[12]{0:T(128)S(1)} %concatenate.6.scal.refs_0_, s32[1]{0:T(128)} %get-tuple-element.47.refs_2_.refs_1_, s32[1]{0:T(128)} %get-tuple-element.51.refs_2_, ...), custom_call_target="tpu_custom_call" | custom-call | bytes 14680064 | tf_op jit(solution)/shard_map/adjoint_block/pallas_call | solution.py:329
  40.6 2.2 %collective-permute-start.7 = (f32[8,128,128]{2,1,0:T(8,128)S(1)}, f32[8,128,128]{2,1,0:T(8,128)S(1)}, u32[]{:S(2)}, u32[]{:S(2)}) collective-permute-start(f32[8,128,128]{2,1,0:T(8,128)S(1)} %get-tuple-element.66), channel_id=1, source_target_pairs={{0,15},{1,2},{2,1},{3,4},{4,3},{5,6},{6,5},{7,8},{8,7},{9,10},{10,... | collective-permute-start | bytes 1572872 | tf_op jit(solution)/shard_map/ppermute | solution.py:360
  42.8 5.6 %forward_block.4 = (f32[24,128,128]{2,1,0:T(8,128)S(1)}, f32[16,128,128]{2,1,0:T(8,128)S(1)}, f32[8,128,128]{2,1,0:T(8,128)S(1)}, f32[8,128,128]{2,1,0:T(8,128)S...) custom-call(s32[12]{0:T(128)S(1)} %concatenate.6.scal.refs_0_, f32[1,6]{1,0:T(1,128)S(1)} %copy-done.7, ...), custom_call_target="tpu_custom_call" | custom-call | bytes 14680064 | tf_op jit(solution)/shard_map/forward_block/pallas_call | solution.py:329
  48.4 0.3 collective-permute-start.8
  48.7 3.3 %collective-permute-start.9 = (f32[8,128,128]{2,1,0:T(8,128)S(1)}, f32[8,128,128]{2,1,0:T(8,128)S(1)}, u32[]{:S(2)}, u32[]{:S(2)}) collective-permute-start(f32[8,128,128]{2,1,0:T(8,128)S(1)} %get-tuple-element.73), channel_id=1, source_target_pairs={{0,15},{1,2},{2,1},{3,4},{4,3},{5,6},{6,5},{7,8},{8,7},{9,10},{10,... | collective-permute-start | bytes 1572872 | tf_op jit(solution)/shard_map/ppermute | solution.py:360
  52.0 0.9 collective-permute-done.7.refs_4_
  52.9 7.6 %adjoint_block.4 = (f32[24,128,128]{2,1,0:T(8,128)S(1)}, f32[16,128,128]{2,1,0:T(8,128)S(1)}, f32[8,128,128]{2,1,0:T(8,128)S(1)}, f32[8,128,128]{2,1,0:T(8,128)S...) custom-call(s32[12]{0:T(128)S(1)} %concatenate.6.scal.refs_0_, s32[1]{0:T(128)} %get-tuple-element.47.refs_2_.refs_1_, ...), custom_call_target="tpu_custom_call" | custom-call | bytes 14680064 | tf_op jit(solution)/shard_map/adjoint_block/pallas_call | solution.py:329
  60.5 2.2 %collective-permute-start.11 = (f32[8,128,128]{2,1,0:T(8,128)S(1)}, f32[8,128,128]{2,1,0:T(8,128)S(1)}, u32[]{:S(2)}, u32[]{:S(2)}) collective-permute-start(f32[8,128,128]{2,1,0:T(8,128)S(1)} %get-tuple-element.80), channel_id=1, source_target_pairs={{0,15},{1,2},{2,1},{3,4},{4,3},{5,6},{6,5},{7,8},{8,7},{9,10},{10,... | collective-permute-start | bytes 1572872 | tf_op jit(solution)/shard_map/ppermute | solution.py:360
  62.8 6.2 %forward_block.5 = (f32[16,128,128]{2,1,0:T(8,128)}, f32[16,128,128]{2,1,0:T(8,128)S(1)}, s32[1]{0:T(128)}) custom-call(s32[12]{0:T(128)S(1)} %concatenate.6.scal.refs_0_, f32[1,6]{1,0:T(1,128)S(1)} %copy-done.7, s32[1]{0:T(128)} %get-tuple-element.71.refs_2_, f32[8,128,128]{2,1,0:T(8,128)S(1)} %collective-permute-done.8.refs_3_, ...), custom_call_target="tpu_custom_call" | custom-call | bytes 14680064 | tf_op jit(solution)/shard_map/forward_block/pallas_call | solution.py:329
  69.0 3.9 %collective-permute-done.11.refs_4_ = f32[8,128,128]{2,1,0:T(8,128)S(1)} collective-permute-done((f32[8,128,128]{2,1,0:T(8,128)S(1)}, f32[8,128,128]{2,1,0:T(8,128)S(1)}, u32[]{:S(2)}, u32[]{:S(2)}) %collective-permute-start.11) | collective-permute-done | bytes 524320 | tf_op jit(solution)/shard_map/ppermute | solution.py:360
  72.9 8.2 %adjoint_block.5 = (f32[16,128,128]{2,1,0:T(8,128)}, f32[8,8,8,128]{3,2,1,0:T(8,128)S(1)}, f32[8,8,8,128]{3,2,1,0:T(8,128)S(1)}, f32[8,8,8,128]{3,2,1,0:T(8,128)...) custom-call(s32[12]{0:T(128)S(1)} %concatenate.6.scal.refs_0_, s32[1]{0:T(128)} %get-tuple-element.47.refs_2_.refs_1_, ...), custom_call_target="tpu_custom_call" | custom-call | bytes 14680064 | tf_op jit(solution)/shard_map/adjoint_block/pallas_call | solution.py:329
  81.1 0.2 collective-permute-start.14
  81.3 0.7 collective-permute-start.12
  82.0 6.4 %collective-permute-done.14 = f32[8,8,8,128]{3,2,1,0:T(8,128)S(1)} collective-permute-done((f32[8,8,8,128]{3,2,1,0:T(8,128)S(1)}, f32[8,8,8,128]{3,2,1,0:T(8,128)S(1)}, u32[]{:S(2)}, u32[]{:S(2)}) %collective-permute-start.14) | collective-permute-done | bytes 262176 | tf_op jit(solution)/shard_map/ppermute | solution.py:462
  88.5 0.6 collective-permute-done.12
  89.1 1.7 %collective-permute-start.13 = (f32[4,8,8,128]{3,2,1,0:T(8,128)S(1)}, f32[4,8,8,128]{3,2,1,0:T(8,128)S(1)}, u32[]{:S(2)}, u32[]{:S(2)}) collective-permute-start(f32[4,8,8,128]{3,2,1,0:T(8,128)S(1)} %fusion), channel_id=1, source_target_pairs={{0,16},{16,0},{32,48},{48,32},{64,80},{80,64},{96,112},{112,96},{1... | collective-permute-start | bytes 393224 | tf_op jit(solution)/shard_map/ppermute | solution.py:462
  90.8 2.6 %collective-permute-done.15 = f32[4,8,8,128]{3,2,1,0:T(8,128)S(1)} collective-permute-done((f32[4,8,8,128]{3,2,1,0:T(8,128)S(1)}, f32[4,8,8,128]{3,2,1,0:T(8,128)S(1)}, u32[]{:S(2)}, u32[]{:S(2)}) %collective-permute-start.15) | collective-permute-done | bytes 131104 | tf_op jit(solution)/shard_map/ppermute | solution.py:462
  93.5 1.1 collective-permute-done.13
  94.6 3.7 %collective-permute-start.16 = (f32[16,8,128]{2,1,0:T(8,128)S(1)}, f32[16,8,128]{2,1,0:T(8,128)S(1)}, u32[]{:S(2)}, u32[]{:S(2)}) collective-permute-start(f32[16,8,128]{2,1,0:T(8,128)S(1)} %get-tuple-element.91), channel_id=1, source_target_pairs={{0,32},{16,48},{32,0},{48,16},{64,96},{80,112},{96,64},{112,80},{1... | collective-permute-start | bytes 196616 | tf_op jit(solution)/shard_map/ppermute | solution.py:462
  98.3 5.5 %collective-permute-start.17 = (f32[16,8,128]{2,1,0:T(8,128)S(1)}, f32[16,8,128]{2,1,0:T(8,128)S(1)}, u32[]{:S(2)}, u32[]{:S(2)}) collective-permute-start(f32[16,8,128]{2,1,0:T(8,128)S(1)} %get-tuple-element.92), channel_id=1, source_target_pairs={{0,64},{16,80},{32,96},{48,112},{64,0},{80,16},{96,32},{112,48},{1... | collective-permute-start | bytes 196616 | tf_op jit(solution)/shard_map/ppermute | solution.py:462
  103.8 4.0 %collective-permute-done.17 = f32[16,8,128]{2,1,0:T(8,128)S(1)} collective-permute-done((f32[16,8,128]{2,1,0:T(8,128)S(1)}, f32[16,8,128]{2,1,0:T(8,128)S(1)}, u32[]{:S(2)}, u32[]{:S(2)}) %collective-permute-start.17) | collective-permute-done | bytes 65568 | tf_op jit(solution)/shard_map/ppermute | solution.py:462
  107.9 2.8 %collective-permute-done.18 = f32[16,8,128]{2,1,0:T(8,128)S(1)} collective-permute-done((f32[16,8,128]{2,1,0:T(8,128)S(1)}, f32[16,8,128]{2,1,0:T(8,128)S(1)}, u32[]{:S(2)}, u32[]{:S(2)}) %collective-permute-start.18) | collective-permute-done | bytes 65568 | tf_op jit(solution)/shard_map/ppermute | solution.py:462
  110.6 0.6 fusion.9
  (44 shorter events, 0.8 us)
Async XLA Ops:
  1.4 10.7 %copy-start.8 = (f32[1,6,2048]{2,0,1:T(1,128)S(1)}, f32[1,6,2048]{2,0,1:T(1,128)}, u32[]{:S(2)}) copy-start(f32[1,6,2048]{2,0,1:T(1,128)} %param.21) | copy-start | bytes 147460
  1.4 10.8 %copy-start.9 = (s32[1,3,2048]{2,0,1:T(1,128)S(1)}, s32[1,3,2048]{2,0,1:T(1,128)}, u32[]{:S(2)}) copy-start(s32[1,3,2048]{2,0,1:T(1,128)} %param.20) | copy-start | bytes 73732
  1.4 20.2 %copy-start.4 = (f32[16,128,128]{2,1,0:T(8,128)S(1)}, f32[16,128,128]{2,1,0:T(8,128)}, u32[]{:S(2)}) copy-start(f32[16,128,128]{2,1,0:T(8,128)} %refs_7_.1) | copy-start | bytes 3145732
  3.5 18.1 %copy-start.2 = (f32[1,16,128,128]{3,2,1,0:T(8,128)S(1)}, f32[1,16,128,128]{3,2,1,0:T(8,128)}, u32[]{:S(2)}) copy-start(f32[1,16,128,128]{3,2,1,0:T(8,128)} %param.15) | copy-start | bytes 3145732
  3.5 18.1 %copy-start.3 = (f32[1,16,128,128]{3,2,1,0:T(8,128)S(1)}, f32[1,16,128,128]{3,2,1,0:T(8,128)}, u32[]{:S(2)}) copy-start(f32[1,16,128,128]{3,2,1,0:T(8,128)} %param.14) | copy-start | bytes 3145732
  3.5 18.1 %copy-start.5 = (bf16[256,128]{1,0:T(8,128)(2,1)S(1)}, bf16[256,128]{1,0:T(8,128)(2,1)}, u32[]{:S(2)}) copy-start(bf16[256,128]{1,0:T(8,128)(2,1)} %constant.62.clone.refs_9_.refs_11_.refs_12_) | copy-start | bytes 196612
  3.5 18.1 %copy-start.6 = (bf16[128,256]{1,0:T(8,128)(2,1)S(1)}, bf16[128,256]{1,0:T(8,128)(2,1)}, u32[]{:S(2)}) copy-start(bf16[128,256]{1,0:T(8,128)(2,1)} %constant.63.clone.refs_10_.refs_12_.refs_13_) | copy-start | bytes 196612
  3.6 18.1 %copy-start.7 = (f32[1,6]{1,0:T(1,128)S(1)}, f32[1,6]{1,0:T(1,128)}, u32[]{:S(2)}) copy-start(f32[1,6]{1,0:T(1,128)} %refs_1_.5) | copy-start | bytes 76
  3.6 11.3 %collective-permute-start = (f32[16,128,128]{2,1,0:T(8,128)S(1)}, f32[16,128,128]{2,1,0:T(8,128)S(1)}, u32[]{:S(2)}, u32[]{:S(2)}) collective-permute-start(f32[16,128,128]{2,1,0:T(8,128)S(1)} %get-tuple-element.48), channel_id=1, source_target_pairs={{0,1},{1,0},{2,3},{3,2},{4,5},{5,4},{6,7},{7,6},{8,9},{9,8},{10,11... | collective-permute-start | bytes 3145736 | tf_op jit(solution)/shard_map/ppermute | solution.py:361
  3.7 18.0 %collective-permute-start.1 = (f32[16,128,128]{2,1,0:T(8,128)S(1)}, f32[16,128,128]{2,1,0:T(8,128)S(1)}, u32[]{:S(2)}, u32[]{:S(2)}) collective-permute-start(f32[16,128,128]{2,1,0:T(8,128)S(1)} %get-tuple-element.49), channel_id=1, source_target_pairs={{0,15},{1,2},{2,1},{3,4},{4,3},{5,6},{6,5},{7,8},{8,7},{9,10},{10,... | collective-permute-start | bytes 3145736 | tf_op jit(solution)/shard_map/ppermute | solution.py:360
  11.1 22.2 %collective-permute-start.2 = (f32[12,128,128]{2,1,0:T(8,128)S(1)}, f32[12,128,128]{2,1,0:T(8,128)S(1)}, u32[]{:S(2)}, u32[]{:S(2)}) collective-permute-start(f32[12,128,128]{2,1,0:T(8,128)S(1)} %get-tuple-element.52), channel_id=1, source_target_pairs={{0,1},{1,0},{2,3},{3,2},{4,5},{5,4},{6,7},{7,6},{8,9},{9,8},{10,11... | collective-permute-start | bytes 2359304 | tf_op jit(solution)/shard_map/ppermute | solution.py:361
  11.2 22.1 %collective-permute-start.3 = (f32[12,128,128]{2,1,0:T(8,128)S(1)}, f32[12,128,128]{2,1,0:T(8,128)S(1)}, u32[]{:S(2)}, u32[]{:S(2)}) collective-permute-start(f32[12,128,128]{2,1,0:T(8,128)S(1)} %get-tuple-element.53), channel_id=1, source_target_pairs={{0,15},{1,2},{2,1},{3,4},{4,3},{5,6},{6,5},{7,8},{8,7},{9,10},{10,... | collective-permute-start | bytes 2359304 | tf_op jit(solution)/shard_map/ppermute | solution.py:360
  21.7 11.6 %copy-start = (f32[1,16,128,128]{3,2,1,0:T(8,128)S(1)}, f32[1,16,128,128]{3,2,1,0:T(8,128)}, u32[]{:S(2)}) copy-start(f32[1,16,128,128]{3,2,1,0:T(8,128)} %param.16) | copy-start | bytes 3145732
  21.7 11.6 %copy-start.1 = (f32[1,16,128,128]{3,2,1,0:T(8,128)S(1)}, f32[1,16,128,128]{3,2,1,0:T(8,128)}, u32[]{:S(2)}) copy-start(f32[1,16,128,128]{3,2,1,0:T(8,128)} %param.17) | copy-start | bytes 3145732
  27.7 15.1 %collective-permute-start.4 = (f32[8,128,128]{2,1,0:T(8,128)S(1)}, f32[8,128,128]{2,1,0:T(8,128)S(1)}, u32[]{:S(2)}, u32[]{:S(2)}) collective-permute-start(f32[8,128,128]{2,1,0:T(8,128)S(1)} %get-tuple-element.60), channel_id=1, source_target_pairs={{0,1},{1,0},{2,3},{3,2},{4,5},{5,4},{6,7},{7,6},{8,9},{9,8},{10,11... | collective-permute-start | bytes 1572872 | tf_op jit(solution)/shard_map/ppermute | solution.py:361
  27.8 15.0 %collective-permute-start.5 = (f32[8,128,128]{2,1,0:T(8,128)S(1)}, f32[8,128,128]{2,1,0:T(8,128)S(1)}, u32[]{:S(2)}, u32[]{:S(2)}) collective-permute-start(f32[8,128,128]{2,1,0:T(8,128)S(1)} %get-tuple-element.61), channel_id=1, source_target_pairs={{0,15},{1,2},{2,1},{3,4},{4,3},{5,6},{6,5},{7,8},{8,7},{9,10},{10,... | collective-permute-start | bytes 1572872 | tf_op jit(solution)/shard_map/ppermute | solution.py:360
  40.5 11.5 %collective-permute-start.6 = (f32[8,128,128]{2,1,0:T(8,128)S(1)}, f32[8,128,128]{2,1,0:T(8,128)S(1)}, u32[]{:S(2)}, u32[]{:S(2)}) collective-permute-start(f32[8,128,128]{2,1,0:T(8,128)S(1)} %get-tuple-element.65), channel_id=1, source_target_pairs={{0,1},{1,0},{2,3},{3,2},{4,5},{5,4},{6,7},{7,6},{8,9},{9,8},{10,11... | collective-permute-start | bytes 1572872 | tf_op jit(solution)/shard_map/ppermute | solution.py:361
  40.6 12.3 %collective-permute-start.7 = (f32[8,128,128]{2,1,0:T(8,128)S(1)}, f32[8,128,128]{2,1,0:T(8,128)S(1)}, u32[]{:S(2)}, u32[]{:S(2)}) collective-permute-start(f32[8,128,128]{2,1,0:T(8,128)S(1)} %get-tuple-element.66), channel_id=1, source_target_pairs={{0,15},{1,2},{2,1},{3,4},{4,3},{5,6},{6,5},{7,8},{8,7},{9,10},{10,... | collective-permute-start | bytes 1572872 | tf_op jit(solution)/shard_map/ppermute | solution.py:360
  48.4 14.4 %collective-permute-start.8 = (f32[8,128,128]{2,1,0:T(8,128)S(1)}, f32[8,128,128]{2,1,0:T(8,128)S(1)}, u32[]{:S(2)}, u32[]{:S(2)}) collective-permute-start(f32[8,128,128]{2,1,0:T(8,128)S(1)} %get-tuple-element.72), channel_id=1, source_target_pairs={{0,1},{1,0},{2,3},{3,2},{4,5},{5,4},{6,7},{7,6},{8,9},{9,8},{10,11... | collective-permute-start | bytes 1572872 | tf_op jit(solution)/shard_map/ppermute | solution.py:361
  48.7 14.1 %collective-permute-start.9 = (f32[8,128,128]{2,1,0:T(8,128)S(1)}, f32[8,128,128]{2,1,0:T(8,128)S(1)}, u32[]{:S(2)}, u32[]{:S(2)}) collective-permute-start(f32[8,128,128]{2,1,0:T(8,128)S(1)} %get-tuple-element.73), channel_id=1, source_target_pairs={{0,15},{1,2},{2,1},{3,4},{4,3},{5,6},{6,5},{7,8},{8,7},{9,10},{10,... | collective-permute-start | bytes 1572872 | tf_op jit(solution)/shard_map/ppermute | solution.py:360
  60.4 8.5 %collective-permute-start.10 = (f32[8,128,128]{2,1,0:T(8,128)S(1)}, f32[8,128,128]{2,1,0:T(8,128)S(1)}, u32[]{:S(2)}, u32[]{:S(2)}) collective-permute-start(f32[8,128,128]{2,1,0:T(8,128)S(1)} %get-tuple-element.79), channel_id=1, source_target_pairs={{0,1},{1,0},{2,3},{3,2},{4,5},{5,4},{6,7},{7,6},{8,9},{9,8},{10,11... | collective-permute-start | bytes 1572872 | tf_op jit(solution)/shard_map/ppermute | solution.py:361
  60.5 12.3 %collective-permute-start.11 = (f32[8,128,128]{2,1,0:T(8,128)S(1)}, f32[8,128,128]{2,1,0:T(8,128)S(1)}, u32[]{:S(2)}, u32[]{:S(2)}) collective-permute-start(f32[8,128,128]{2,1,0:T(8,128)S(1)} %get-tuple-element.80), channel_id=1, source_target_pairs={{0,15},{1,2},{2,1},{3,4},{4,3},{5,6},{6,5},{7,8},{8,7},{9,10},{10,... | collective-permute-start | bytes 1572872 | tf_op jit(solution)/shard_map/ppermute | solution.py:360
  81.1 7.2 %collective-permute-start.14 = (f32[8,8,8,128]{3,2,1,0:T(8,128)S(1)}, f32[8,8,8,128]{3,2,1,0:T(8,128)S(1)}, u32[]{:S(2)}, u32[]{:S(2)}) collective-permute-start(f32[8,8,8,128]{3,2,1,0:T(8,128)S(1)} %get-tuple-element.90), channel_id=1, source_target_pairs={{0,16},{16,0},{32,48},{48,32},{64,80},{80,64},{96,112},{112,96},{1... | collective-permute-start | bytes 786440 | tf_op jit(solution)/shard_map/ppermute | solution.py:462
  81.3 7.8 %collective-permute-start.12 = (f32[8,8,8,128]{3,2,1,0:T(8,128)S(1)}, f32[8,8,8,128]{3,2,1,0:T(8,128)S(1)}, u32[]{:S(2)}, u32[]{:S(2)}) collective-permute-start(f32[8,8,8,128]{3,2,1,0:T(8,128)S(1)} %get-tuple-element.88), channel_id=1, source_target_pairs={{0,128},{16,144},{32,160},{48,176},{64,192},{80,208},{96,224},{112... | collective-permute-start | bytes 786440 | tf_op jit(solution)/shard_map/ppermute | solution.py:462
  88.4 5.1 %collective-permute-start.15 = (f32[4,8,8,128]{3,2,1,0:T(8,128)S(1)}, f32[4,8,8,128]{3,2,1,0:T(8,128)S(1)}, u32[]{:S(2)}, u32[]{:S(2)}) collective-permute-start(f32[4,8,8,128]{3,2,1,0:T(8,128)S(1)} %add_bitcast_fusion), channel_id=1, source_target_pairs={{0,128},{16,144},{32,160},{48,176},{64,192},{80,208},{96,224},{112... | collective-permute-start | bytes 393224 | tf_op jit(solution)/shard_map/ppermute | solution.py:462
  89.1 5.5 %collective-permute-start.13 = (f32[4,8,8,128]{3,2,1,0:T(8,128)S(1)}, f32[4,8,8,128]{3,2,1,0:T(8,128)S(1)}, u32[]{:S(2)}, u32[]{:S(2)}) collective-permute-start(f32[4,8,8,128]{3,2,1,0:T(8,128)S(1)} %fusion), channel_id=1, source_target_pairs={{0,16},{16,0},{32,48},{48,32},{64,80},{80,64},{96,112},{112,96},{1... | collective-permute-start | bytes 393224 | tf_op jit(solution)/shard_map/ppermute | solution.py:462
  94.6 9.2 %collective-permute-start.16 = (f32[16,8,128]{2,1,0:T(8,128)S(1)}, f32[16,8,128]{2,1,0:T(8,128)S(1)}, u32[]{:S(2)}, u32[]{:S(2)}) collective-permute-start(f32[16,8,128]{2,1,0:T(8,128)S(1)} %get-tuple-element.91), channel_id=1, source_target_pairs={{0,32},{16,48},{32,0},{48,16},{64,96},{80,112},{96,64},{112,80},{1... | collective-permute-start | bytes 196616 | tf_op jit(solution)/shard_map/ppermute | solution.py:462
  98.3 9.6 %collective-permute-start.17 = (f32[16,8,128]{2,1,0:T(8,128)S(1)}, f32[16,8,128]{2,1,0:T(8,128)S(1)}, u32[]{:S(2)}, u32[]{:S(2)}) collective-permute-start(f32[16,8,128]{2,1,0:T(8,128)S(1)} %get-tuple-element.92), channel_id=1, source_target_pairs={{0,64},{16,80},{32,96},{48,112},{64,0},{80,16},{96,32},{112,48},{1... | collective-permute-start | bytes 196616 | tf_op jit(solution)/shard_map/ppermute | solution.py:462
  103.8 6.8 %collective-permute-start.18 = (f32[16,8,128]{2,1,0:T(8,128)S(1)}, f32[16,8,128]{2,1,0:T(8,128)S(1)}, u32[]{:S(2)}, u32[]{:S(2)}) collective-permute-start(f32[16,8,128]{2,1,0:T(8,128)S(1)} %get-tuple-element.93), channel_id=1, source_target_pairs={{0,96},{16,112},{32,64},{48,80},{64,32},{80,48},{96,0},{112,16},{1... | collective-permute-start | bytes 196616 | tf_op jit(solution)/shard_map/ppermute | solution.py:462

commit v3 on v2

--- a/solution.py
+++ b/solution.py
@@ -9,7 +9,7 @@
 from jax.sharding import PartitionSpec as P
 
 SCALE = 5040.0
-CENTRE = -43050.0
+CENTRE_Z, CENTRE_Y = -43008.0, -42.0
 SIDE = (8064.0, -1008.0, 128.0, -9.0)
 DT_OVER_H = 0.07
 DAMPING_RATE = 0.15
@@ -22,11 +22,12 @@
 VMEM_SPEC = pl.BlockSpec(memory_space=pltpu.VMEM)
 
 
-def banded(n):
+def banded(n, centre):
     offset = np.abs(np.arange(n)[:, None] - np.arange(n)[None, :])
     band = np.zeros((n, n), np.float32)
     for distance, coeff in enumerate(SIDE, start=1):
         band[offset == distance] = coeff
+    band[offset == 0] = centre
     return band
 
 
@@ -45,8 +46,7 @@
         inverse = 1.0 / (1.0 + damp)
         planes[kind, 0] = inverse
         planes[kind, 1] = 2.0 * inverse
-        planes[kind, 2] = (1.0 - damp) * inverse
-    planes[2] = jnp.zeros((3, cells_y, cells_z), F32)
+    planes[2] = jnp.zeros((2, cells_y, cells_z), F32)
 
 
 def kind_of(scal, x, total_x):
@@ -84,14 +84,18 @@
         base = group * BATCH
         high, low = halves(src[pl.ds(base + 4, BATCH)])
         side_by_side = jnp.concatenate([high, low], axis=2).reshape(BATCH * cells_y, 2 * cells_z)
-        along_z = jnp.dot(side_by_side, tz, preferred_element_type=F32)
+        along = tz
+        if inject is not None:
+            first_row = pl.multiple_of((base + inject_off) * cells_y, cells_y)
+            left = r["left"][pl.ds(first_row, BATCH * cells_y), :]
+            side_by_side, along = jnp.concatenate([side_by_side, left], axis=1), r["rights"][level]
+        along_z = jnp.dot(side_by_side, along, preferred_element_type=F32)
+        if inject is not None:
+            along_z = along_z[:, :cells_z] + along_z[:, cells_z:]
         stacked = jnp.concatenate(
             [jnp.concatenate([part[u] for u in range(BATCH)], axis=1) for part in (high, low)], axis=0
         )
         along_y = jnp.dot(ty, stacked, preferred_element_type=F32)
-        if inject is not None:
-            first_row = pl.multiple_of((base + inject_off) * cells_y, cells_y)
-            along_z = along_z + placed(r["left"][pl.ds(first_row, BATCH * cells_y), :], r["rights"][level], cells_z)
         partial = [
             along_z[u * cells_y : (u + 1) * cells_y] + along_y[:, u * cells_z : (u + 1) * cells_z]
             for u in range(BATCH)
@@ -102,16 +106,12 @@
             column = [src[base + i, at, :] for i in range(BATCH + 8)]
             for u in range(BATCH):
                 centre = column[u + 4]
-                total = partial[u][at, :] + CENTRE * centre
+                total = partial[u][at, :]
                 for distance, coeff in enumerate(SIDE, start=1):
                     total = total + coeff * (column[u + 4 - distance] + column[u + 4 + distance])
                 kind = kinds[u]
                 before = prev[base + u + prev_off, at, :]
-                new = (
-                    planes[kind, 0, at, :] * (weight[base + u + weight_off, at, :] * total)
-                    + planes[kind, 1, at, :] * centre
-                    - planes[kind, 2, at, :] * before
-                )
+                new = weight[base + u + weight_off, at, :] * total + (planes[kind, 1, at, :] * (centre - before) + before)
                 dest[base + u, at, :] = new
                 if each is not None:
                     each(base + u, at, new, centre, before)
@@ -125,8 +125,7 @@
 
             def one_layer(x, c):
                 left = one_hot_rows(r["spots"], load, x + inject_off, 1, cells_y)
-                kind = kind_of(scal, low_x + x, total_x)
-                term = planes[kind, 0] * (weight[x + weight_off] * placed(left, more, cells_z))
+                term = weight[x + weight_off] * placed(left, more, cells_z)
                 dest[x] = dest[x] + term
                 if late is not None:
                     late(x, slice(None), term)
@@ -137,15 +136,14 @@
         lax.fori_loop(1, r["loads"][0], another_load, 0)
 
 
-def add_source(scal, amplitude, weight, weight_off, planes, dest, low_x, layers, total_x, late=None):
+def add_source(scal, amplitude, weight, weight_off, dest, low_x, layers, late=None):
     x = scal[7] - scal[6] - low_x
 
     @pl.when((x >= 0) & (x < layers))
     def _():
-        kind = kind_of(scal, low_x + x, total_x)
         row = pl.ds(scal[8], 1)
         lane = lax.broadcasted_iota(jnp.int32, (1, dest.shape[2]), 1)
-        gain = planes[kind, 0, row, :] * weight[x + weight_off, row, :] * (SCALE * amplitude)
+        gain = weight[x + weight_off, row, :] * (SCALE * amplitude)
         term = jnp.where(lane == scal[9], gain, 0.0)
         dest[x, row, :] = dest[x, row, :] + term
         if late is not None:
@@ -169,13 +167,19 @@
         prev = r["prev"]
         thin_a, thin_b = pl.ds((1 - odd) * (4 + width), 4), pl.ds(odd * (4 + width), 4)
         prev[thin_a] = r["from_a"][8:12]
-        prev[thin_b] = r["from_b"][8:12]
+        prev[thin_b] = jnp.where(at_edge, 0.0, r["from_b"][8:12])
         prev[4 : 4 + width] = r["own_prev"][...]
         if forward:
             gain = DT_OVER_H * DT_OVER_H / SCALE
             weight[thin_a] = gain * r["from_a"][12:] * r["from_a"][12:]
             weight[thin_b] = gain * r["from_b"][12:] * r["from_b"][12:]
             weight[4 : 4 + width] = gain * r["speeds"][...] * r["speeds"][...]
+
+            def damp(x, carry):
+                weight[x] = planes[kind_of(scal, x - 4, total_x), 0] * weight[x]
+                return carry
+
+            lax.fori_loop(0, width + 8, damp, 0)
     else:
         prev = r["prev"]
     tz, ty = r["tz"][...], r["ty"][...]
@@ -183,7 +187,7 @@
     inject = (lambda n, off: None) if forward else (lambda n, off: (r, n, off))
     substep(scal, ext, prev, 0, weight, 0, planes, tz, ty, inject(level, 0), middle, -4, width + 8, total_x)
     if forward:
-        add_source(scal, r["wave"][0, level], weight, 0, planes, middle, -4, width + 8, total_x)
+        add_source(scal, r["wave"][0, level], weight, 0, middle, -4, width + 8)
 
     each = late = None
     image = r.get("image")
@@ -221,7 +225,7 @@
 
     substep(scal, middle, ext, 8, weight, 4, planes, tz, ty, inject(level - 1, 4), final, 0, width, total_x, each, late)
     if forward:
-        add_source(scal, r["wave"][0, level + 1], weight, 4, planes, final, 0, width, total_x, late)
+        add_source(scal, r["wave"][0, level + 1], weight, 4, final, 0, width, late)
     if not last:
         r["to_a"][...] = final[pl.ds((1 - odd) * half, half)]
         r["to_b"][...] = final[pl.ds(odd * half, half)]
@@ -240,7 +244,7 @@
         lax.fori_loop(0, 8, one_chunk, 0)
 
 
-def receivers_kernel(low_off, layers, cells_y, cells_z, scal, cells, values, loads, spots, table, left, rights, planes, counts, entries):
+def receivers_kernel(low_off, layers, cells_y, cells_z, scal, cells, values, tz, loads, spots, table, left, rights, planes, counts, entries):
     fill_planes(scal, planes, cells_y, cells_z)
     steps, receivers = values.shape
     groups = receivers // 128
@@ -292,7 +296,9 @@
         at = slice(group * BATCH * cells_y, (group + 1) * BATCH * cells_y)
         left[at, :] = one_hot_rows(spots, 0, group * BATCH, BATCH, cells_y)
     for step in range(steps):
-        rights[step] = right_of(table, 0, step, cells_z)
+        right = right_of(table, 0, step, cells_z)
+        beside = jnp.concatenate([tz[...], jnp.zeros(tz.shape, BF16)], axis=1)
+        rights[step] = jnp.concatenate([beside, right], axis=0)
 
 
 def pack_kernel(plan, width, count, scal, *refs):
@@ -348,9 +354,9 @@
     me = lax.axis_index("shot").astype(jnp.int32)
     place = lax.axis_index("space").astype(jnp.int32)
     scal = jnp.concatenate([layer_widths, (place * width)[None], source_cell[0], (place % 2)[None], me[None]])
-    band = banded(cells_z)
+    band = banded(cells_z, CENTRE_Z)
     tz = jnp.asarray(np.concatenate([band, band], axis=0), BF16)
-    ty = jnp.asarray(np.concatenate([banded(cells_y)] * 2, axis=1), BF16)
+    ty = jnp.asarray(np.concatenate([banded(cells_y, CENTRE_Y)] * 2, axis=1), BF16)
     sds = lambda n: jax.ShapeDtypeStruct((n, cells_y, cells_z), F32)
     count = lax.axis_size("space")
     swap_a = [(i, i ^ 1) for i in range(count)]
@@ -372,10 +378,10 @@
             jax.ShapeDtypeStruct((slots, LOAD), jnp.int32),
             jax.ShapeDtypeStruct((receivers, 128), F32),
             jax.ShapeDtypeStruct(((width + 8) * cells_y, LOAD), BF16),
-            jax.ShapeDtypeStruct((residuals.shape[1], LOAD, 2 * cells_z), BF16),
-            jax.ShapeDtypeStruct((3, 3, cells_y, cells_z), F32),
+            jax.ShapeDtypeStruct((residuals.shape[1], 2 * cells_z + LOAD, 2 * cells_z), BF16),
+            jax.ShapeDtypeStruct((3, 2, cells_y, cells_z), F32),
         ],
-        [scal, receiver_cells[0], residuals[0]],
+        [scal, receiver_cells[0], residuals[0], tz],
         [pltpu.VMEM((1, receivers), F32), pltpu.VMEM((128, receivers), BF16)],
         name="list_receivers",
         out_specs=[SMEM_SPEC] + [VMEM_SPEC] * 5,

time: 111 us -> 110 us (level)
  Pallas kernels: 47.5 us -> 45 us
    pallas_call x7, Pallas kernels: 43.4 us -> 41 us  [call(): pl.pallas_call(kernel, out_shape=out_shapes, in_specs=[SMEM_SPEC] * smem...]
  transfers between devices with their start and end apart: 19 -> 19, of which waited for: 9 -> 9; matrix products, arithmetic and copies ran while one was open for 0% -> 0% of each run, Pallas kernels for 33% -> 32%
where the time goes in v3:
time: 110 us; the launch traced here: 109 us
  Pallas kernels  45 us (41%)
  starting transfers between devices  32.5 us (30%)
  waiting for transfers between devices  29.3 us (27%)
    pallas_call x7, Pallas kernels, call(): pl.pallas_call(kernel, out_shape=out_shapes, in_specs=[SMEM_SPEC] * smem...  41 us
    ppermute x6, starting transfers between devices, exchange(): from_b = lax.ppermute(to_b, 'space', swap_b)  19.9 us
    ppermute x7, waiting for transfers between devices, flip(): lax.ppermute(value, 'shot', [(i, i ^ bit) for i in range(lax.axis_size('s...  17.4 us
    ppermute x7, starting transfers between devices, flip(): lax.ppermute(value, 'shot', [(i, i ^ bit) for i in range(lax.axis_size('s...  11.9 us
    ppermute x6, waiting for transfers between devices, exchange(): from_b = lax.ppermute(to_b, 'space', swap_b)  11.9 us
    pallas_call x2, Pallas kernels, pack(): pl.pallas_call(functools.partial(pack_kernel, plan, arrays[0].shape[0], l...  4.02 us
  transfers between devices with their start and end apart: 19, of which 9 were waited for; matrix products, arithmetic and copies ran while one was open for 0% of the time, Pallas kernels for 32%

profile of v3, /device:TPU:32, one launch (start us, length us, event | category | flops | bytes accessed | tf_op | source)
XLA Modules:
  0.0 109.4 jit_solution(16385653316443914632)
XLA Ops:
  0.6 0.8 concatenate.6.scal.refs_0_
  1.4 2.1 %pack.2 = (f32[16,128,128]{2,1,0:T(8,128)S(1)}, f32[16,128,128]{2,1,0:T(8,128)S(1)}) custom-call(s32[12]{0:T(128)S(1)} %concatenate.6.scal.refs_0_, f32[16,128,128]{2,1,0:T(8,128)} %bitcast.62, f32[16,128,128]{2,1,0:T(8,128)} %bitcast.64, f32[16,128,128]{2,1,0:T(8,128)} %refs_7_.1), custom_call_target="tpu_custom_call" | custom-call | bytes 4194304 | tf_op jit(solution)/shard_map/pack/pallas_call | solution.py:321
  3.7 5.5 %collective-permute-start.1 = (f32[16,128,128]{2,1,0:T(8,128)S(1)}, f32[16,128,128]{2,1,0:T(8,128)S(1)}, u32[]{:S(2)}, u32[]{:S(2)}) collective-permute-start(f32[16,128,128]{2,1,0:T(8,128)S(1)} %get-tuple-element.49), channel_id=1, source_target_pairs={{0,15},{1,2},{2,1},{3,4},{4,3},{5,6},{6,5},{7,8},{8,7},{9,10},{10,... | collective-permute-start | bytes 3145736 | tf_op jit(solution)/shard_map/ppermute | solution.py:366
  9.2 1.9 %pack.3 = (f32[12,128,128]{2,1,0:T(8,128)S(1)}, f32[12,128,128]{2,1,0:T(8,128)S(1)}) custom-call(s32[12]{0:T(128)S(1)} %concatenate.6.scal.refs_0_, f32[16,128,128]{2,1,0:T(8,128)} %bitcast.58, f32[16,128,128]{2,1,0:T(8,128)} %bitcast.60), custom_call_target="tpu_custom_call" | custom-call | bytes 4194304 | tf_op jit(solution)/shard_map/pack/pallas_call | solution.py:321
  11.2 0.9 collective-permute-start.3
  12.2 2.7 %list_receivers.1 = (s32[1]{0:T(128)}, s32[8,256]{1,0:T(8,128)S(1)}, f32[2048,128]{1,0:T(8,128)S(1)}, bf16[3072,256]{1,0:T(8,128)(2,1)S(1)}, bf16[6,512,256]{2,1...) custom-call(s32[12]{0:T(128)S(1)} %concatenate.6.scal.refs_0_, s32[3,2048]{1,0:T(4,128)S(1)} %bitcast.71, ...), custom_call_target="tpu_custom_call" | custom-call | bytes 14680064 | tf_op jit(solution)/shard_map/list_receivers/pallas_call | solution.py:335
  14.9 6.7 %collective-permute-done.1.refs_4_ = f32[16,128,128]{2,1,0:T(8,128)S(1)} collective-permute-done((f32[16,128,128]{2,1,0:T(8,128)S(1)}, f32[16,128,128]{2,1,0:T(8,128)S(1)}, u32[]{:S(2)}, u32[]{:S(2)}) %collective-permute-start.1) | collective-permute-done | bytes 1048608 | tf_op jit(solution)/shard_map/ppermute | solution.py:366
  21.7 5.8 %forward_block.3 = (f32[24,128,128]{2,1,0:T(8,128)S(1)}, f32[16,128,128]{2,1,0:T(8,128)S(1)}, f32[24,128,128]{2,1,0:T(8,128)S(1)}, f32[8,128,128]{2,1,0:T(8,128)...) custom-call(s32[12]{0:T(128)S(1)} %concatenate.6.scal.refs_0_, ...), custom_call_target="tpu_custom_call" | custom-call | bytes 14680064 | tf_op jit(solution)/shard_map/forward_block/pallas_call | solution.py:335
  27.6 5.4 %collective-permute-start.5 = (f32[8,128,128]{2,1,0:T(8,128)S(1)}, f32[8,128,128]{2,1,0:T(8,128)S(1)}, u32[]{:S(2)}, u32[]{:S(2)}) collective-permute-start(f32[8,128,128]{2,1,0:T(8,128)S(1)} %get-tuple-element.61), channel_id=1, source_target_pairs={{0,15},{1,2},{2,1},{3,4},{4,3},{5,6},{6,5},{7,8},{8,7},{9,10},{10,... | collective-permute-start | bytes 1572872 | tf_op jit(solution)/shard_map/ppermute | solution.py:366
  33.1 6.8 %adjoint_block.3 = (f32[24,128,128]{2,1,0:T(8,128)S(1)}, f32[16,128,128]{2,1,0:T(8,128)S(1)}, f32[8,128,128]{2,1,0:T(8,128)S(1)}, f32[8,128,128]{2,1,0:T(8,128)S(1)}, s32[1]{0:T(128)}) custom-call(s32[12]{0:T(128)S(1)} %concatenate.6.scal.refs_0_, s32[1]{0:T(128)} %get-tuple-element.47.refs_2_.refs_1_, s32[1]{0:T(128)} %get-tuple-element.51.refs_2_, ...), custom_call_target="tpu_custom_call" | custom-call | bytes 14680064 | tf_op jit(solution)/shard_map/adjoint_block/pallas_call | solution.py:335
  40.0 2.5 %collective-permute-start.7 = (f32[8,128,128]{2,1,0:T(8,128)S(1)}, f32[8,128,128]{2,1,0:T(8,128)S(1)}, u32[]{:S(2)}, u32[]{:S(2)}) collective-permute-start(f32[8,128,128]{2,1,0:T(8,128)S(1)} %get-tuple-element.66), channel_id=1, source_target_pairs={{0,15},{1,2},{2,1},{3,4},{4,3},{5,6},{6,5},{7,8},{8,7},{9,10},{10,... | collective-permute-start | bytes 1572872 | tf_op jit(solution)/shard_map/ppermute | solution.py:366
  42.4 5.3 %forward_block.4 = (f32[24,128,128]{2,1,0:T(8,128)S(1)}, f32[16,128,128]{2,1,0:T(8,128)S(1)}, f32[8,128,128]{2,1,0:T(8,128)S(1)}, f32[8,128,128]{2,1,0:T(8,128)S...) custom-call(s32[12]{0:T(128)S(1)} %concatenate.6.scal.refs_0_, f32[1,6]{1,0:T(1,128)S(1)} %copy-done.7, ...), custom_call_target="tpu_custom_call" | custom-call | bytes 14680064 | tf_op jit(solution)/shard_map/forward_block/pallas_call | solution.py:335
  47.7 0.3 collective-permute-start.8
  48.0 3.1 %collective-permute-start.9 = (f32[8,128,128]{2,1,0:T(8,128)S(1)}, f32[8,128,128]{2,1,0:T(8,128)S(1)}, u32[]{:S(2)}, u32[]{:S(2)}) collective-permute-start(f32[8,128,128]{2,1,0:T(8,128)S(1)} %get-tuple-element.73), channel_id=1, source_target_pairs={{0,15},{1,2},{2,1},{3,4},{4,3},{5,6},{6,5},{7,8},{8,7},{9,10},{10,... | collective-permute-start | bytes 1572872 | tf_op jit(solution)/shard_map/ppermute | solution.py:366
  51.1 1.2 %collective-permute-done.7.refs_4_ = f32[8,128,128]{2,1,0:T(8,128)S(1)} collective-permute-done((f32[8,128,128]{2,1,0:T(8,128)S(1)}, f32[8,128,128]{2,1,0:T(8,128)S(1)}, u32[]{:S(2)}, u32[]{:S(2)}) %collective-permute-start.7) | collective-permute-done | bytes 524320 | tf_op jit(solution)/shard_map/ppermute | solution.py:366
  52.3 7.0 %adjoint_block.4 = (f32[24,128,128]{2,1,0:T(8,128)S(1)}, f32[16,128,128]{2,1,0:T(8,128)S(1)}, f32[8,128,128]{2,1,0:T(8,128)S(1)}, f32[8,128,128]{2,1,0:T(8,128)S...) custom-call(s32[12]{0:T(128)S(1)} %concatenate.6.scal.refs_0_, s32[1]{0:T(128)} %get-tuple-element.47.refs_2_.refs_1_, ...), custom_call_target="tpu_custom_call" | custom-call | bytes 14680064 | tf_op jit(solution)/shard_map/adjoint_block/pallas_call | solution.py:335
  59.4 2.5 %collective-permute-start.11 = (f32[8,128,128]{2,1,0:T(8,128)S(1)}, f32[8,128,128]{2,1,0:T(8,128)S(1)}, u32[]{:S(2)}, u32[]{:S(2)}) collective-permute-start(f32[8,128,128]{2,1,0:T(8,128)S(1)} %get-tuple-element.80), channel_id=1, source_target_pairs={{0,15},{1,2},{2,1},{3,4},{4,3},{5,6},{6,5},{7,8},{8,7},{9,10},{10,... | collective-permute-start | bytes 1572872 | tf_op jit(solution)/shard_map/ppermute | solution.py:366
  61.9 5.9 %forward_block.5 = (f32[16,128,128]{2,1,0:T(8,128)}, f32[16,128,128]{2,1,0:T(8,128)S(1)}, s32[1]{0:T(128)}) custom-call(s32[12]{0:T(128)S(1)} %concatenate.6.scal.refs_0_, f32[1,6]{1,0:T(1,128)S(1)} %copy-done.7, s32[1]{0:T(128)} %get-tuple-element.71.refs_2_, f32[8,128,128]{2,1,0:T(8,128)S(1)} %collective-permute-done.8.refs_3_, ...), custom_call_target="tpu_custom_call" | custom-call | bytes 14680064 | tf_op jit(solution)/shard_map/forward_block/pallas_call | solution.py:335
  67.8 3.9 %collective-permute-done.11.refs_4_ = f32[8,128,128]{2,1,0:T(8,128)S(1)} collective-permute-done((f32[8,128,128]{2,1,0:T(8,128)S(1)}, f32[8,128,128]{2,1,0:T(8,128)S(1)}, u32[]{:S(2)}, u32[]{:S(2)}) %collective-permute-start.11) | collective-permute-done | bytes 524320 | tf_op jit(solution)/shard_map/ppermute | solution.py:366
  71.7 7.6 %adjoint_block.5 = (f32[16,128,128]{2,1,0:T(8,128)}, f32[8,8,8,128]{3,2,1,0:T(8,128)S(1)}, f32[8,8,8,128]{3,2,1,0:T(8,128)S(1)}, f32[8,8,8,128]{3,2,1,0:T(8,128)...) custom-call(s32[12]{0:T(128)S(1)} %concatenate.6.scal.refs_0_, s32[1]{0:T(128)} %get-tuple-element.47.refs_2_.refs_1_, ...), custom_call_target="tpu_custom_call" | custom-call | bytes 14680064 | tf_op jit(solution)/shard_map/adjoint_block/pallas_call | solution.py:335
  79.3 0.2 collective-permute-start.14
  79.5 0.7 collective-permute-start.12
  80.1 6.4 %collective-permute-done.14 = f32[8,8,8,128]{3,2,1,0:T(8,128)S(1)} collective-permute-done((f32[8,8,8,128]{3,2,1,0:T(8,128)S(1)}, f32[8,8,8,128]{3,2,1,0:T(8,128)S(1)}, u32[]{:S(2)}, u32[]{:S(2)}) %collective-permute-start.14) | collective-permute-done | bytes 262176 | tf_op jit(solution)/shard_map/ppermute | solution.py:468
  86.6 0.6 collective-permute-done.12
  87.2 1.7 %collective-permute-start.13 = (f32[4,8,8,128]{3,2,1,0:T(8,128)S(1)}, f32[4,8,8,128]{3,2,1,0:T(8,128)S(1)}, u32[]{:S(2)}, u32[]{:S(2)}) collective-permute-start(f32[4,8,8,128]{3,2,1,0:T(8,128)S(1)} %fusion), channel_id=1, source_target_pairs={{0,16},{16,0},{32,48},{48,32},{64,80},{80,64},{96,112},{112,96},{1... | collective-permute-start | bytes 393224 | tf_op jit(solution)/shard_map/ppermute | solution.py:468
  89.0 2.6 %collective-permute-done.15 = f32[4,8,8,128]{3,2,1,0:T(8,128)S(1)} collective-permute-done((f32[4,8,8,128]{3,2,1,0:T(8,128)S(1)}, f32[4,8,8,128]{3,2,1,0:T(8,128)S(1)}, u32[]{:S(2)}, u32[]{:S(2)}) %collective-permute-start.15) | collective-permute-done | bytes 131104 | tf_op jit(solution)/shard_map/ppermute | solution.py:468
  91.6 1.1 collective-permute-done.13
  92.7 3.7 %collective-permute-start.16 = (f32[16,8,128]{2,1,0:T(8,128)S(1)}, f32[16,8,128]{2,1,0:T(8,128)S(1)}, u32[]{:S(2)}, u32[]{:S(2)}) collective-permute-start(f32[16,8,128]{2,1,0:T(8,128)S(1)} %get-tuple-element.91), channel_id=1, source_target_pairs={{0,32},{16,48},{32,0},{48,16},{64,96},{80,112},{96,64},{112,80},{1... | collective-permute-start | bytes 196616 | tf_op jit(solution)/shard_map/ppermute | solution.py:468
  96.4 5.5 %collective-permute-start.17 = (f32[16,8,128]{2,1,0:T(8,128)S(1)}, f32[16,8,128]{2,1,0:T(8,128)S(1)}, u32[]{:S(2)}, u32[]{:S(2)}) collective-permute-start(f32[16,8,128]{2,1,0:T(8,128)S(1)} %get-tuple-element.92), channel_id=1, source_target_pairs={{0,64},{16,80},{32,96},{48,112},{64,0},{80,16},{96,32},{112,48},{1... | collective-permute-start | bytes 196616 | tf_op jit(solution)/shard_map/ppermute | solution.py:468
  101.9 4.1 %collective-permute-done.17 = f32[16,8,128]{2,1,0:T(8,128)S(1)} collective-permute-done((f32[16,8,128]{2,1,0:T(8,128)S(1)}, f32[16,8,128]{2,1,0:T(8,128)S(1)}, u32[]{:S(2)}, u32[]{:S(2)}) %collective-permute-start.17) | collective-permute-done | bytes 65568 | tf_op jit(solution)/shard_map/ppermute | solution.py:468
  106.0 2.8 %collective-permute-done.18 = f32[16,8,128]{2,1,0:T(8,128)S(1)} collective-permute-done((f32[16,8,128]{2,1,0:T(8,128)S(1)}, f32[16,8,128]{2,1,0:T(8,128)S(1)}, u32[]{:S(2)}, u32[]{:S(2)}) %collective-permute-start.18) | collective-permute-done | bytes 65568 | tf_op jit(solution)/shard_map/ppermute | solution.py:468
  108.8 0.6 fusion.9
  (44 shorter events, 0.8 us)
Async XLA Ops:
  1.4 10.7 %copy-start.8 = (f32[1,6,2048]{2,0,1:T(1,128)S(1)}, f32[1,6,2048]{2,0,1:T(1,128)}, u32[]{:S(2)}) copy-start(f32[1,6,2048]{2,0,1:T(1,128)} %param.21) | copy-start | bytes 147460
  1.4 10.8 %copy-start.9 = (s32[1,3,2048]{2,0,1:T(1,128)S(1)}, s32[1,3,2048]{2,0,1:T(1,128)}, u32[]{:S(2)}) copy-start(s32[1,3,2048]{2,0,1:T(1,128)} %param.20) | copy-start | bytes 73732
  1.4 20.2 %copy-start.4 = (f32[16,128,128]{2,1,0:T(8,128)S(1)}, f32[16,128,128]{2,1,0:T(8,128)}, u32[]{:S(2)}) copy-start(f32[16,128,128]{2,1,0:T(8,128)} %refs_7_.1) | copy-start | bytes 3145732
  3.5 8.7 %copy-start.5 = (bf16[256,128]{1,0:T(8,128)(2,1)S(1)}, bf16[256,128]{1,0:T(8,128)(2,1)}, u32[]{:S(2)}) copy-start(bf16[256,128]{1,0:T(8,128)(2,1)} %constant.62.clone.tz.refs_9_.refs_11_.refs_12_) | copy-start | bytes 196612
  3.5 18.1 %copy-start.2 = (f32[1,16,128,128]{3,2,1,0:T(8,128)S(1)}, f32[1,16,128,128]{3,2,1,0:T(8,128)}, u32[]{:S(2)}) copy-start(f32[1,16,128,128]{3,2,1,0:T(8,128)} %param.15) | copy-start | bytes 3145732
  3.5 18.1 %copy-start.3 = (f32[1,16,128,128]{3,2,1,0:T(8,128)S(1)}, f32[1,16,128,128]{3,2,1,0:T(8,128)}, u32[]{:S(2)}) copy-start(f32[1,16,128,128]{3,2,1,0:T(8,128)} %param.14) | copy-start | bytes 3145732
  3.5 18.1 %copy-start.6 = (bf16[128,256]{1,0:T(8,128)(2,1)S(1)}, bf16[128,256]{1,0:T(8,128)(2,1)}, u32[]{:S(2)}) copy-start(bf16[128,256]{1,0:T(8,128)(2,1)} %constant.63.clone.refs_10_.refs_12_.refs_13_) | copy-start | bytes 196612
  3.6 18.1 %copy-start.7 = (f32[1,6]{1,0:T(1,128)S(1)}, f32[1,6]{1,0:T(1,128)}, u32[]{:S(2)}) copy-start(f32[1,6]{1,0:T(1,128)} %refs_1_.5) | copy-start | bytes 76
  3.6 11.3 %collective-permute-start = (f32[16,128,128]{2,1,0:T(8,128)S(1)}, f32[16,128,128]{2,1,0:T(8,128)S(1)}, u32[]{:S(2)}, u32[]{:S(2)}) collective-permute-start(f32[16,128,128]{2,1,0:T(8,128)S(1)} %get-tuple-element.48), channel_id=1, source_target_pairs={{0,1},{1,0},{2,3},{3,2},{4,5},{5,4},{6,7},{7,6},{8,9},{9,8},{10,11... | collective-permute-start | bytes 3145736 | tf_op jit(solution)/shard_map/ppermute | solution.py:367
  3.7 18.0 %collective-permute-start.1 = (f32[16,128,128]{2,1,0:T(8,128)S(1)}, f32[16,128,128]{2,1,0:T(8,128)S(1)}, u32[]{:S(2)}, u32[]{:S(2)}) collective-permute-start(f32[16,128,128]{2,1,0:T(8,128)S(1)} %get-tuple-element.49), channel_id=1, source_target_pairs={{0,15},{1,2},{2,1},{3,4},{4,3},{5,6},{6,5},{7,8},{8,7},{9,10},{10,... | collective-permute-start | bytes 3145736 | tf_op jit(solution)/shard_map/ppermute | solution.py:366
  11.1 21.9 %collective-permute-start.2 = (f32[12,128,128]{2,1,0:T(8,128)S(1)}, f32[12,128,128]{2,1,0:T(8,128)S(1)}, u32[]{:S(2)}, u32[]{:S(2)}) collective-permute-start(f32[12,128,128]{2,1,0:T(8,128)S(1)} %get-tuple-element.52), channel_id=1, source_target_pairs={{0,1},{1,0},{2,3},{3,2},{4,5},{5,4},{6,7},{7,6},{8,9},{9,8},{10,11... | collective-permute-start | bytes 2359304 | tf_op jit(solution)/shard_map/ppermute | solution.py:367
  11.2 21.9 %collective-permute-start.3 = (f32[12,128,128]{2,1,0:T(8,128)S(1)}, f32[12,128,128]{2,1,0:T(8,128)S(1)}, u32[]{:S(2)}, u32[]{:S(2)}) collective-permute-start(f32[12,128,128]{2,1,0:T(8,128)S(1)} %get-tuple-element.53), channel_id=1, source_target_pairs={{0,15},{1,2},{2,1},{3,4},{4,3},{5,6},{6,5},{7,8},{8,7},{9,10},{10,... | collective-permute-start | bytes 2359304 | tf_op jit(solution)/shard_map/ppermute | solution.py:366
  21.7 11.4 %copy-start = (f32[1,16,128,128]{3,2,1,0:T(8,128)S(1)}, f32[1,16,128,128]{3,2,1,0:T(8,128)}, u32[]{:S(2)}) copy-start(f32[1,16,128,128]{3,2,1,0:T(8,128)} %param.16) | copy-start | bytes 3145732
  21.7 11.4 %copy-start.1 = (f32[1,16,128,128]{3,2,1,0:T(8,128)S(1)}, f32[1,16,128,128]{3,2,1,0:T(8,128)}, u32[]{:S(2)}) copy-start(f32[1,16,128,128]{3,2,1,0:T(8,128)} %param.17) | copy-start | bytes 3145732
  27.5 15.0 %collective-permute-start.4 = (f32[8,128,128]{2,1,0:T(8,128)S(1)}, f32[8,128,128]{2,1,0:T(8,128)S(1)}, u32[]{:S(2)}, u32[]{:S(2)}) collective-permute-start(f32[8,128,128]{2,1,0:T(8,128)S(1)} %get-tuple-element.60), channel_id=1, source_target_pairs={{0,1},{1,0},{2,3},{3,2},{4,5},{5,4},{6,7},{7,6},{8,9},{9,8},{10,11... | collective-permute-start | bytes 1572872 | tf_op jit(solution)/shard_map/ppermute | solution.py:367
  27.6 14.9 %collective-permute-start.5 = (f32[8,128,128]{2,1,0:T(8,128)S(1)}, f32[8,128,128]{2,1,0:T(8,128)S(1)}, u32[]{:S(2)}, u32[]{:S(2)}) collective-permute-start(f32[8,128,128]{2,1,0:T(8,128)S(1)} %get-tuple-element.61), channel_id=1, source_target_pairs={{0,15},{1,2},{2,1},{3,4},{4,3},{5,6},{6,5},{7,8},{8,7},{9,10},{10,... | collective-permute-start | bytes 1572872 | tf_op jit(solution)/shard_map/ppermute | solution.py:366
  39.9 11.2 %collective-permute-start.6 = (f32[8,128,128]{2,1,0:T(8,128)S(1)}, f32[8,128,128]{2,1,0:T(8,128)S(1)}, u32[]{:S(2)}, u32[]{:S(2)}) collective-permute-start(f32[8,128,128]{2,1,0:T(8,128)S(1)} %get-tuple-element.65), channel_id=1, source_target_pairs={{0,1},{1,0},{2,3},{3,2},{4,5},{5,4},{6,7},{7,6},{8,9},{9,8},{10,11... | collective-permute-start | bytes 1572872 | tf_op jit(solution)/shard_map/ppermute | solution.py:367
  40.0 12.3 %collective-permute-start.7 = (f32[8,128,128]{2,1,0:T(8,128)S(1)}, f32[8,128,128]{2,1,0:T(8,128)S(1)}, u32[]{:S(2)}, u32[]{:S(2)}) collective-permute-start(f32[8,128,128]{2,1,0:T(8,128)S(1)} %get-tuple-element.66), channel_id=1, source_target_pairs={{0,15},{1,2},{2,1},{3,4},{4,3},{5,6},{6,5},{7,8},{8,7},{9,10},{10,... | collective-permute-start | bytes 1572872 | tf_op jit(solution)/shard_map/ppermute | solution.py:366
  47.7 14.1 %collective-permute-start.8 = (f32[8,128,128]{2,1,0:T(8,128)S(1)}, f32[8,128,128]{2,1,0:T(8,128)S(1)}, u32[]{:S(2)}, u32[]{:S(2)}) collective-permute-start(f32[8,128,128]{2,1,0:T(8,128)S(1)} %get-tuple-element.72), channel_id=1, source_target_pairs={{0,1},{1,0},{2,3},{3,2},{4,5},{5,4},{6,7},{7,6},{8,9},{9,8},{10,11... | collective-permute-start | bytes 1572872 | tf_op jit(solution)/shard_map/ppermute | solution.py:367
  48.0 13.9 %collective-permute-start.9 = (f32[8,128,128]{2,1,0:T(8,128)S(1)}, f32[8,128,128]{2,1,0:T(8,128)S(1)}, u32[]{:S(2)}, u32[]{:S(2)}) collective-permute-start(f32[8,128,128]{2,1,0:T(8,128)S(1)} %get-tuple-element.73), channel_id=1, source_target_pairs={{0,15},{1,2},{2,1},{3,4},{4,3},{5,6},{6,5},{7,8},{8,7},{9,10},{10,... | collective-permute-start | bytes 1572872 | tf_op jit(solution)/shard_map/ppermute | solution.py:366
  59.3 8.5 %collective-permute-start.10 = (f32[8,128,128]{2,1,0:T(8,128)S(1)}, f32[8,128,128]{2,1,0:T(8,128)S(1)}, u32[]{:S(2)}, u32[]{:S(2)}) collective-permute-start(f32[8,128,128]{2,1,0:T(8,128)S(1)} %get-tuple-element.79), channel_id=1, source_target_pairs={{0,1},{1,0},{2,3},{3,2},{4,5},{5,4},{6,7},{7,6},{8,9},{9,8},{10,11... | collective-permute-start | bytes 1572872 | tf_op jit(solution)/shard_map/ppermute | solution.py:367
  59.4 12.3 %collective-permute-start.11 = (f32[8,128,128]{2,1,0:T(8,128)S(1)}, f32[8,128,128]{2,1,0:T(8,128)S(1)}, u32[]{:S(2)}, u32[]{:S(2)}) collective-permute-start(f32[8,128,128]{2,1,0:T(8,128)S(1)} %get-tuple-element.80), channel_id=1, source_target_pairs={{0,15},{1,2},{2,1},{3,4},{4,3},{5,6},{6,5},{7,8},{8,7},{9,10},{10,... | collective-permute-start | bytes 1572872 | tf_op jit(solution)/shard_map/ppermute | solution.py:366
  79.3 7.2 %collective-permute-start.14 = (f32[8,8,8,128]{3,2,1,0:T(8,128)S(1)}, f32[8,8,8,128]{3,2,1,0:T(8,128)S(1)}, u32[]{:S(2)}, u32[]{:S(2)}) collective-permute-start(f32[8,8,8,128]{3,2,1,0:T(8,128)S(1)} %get-tuple-element.90), channel_id=1, source_target_pairs={{0,16},{16,0},{32,48},{48,32},{64,80},{80,64},{96,112},{112,96},{1... | collective-permute-start | bytes 786440 | tf_op jit(solution)/shard_map/ppermute | solution.py:468
  79.5 7.8 %collective-permute-start.12 = (f32[8,8,8,128]{3,2,1,0:T(8,128)S(1)}, f32[8,8,8,128]{3,2,1,0:T(8,128)S(1)}, u32[]{:S(2)}, u32[]{:S(2)}) collective-permute-start(f32[8,8,8,128]{3,2,1,0:T(8,128)S(1)} %get-tuple-element.88), channel_id=1, source_target_pairs={{0,128},{16,144},{32,160},{48,176},{64,192},{80,208},{96,224},{112... | collective-permute-start | bytes 786440 | tf_op jit(solution)/shard_map/ppermute | solution.py:468
  86.5 5.1 %collective-permute-start.15 = (f32[4,8,8,128]{3,2,1,0:T(8,128)S(1)}, f32[4,8,8,128]{3,2,1,0:T(8,128)S(1)}, u32[]{:S(2)}, u32[]{:S(2)}) collective-permute-start(f32[4,8,8,128]{3,2,1,0:T(8,128)S(1)} %add_bitcast_fusion), channel_id=1, source_target_pairs={{0,128},{16,144},{32,160},{48,176},{64,192},{80,208},{96,224},{112... | collective-permute-start | bytes 393224 | tf_op jit(solution)/shard_map/ppermute | solution.py:468
  87.2 5.4 %collective-permute-start.13 = (f32[4,8,8,128]{3,2,1,0:T(8,128)S(1)}, f32[4,8,8,128]{3,2,1,0:T(8,128)S(1)}, u32[]{:S(2)}, u32[]{:S(2)}) collective-permute-start(f32[4,8,8,128]{3,2,1,0:T(8,128)S(1)} %fusion), channel_id=1, source_target_pairs={{0,16},{16,0},{32,48},{48,32},{64,80},{80,64},{96,112},{112,96},{1... | collective-permute-start | bytes 393224 | tf_op jit(solution)/shard_map/ppermute | solution.py:468
  92.7 9.2 %collective-permute-start.16 = (f32[16,8,128]{2,1,0:T(8,128)S(1)}, f32[16,8,128]{2,1,0:T(8,128)S(1)}, u32[]{:S(2)}, u32[]{:S(2)}) collective-permute-start(f32[16,8,128]{2,1,0:T(8,128)S(1)} %get-tuple-element.91), channel_id=1, source_target_pairs={{0,32},{16,48},{32,0},{48,16},{64,96},{80,112},{96,64},{112,80},{1... | collective-permute-start | bytes 196616 | tf_op jit(solution)/shard_map/ppermute | solution.py:468
  96.4 9.6 %collective-permute-start.17 = (f32[16,8,128]{2,1,0:T(8,128)S(1)}, f32[16,8,128]{2,1,0:T(8,128)S(1)}, u32[]{:S(2)}, u32[]{:S(2)}) collective-permute-start(f32[16,8,128]{2,1,0:T(8,128)S(1)} %get-tuple-element.92), channel_id=1, source_target_pairs={{0,64},{16,80},{32,96},{48,112},{64,0},{80,16},{96,32},{112,48},{1... | collective-permute-start | bytes 196616 | tf_op jit(solution)/shard_map/ppermute | solution.py:468
  101.9 6.8 %collective-permute-start.18 = (f32[16,8,128]{2,1,0:T(8,128)S(1)}, f32[16,8,128]{2,1,0:T(8,128)S(1)}, u32[]{:S(2)}, u32[]{:S(2)}) collective-permute-start(f32[16,8,128]{2,1,0:T(8,128)S(1)} %get-tuple-element.93), channel_id=1, source_target_pairs={{0,96},{16,112},{32,64},{48,80},{64,32},{80,48},{96,0},{112,16},{1... | collective-permute-start | bytes 196616 | tf_op jit(solution)/shard_map/ppermute | solution.py:468
